TPU v7x, 256 devices: a whole 4x4x8 slice. The times are simulated.
256 devices in a mesh: frame: 32 (over x, z), head: 8 (over y, core).
Axes of the slice: x: 4, y: 4, z: 8, core: 2. Of those that a mesh axis runs over, the one named last changes fastest.
Arguments:
- queries: bfloat16 [64, 16, 32, 1792], P('frame', None, None, 'head'), may hold values from -6 to 6
- key_vectors: bfloat16 [64, 16, 32, 1792], P('frame', None, None, 'head'), may hold values from -6 to 6
- value_vectors: bfloat16 [64, 16, 32, 1792], P('frame', None, None, 'head'), may hold values from -8 to 8
- frame_index: int32 [64], P('frame'), may hold values from 0 to 127, as said below
- height_index: int32 [16], replicated, may hold values from 0 to 31, as said below
- width_index: int32 [32], replicated, may hold values from 0 to 63, as said below
- frame_block: int32 [64], P('frame'), may hold values from 0 to 20, never falling along the last dimension, each value on 1 to 6 neighbouring positions
- conv_weight: bfloat16 [3, 1792, 2240], P(None, 'head'), may hold values from -0.078125 to 0.078125
- conv_bias: float32 [2240], replicated, may hold values from -0.8 to 0.8
Outputs:
- mixed_frames: bfloat16 [16, 64, 32, 2240], P('head', 'frame')
Inputs may be any that keep to these rules, and one draw needn't show every extreme that they name: `frame_index`: strictly increasing over the frames, first entry 0, last entry 127. `height_index`: strictly increasing over the rows, first entry 0, last entry 31. `width_index`: strictly increasing over the columns, first entry 0, last entry 63.
All inputs are finite; a program needn't handle non-finite values.
Results may differ from a plain program's by a relative error of at most 0.0043.
The roundings to bfloat16 on the way count: a program that leaves them out, or rounds other values in their place, can miss the bound.
Values may be sent and summed in bfloat16 or wider, within the bound.
No kernel may reach another device: no remote copies, remote signals or barrier semaphores. Data moves between devices by JAX's collectives and lax.ppermute only.
A program may use at most 128 MiB of HBM per device.

v0:
```python
import jax
import jax.numpy as jnp
from jax import lax
from jax.sharding import PartitionSpec as P

HD = 112


EPSILON = 1e-06
HIGHEST = lax.Precision.HIGHEST


def prefix(value, axis, join, neutral, backward):
    count, mine = (lax.axis_size(axis), lax.axis_index(axis))
    pieces = jax.tree.map(lambda part: lax.all_gather(part, axis), value)
    if backward:
        pieces = jax.tree.map(lambda part: part[::-1], pieces)
        mine = count - 1 - mine
    so_far = jax.tree.map(
        lambda part, zero: jnp.full_like(part, 0) + jnp.asarray(zero, part.dtype), value, neutral
    )

    def step(position, so_far):
        longer = join(so_far, jax.tree.map(lambda part: part[position], pieces))
        return jax.tree.map(lambda new, old: jnp.where(position < mine, new, old), longer, so_far)

    return lax.fori_loop(0, count - 1, step, so_far)


def shifted(value, axis, by):
    length = lax.axis_size(axis)
    pairs = [(i, i + by) for i in range(length) if 0 <= i + by < length]
    return lax.ppermute(value, axis, pairs)


def spin_part(section, positions, axis_slot):
    half_size = section.shape[-1] // 2
    inverse = 10000.0 ** (-2.0 * jnp.arange(half_size, dtype=jnp.float32) / section.shape[-1])
    angles = positions.astype(jnp.float32)[:, None] * inverse[None, :]
    target = [1, 1, 1, 1, half_size]
    target[axis_slot] = positions.shape[0]
    angles = angles.reshape(target)
    cosine = jnp.cos(angles)
    sine_values = jnp.sin(angles)
    lower_half = section[..., :half_size]
    upper_half = section[..., half_size:]
    return jnp.concatenate(
        [
            lower_half * cosine - upper_half * sine_values,
            upper_half * cosine + lower_half * sine_values,
        ],
        axis=-1,
    )


def rotate(values, frame_pos, height_pos, width_pos):
    head_size = values.shape[-1]
    side_size = head_size * 5 // 14 // 2 * 2
    first_size = head_size - 2 * side_size
    return jnp.concatenate(
        [
            spin_part(values[..., :first_size], frame_pos, 0),
            spin_part(values[..., first_size : first_size + side_size], height_pos, 1),
            spin_part(values[..., first_size + side_size :], width_pos, 2),
        ],
        axis=-1,
    )


def add_pair(earlier, later):
    return (earlier[0] + later[0], earlier[1] + later[1])


def join_tails(earlier, later):
    high_id, high_state, high_sum = earlier
    low_id, low_state, low_sum = later
    vacant = low_id < 0.0
    same_block = high_id == low_id
    joined_id = jnp.where(vacant, high_id, low_id)
    joined_state = jnp.where(vacant, high_state, low_state + jnp.where(same_block, high_state, 0.0))
    joined_sum = jnp.where(vacant, high_sum, low_sum + jnp.where(same_block, high_sum, 0.0))
    return (joined_id, joined_state, joined_sum)


def conv_taps(rows, weight, frame_count):
    result = jnp.einsum(
        "yfxc,co->yfxo", rows[:, 2 : 2 + frame_count], weight[0], preferred_element_type=jnp.float32
    )
    result = result + jnp.einsum(
        "yfxc,co->yfxo", rows[:, 1 : 1 + frame_count], weight[1], preferred_element_type=jnp.float32
    )
    result = result + jnp.einsum(
        "yfxc,co->yfxo", rows[:, 0:frame_count], weight[2], preferred_element_type=jnp.float32
    )
    return result


def per_device(
    queries,
    key_vectors,
    value_vectors,
    frame_index,
    height_index,
    width_index,
    frame_block,
    conv_weight,
    conv_bias,
):
    frame_count, height_count, width_count, channel_count = queries.shape
    head_count = channel_count // HD
    split_shape = (frame_count, height_count, width_count, head_count, HD)
    query_pos = jax.nn.relu(queries.astype(jnp.float32)).reshape(split_shape)
    key_pos = jax.nn.relu(key_vectors.astype(jnp.float32)).reshape(split_shape)
    value_rows = value_vectors.astype(jnp.float32).reshape(split_shape)
    query_rot = rotate(query_pos, frame_index, height_index, width_index)
    key_rot = rotate(key_pos, frame_index, height_index, width_index)
    frame_states = jnp.einsum("fyxhd,fyxhe->fhde", key_rot, value_rows, precision=HIGHEST)
    frame_sums = jnp.sum(key_pos, axis=(1, 2))
    block_float = frame_block.astype(jnp.float32)
    allowed = (frame_block[None, :] <= frame_block[:, None]).astype(jnp.float32)
    device_state = jnp.sum(frame_states, axis=0)
    device_sum = jnp.sum(frame_sums, axis=0)
    leading = (frame_block == frame_block[0]).astype(jnp.float32)
    lead_state = jnp.einsum("f,fhde->hde", leading, frame_states, precision=HIGHEST)
    lead_sum = jnp.einsum("f,fhd->hd", leading, frame_sums, precision=HIGHEST)
    lead_id = block_float[0]
    before_state, before_sum = prefix(
        (device_state, device_sum),
        "frame",
        add_pair,
        (jnp.zeros_like(device_state), jnp.zeros_like(device_sum)),
        False,
    )
    tail_id, tail_state, tail_sum = prefix(
        (lead_id, lead_state, lead_sum),
        "frame",
        join_tails,
        (jnp.full((), -1.0, jnp.float32), jnp.zeros_like(lead_state), jnp.zeros_like(lead_sum)),
        True,
    )
    matching = (block_float == tail_id).astype(jnp.float32)
    tail_states = matching[:, None, None, None] * tail_state[None]
    tail_sums = matching[:, None, None] * tail_sum[None]
    states = (
        before_state[None]
        + jnp.einsum("tf,fhde->thde", allowed, frame_states, precision=HIGHEST)
        + tail_states
    )
    key_totals = (
        before_sum[None]
        + jnp.einsum("tf,fhd->thd", allowed, frame_sums, precision=HIGHEST)
        + tail_sums
    )
    numerator = jnp.einsum("tyxhd,thde->tyxhe", query_rot, states, precision=HIGHEST)
    denominator = jnp.einsum("tyxhd,thd->tyxh", query_pos, key_totals, precision=HIGHEST) + EPSILON
    attended = (
        (numerator / denominator[..., None])
        .astype(jnp.bfloat16)
        .reshape(frame_count, height_count, width_count, channel_count)
    )
    ordered = jnp.transpose(attended, (1, 0, 2, 3))
    previous = shifted(ordered, "frame", 1)
    extended = jnp.concatenate([previous, ordered], axis=1)
    summed = lax.psum_scatter(
        conv_taps(extended, conv_weight, frame_count), "head", scatter_dimension=0, tiled=True
    )
    return jax.nn.silu(summed + conv_bias).astype(jnp.bfloat16)


def solution(mesh):
    placed = (
        P("frame", None, None, "head"),
        P("frame", None, None, "head"),
        P("frame", None, None, "head"),
        P("frame"),
        P(),
        P(),
        P("frame"),
        P(None, "head", None),
        P(),
    )
    return jax.shard_map(
        per_device,
        mesh=mesh,
        in_specs=placed,
        out_specs=P("head", "frame", None, None),
        check_vma=False,
    )
```

profile of v0, /device:TPU:1, one launch (start us, length us, event | category | flops | bytes accessed | tf_op | source)
XLA Modules:
  0.0 440.1 jit_solution(9318961820425124567)
XLA Ops:
  6.6 1.3 fusion.16
  8.5 2.5 fusion.41
  11.0 6.4 %fusion.40 = (f32[2,16,32,2,20]{4,3,2,1,0:T(2,128)}, f32[2,16,32,2,20]{4,3,2,1,0:T(2,128)}, f32[2,16,32,2,20]{4,3,2,1,0:T(2,128)}, f32[2,16,32,2,20]{4,3,2,1,0:T(2,128)}) fusion(f32[2,16,32,2,112]{4,3,2,1,0:T(2,128)S(1)} %reshape.194), kind=kLoop, calls=%fused_computation.79 | loop fusion | bytes 1310720 | tf_op jit(solution)/shard_map/slice | solution.py:45
  17.7 1.1 reshape.195
  19.9 3.7 multiply_add_fusion.5
  23.6 4.6 %multiply_add_fusion.3 = (f32[2,16,32,2,20]{4,2,1,3,0:T(8,128)}, f32[2,16,32,2,20]{4,2,1,3,0:T(8,128)}, f32[2,16,32,2,20]{4,2,1,3,0:T(8,128)}, f32[2,16,32,2,20]...) fusion(f32[2,16,32,2,20]{4,3,2,1,0:T(2,128)S(1)} %copy-done.4, ...), kind=kLoop, calls=%fused_computation.26 | loop fusion | flops 983040 | bytes 2629120 | tf_op jit(solution)/shard_map/add | solution.py:50
  28.3 5.1 %concatenate.9 = f32[2,16,32,2,112]{4,2,1,3,0:T(8,128)} concatenate(f32[2,16,32,2,16]{4,2,1,3,0:T(8,128)} %get-tuple-element.344, f32[2,16,32,2,16]{4,2,1,3,0:T(8,128)} %get-tuple-element.343, f32[2,16,32,2,20]{4,2,1,3,0:T(8,128)} %get-tuple-element.364, f32[2,16,32,2,20]{4,2,1,3,0:T(8,128)} %get-tuple-element.365, f32[2,16,32,2,20]{4,2,1,3,0:T(8,128)} %get-tuple-element.340, ...), dimensions={4} | concatenate | bytes 1835008 | tf_op jit(solution)/shard_map/concatenate | solution.py:60
  33.3 3.0 fusion.42
  36.4 1.3 fusion.19
  39.3 64.5 %all-reduce = f32[32]{0:T(128)S(1)} all-reduce(f32[32]{0:T(128)S(1)} %slice_dynamic-update-slice_fusion), channel_id=1, replica_groups=mesh['frame'=32,'head'=8] {'frame'}, use_global_device_ids=true, to_apply=%add | all-reduce | flops 32 | bytes 256
  104.2 32.3 %all-gather.3 = f32[32,2,112]{2,1,0:T(2,128)S(1)} all-gather(f32[1,2,112]{2,1,0:T(2,128)S(1)} %bitcast.107), channel_id=4, replica_groups=mesh['frame'=32,'head'=8] {'frame'}, dimensions={0}, use_global_device_ids=true | all-gather | bytes 29568 | tf_op jit(solution)/shard_map/all_gather | solution.py:15
  136.5 35.2 %all_gather.30 = f32[32,2,112]{2,1,0:T(2,128)S(1)} all-gather(f32[1,2,112]{2,1,0:T(2,128)S(1)} %all_gather.29), channel_id=1, replica_groups=mesh['frame'=32,'head'=8] {'frame'}, dimensions={0}, use_global_device_ids=true | all-gather | bytes 29568 | tf_op jit(solution)/shard_map/all_gather | solution.py:15
  171.7 4.7 %concatenate.10 = f32[2,16,32,2,112]{4,2,1,3,0:T(8,128)} concatenate(f32[2,16,32,2,16]{4,2,1,3,0:T(8,128)S(1)} %get-tuple-element.366, f32[2,16,32,2,16]{4,2,1,3,0:T(8,128)S(1)} %get-tuple-element.367, f32[2,16,32,2,20]{4,2,1,3,0:T(8,128)} %get-tuple-element.361, f32[2,16,32,2,20]{4,2,1,3,0:T(8,128)} %get-tuple-element.360, f32[2,16,32,2,20]{4,2,1,3,0:T(8,128)} %get-tuple-element.362, ...), dimensions={4} | concatenate | bytes 1835008 | tf_op jit(solution)/shard_map/concatenate | solution.py:60
  176.4 30.5 %while.34 = (s32[]{:T(128)}, f32[2,112,112]{2,1,0:T(8,128)S(1)}, f32[2,112]{1,0:T(2,128)S(1)}, s32[]{:T(128)}, f32[32,2,112,112]{3,2,1,0:T(8,128)}, /*index=5*/f32[32,2,112]{2,1,0:T(2,128)S(1)}, s32[]{:T(128)}, s32[]{:T(128)}) while((s32[]{:T(128)}, f32[2,112,112]{2,1,0:T(8,128)S(1)}, f32[2,112]{1,0:T(2,128)S(1)}, s32[]{:T(128)}, ...), condition=%wide.region_3.4_spmd.clone, body=%wide.region_2.3_spmd.clone.sunk | while | flops 75940 | bytes 303867 | solution.py:27
  178.4 0.9 add_select_fusion.4
  183.3 1.0 add_select_fusion.4
  187.3 0.9 add_select_fusion.4
  188.2 0.9 add_select_fusion.4
  189.2 0.9 add_select_fusion.4
  190.2 0.9 add_select_fusion.4
  192.2 0.9 add_select_fusion.4
  193.2 0.9 add_select_fusion.4
  206.9 4.1 rev.10
  211.1 108.9 %while.35 = (s32[]{:T(128)}, f32[]{:T(128)}, f32[2,112,112]{2,1,0:T(8,128)S(1)}, f32[2,112]{1,0:T(2,128)S(1)}, s32[]{:T(128)}, /*index=5*/f32[32]{0:T(128)S(1)},...) while((s32[]{:T(128)}, f32[]{:T(128)}, ...), condition=%wide.region_6.7_spmd.clone, body=%wide.region_5.6_spmd.clone.sunk | while | flops 126568 | bytes 303951 | solution.py:27
  213.6 0.9 select_select_fusion.4
  217.1 0.9 select_select_fusion.4
  220.6 0.9 select_select_fusion.4
  224.1 0.9 select_select_fusion.4
  227.7 0.9 select_select_fusion.4
  231.2 0.9 select_select_fusion.4
  234.7 0.9 select_select_fusion.4
  238.2 0.9 select_select_fusion.4
  241.7 0.9 select_select_fusion.4
  245.2 0.9 select_select_fusion.4
  248.7 0.9 select_select_fusion.4
  252.3 0.9 select_select_fusion.4
  255.8 0.9 select_select_fusion.4
  259.3 0.9 select_select_fusion.4
  262.8 0.9 select_select_fusion.4
  266.3 0.9 select_select_fusion.4
  269.8 0.9 select_select_fusion.4
  273.3 0.9 select_select_fusion.4
  276.8 0.9 select_select_fusion.4
  280.4 0.9 select_select_fusion.4
  283.9 0.9 select_select_fusion.4
  287.4 0.9 select_select_fusion.4
  290.9 0.9 select_select_fusion.4
  294.4 0.9 select_select_fusion.4
  297.9 0.9 select_select_fusion.4
  301.4 0.9 select_select_fusion.4
  305.0 0.9 select_select_fusion.4
  308.5 0.9 select_select_fusion.4
  312.0 0.9 select_select_fusion.4
  315.5 0.9 select_select_fusion.4
  319.0 0.9 select_select_fusion.4
  320.2 4.1 fusion.22
  325.1 1.0 fusion.17
  327.3 1.6 collective-permute-start
  328.9 2.6 fusion.9
  331.5 3.5 collective-permute-done
  335.0 1.4 fusion.3
  336.4 5.1 %add_add_fusion = f32[16,2,32,2240]{3,2,1,0:T(8,128)} fusion(f32[16,2,32,2240]{3,2,1,0:T(8,128)S(1)} %fusion.9, f32[16,2,32,2240]{3,2,1,0:T(8,128)S(1)} %fusion.3, bf16[16,2,32,224]{3,2,1,0:T(8,128)(2,1)S(1)} %collective-permute-done, bf16[3,224,2240]{2,1,0:T(8,128)(2,1)S(1)} %copy-done.5), kind=kOutput, calls=%fused_computation.6 | convolution fusion | flops 1032192000 | bytes 29605888 | tf_op jit(solution)/shard_map/yfxc,co->yfxo/dot_general | solution.py:92
  341.5 89.7 %reduce-scatter.2.cloned.1.call-done = f32[2,2,32,2240]{3,2,1,0:T(8,128)} async-done(((f32[16,2,32,2240]{3,2,1,0:T(8,128)}), f32[2,2,32,2240]{3,2,1,0:T(8,128)}) %reduce-scatter.2.cloned.1.call-update) | async-done | bytes 1146896 | tf_op jit(solution)/shard_map/reduce_scatter | solution.py:164
  431.2 2.4 multiply_convert_fusion
  (188 shorter events, 48.0 us)
Async XLA Ops:
  6.5 169.9 %all-gather.7.cloned.1.call-start = ((), (), s32[]{:S(2)}) async-start(), calls=%async_computation.2 | async-start | bytes 3784704 | tf_op jit(solution)/shard_map/all_gather | solution.py:15
  11.0 6.4 %copy-start.11 = (s32[2]{0:T(128)S(1)}, s32[2]{0:T(128)}, u32[]{:S(2)}) copy-start(s32[2]{0:T(128)} %param.16) | copy-start | bytes 28
  11.0 6.4 %copy-start.12 = (s32[16]{0:T(128)S(1)}, s32[16]{0:T(128)}, u32[]{:S(2)}) copy-start(s32[16]{0:T(128)} %param.17) | copy-start | bytes 196
  11.0 6.4 %copy-start.13 = (s32[32]{0:T(128)S(1)}, s32[32]{0:T(128)}, u32[]{:S(2)}) copy-start(s32[32]{0:T(128)} %param.18) | copy-start | bytes 388
  11.0 6.7 %copy-start.7 = (bf16[2,16,32,224]{3,2,1,0:T(8,128)(2,1)S(1)}, bf16[2,16,32,224]{3,2,1,0:T(8,128)(2,1)}, u32[]{:S(2)}) copy-start(bf16[2,16,32,224]{3,2,1,0:T(8,128)(2,1)} %param.15) | copy-start | bytes 1376260
  11.0 7.8 %copy-start.6 = (bf16[2,16,32,224]{3,2,1,0:T(8,128)(2,1)S(1)}, bf16[2,16,32,224]{3,2,1,0:T(8,128)(2,1)}, u32[]{:S(2)}) copy-start(bf16[2,16,32,224]{3,2,1,0:T(8,128)(2,1)} %param.13) | copy-start | bytes 1376260
  19.9 3.8 copy-start.1
  19.9 3.8 copy-start.2
  19.9 3.8 copy-start.3
  19.9 3.8 copy-start.4
  28.3 8.2 %copy-start.14 = (s32[2]{0:T(128)S(1)}, s32[2]{0:T(128)}, u32[]{:S(2)}) copy-start(s32[2]{0:T(128)} %param.19) | copy-start | bytes 28
  28.3 9.6 %copy-start.15 = (u32[256]{0:T(256)S(1)}, u32[256]{0:T(256)}, u32[]{:S(2)}) copy-start(u32[256]{0:T(256)} %constant.94) | copy-start | bytes 3076
  36.3 1.5 copy-start.8
  36.4 170.5 %all-gather.9.cloned.1.call-start = ((), (), s32[]{:S(2)}) async-start(), calls=%async_computation.3 | async-start | bytes 3784704 | tf_op jit(solution)/shard_map/all_gather | solution.py:15
  37.8 393.4 %reduce-scatter.2.cloned.1.call-start = ((), (), s32[]{:S(2)}) async-start(), calls=%async_computation.1 | async-start | bytes 10616832 | tf_op jit(solution)/shard_map/reduce_scatter | solution.py:164
  211.1 113.3 %copy-start.9 = (f32[2,2,112,112]{3,2,1,0:T(8,128)S(1)}, f32[2,2,112,112]{3,2,1,0:T(8,128)}, u32[]{:S(2)}) copy-start(f32[2,2,112,112]{3,2,1,0:T(8,128)} %copy-done.8) | copy-start | bytes 602116
  211.1 114.0 %copy-start = (f32[2,16,32,2,112]{4,2,1,3,0:T(8,128)S(1)}, f32[2,16,32,2,112]{4,2,1,3,0:T(8,128)}, u32[]{:S(2)}) copy-start(f32[2,16,32,2,112]{4,2,1,3,0:T(8,128)} %concatenate.10) | copy-start | bytes 2752516
  327.3 7.7 %copy-start.5 = (bf16[3,224,2240]{2,1,0:T(8,128)(2,1)S(1)}, bf16[3,224,2240]{2,1,0:T(8,128)(2,1)}, u32[]{:S(2)}) copy-start(bf16[3,224,2240]{2,1,0:T(8,128)(2,1)} %param.20) | copy-start | bytes 9031684
  327.3 7.7 %collective-permute-start = (bf16[16,2,32,224]{3,2,1,0:T(8,128)(2,1)S(1)}, bf16[16,2,32,224]{3,2,1,0:T(8,128)(2,1)S(1)}, u32[]{:S(2)}, u32[]{:S(2)}) collective-permute-start(bf16[16,2,32,224]{3,2,1,0:T(8,128)(2,1)S(1)} %bitcast.99), channel_id=1, source_target_pairs={{0,8},{8,16},{16,24},{24,32},{32,40},{40,48},{48,56},{56,64},{64,7... | collective-permute-start | bytes 1376264 | tf_op jit(solution)/shard_map/ppermute | solution.py:33
  341.4 89.8 %copy-start.10 = (f32[2240]{0:T(1024)S(1)}, f32[2240]{0:T(1024)}, u32[]{:S(2)}) copy-start(f32[2240]{0:T(1024)} %param.21) | copy-start | bytes 26884
Sparse Core Ops, SparseCore 0:
  36.5 80.5 all-gather.6
  119.7 77.3 all-gather.8
  341.6 89.5 reduce-scatter.1
where the time goes:
time: 443 us; the launch traced here: 440 us
  blocking collectives  132 us (30%)
  waiting for transfers between devices  93.3 us (21%)
  other arithmetic  72.5 us (16%)
  loops' own time  60.5 us (14%)
  local copies, waits for them, and re-layouts  47.1 us (11%)
  matrix products  19.6 us (4%)
  between operations  13.5 us (3%)
    reduce_scatter x1, waiting for transfers between devices, per_device(): lax.psum_scatter(conv_taps(extended, conv_weight, frame_count), 'head', s...  89.7 us
    all_gather x2, blocking collectives, prefix(): pieces = jax.tree.map(lambda part: lax.all_gather(part, axis), value)  67.5 us
    unnamed x1, blocking collectives  64.5 us
    another operation x2, loops' own time, prefix(): return lax.fori_loop(0, count - 1, step, so_far)  60.5 us
    select_n x124, other arithmetic, step(): jnp.where(position < mine, new, old)  59.6 us
    dynamic_slice x31, local copies, waits for them, and re-layouts, step(): longer = join(so_far, jax.tree.map(lambda part: part[position], pieces))  19.2 us
    concatenate x2, local copies, waits for them, and re-layouts, rotate(): jnp.concatenate([spin_part(values[..., :first_size], frame_pos, 0), spin_...  9.74 us
  transfers between devices with their start and end apart: 4, of which 2 were waited for; matrix products, arithmetic and copies ran while one was open for 9% of the time, Pallas kernels for 0%

commit v1 on v0

v1 whole, which is shorter than its diff:
```python
import functools

import jax
import jax.numpy as jnp
import numpy as np
from jax import lax
from jax.experimental import pallas as pl
from jax.experimental.pallas import tpu as pltpu
from jax.sharding import PartitionSpec as P

HD = 112
LANES = 2 * HD
SIDE = HD * 5 // 14 // 2 * 2
ROWS = 120
EPSILON = 1e-06
BF = jnp.bfloat16
F32 = jnp.float32


def lane_tables():
    first = HD - 2 * SIDE
    freq = np.zeros(LANES, np.float64)
    section = np.zeros(LANES, np.int32)
    pairing = np.zeros((LANES, LANES), np.float32)
    for head in range(2):
        start = head * HD
        for number, size in enumerate((first, SIDE, SIDE)):
            half = size // 2
            for j in range(half):
                low, high = start + j, start + j + half
                freq[low] = freq[high] = 10000.0 ** (-2.0 * j / size)
                section[low] = section[high] = number
                pairing[high, low] = -1.0
                pairing[low, high] = 1.0
            start += size
    same_head = (np.arange(LANES)[:, None] // HD == np.arange(LANES)[None, :] // HD).astype(np.float32)
    return freq.astype(np.float32), section, pairing, same_head


FREQ, SECTION, PAIRING, SAME_HEAD = lane_tables()


def split_hi_lo(value):
    hi = value.astype(BF)
    return hi, (value - hi.astype(F32)).astype(BF)


def dot(a, b):
    return jnp.dot(a, b, preferred_element_type=F32)


def dot_t(a, b):
    return lax.dot_general(a, b, (((0,), (0,)), ((), ())), preferred_element_type=F32)


def rotated(positive, time_cos, time_sin, side_cos, side_sin, pairing):
    height, width, lanes = positive.shape
    flat = positive.reshape(height * width, lanes)
    partner = dot(flat, pairing)
    cos = (side_cos[:height] + time_cos)[:, None, :] + side_cos[height:][None, :, :]
    sin = (side_sin[:height] + time_sin)[:, None, :] + side_sin[height:][None, :, :]
    wide = flat.astype(F32)
    return wide, wide * cos.reshape(height * width, lanes) + partner * sin.reshape(height * width, lanes)


def state_kernel(ids, k_ref, v_ref, tc_ref, ts_ref, sc_ref, ss_ref, pair_ref, out_ref):
    g = pl.program_id(0)
    key = jnp.maximum(k_ref[0], 0)
    wide, rot = rotated(key, tc_ref[pl.ds(g, 1)], ts_ref[pl.ds(g, 1)], sc_ref[...], ss_ref[...], pair_ref[...])
    value = v_ref[0].reshape(wide.shape)
    hi, lo = split_hi_lo(rot)
    outer = dot_t(hi, value) + dot_t(lo, value)
    lane = lax.broadcasted_iota(jnp.int32, (HD, LANES), 1)
    out_ref[0, :HD] = jnp.where(lane < HD, outer[:HD], outer[HD:])
    row = lax.broadcasted_iota(jnp.int32, (ROWS - HD, LANES), 0)
    total = jnp.broadcast_to(jnp.sum(wide, axis=0, keepdims=True), row.shape)
    block = ids[g].astype(F32)
    position = ids[2 + g].astype(F32)
    out_ref[0, HD:] = jnp.where(row == 0, total, jnp.where(row == 1, block, jnp.where(row == 2, position, 0.0)))


def attend_kernel(q_ref, halo_ref, st_ref, tc_ref, ts_ref, sc_ref, ss_ref, pair_ref, same_ref, out_ref):
    e = pl.program_id(0)
    query = jnp.maximum(jnp.where(e < 2, halo_ref[0], q_ref[0]), 0)
    height, width, lanes = query.shape
    wide, rot = rotated(query, tc_ref[pl.ds(e, 1)], ts_ref[pl.ds(e, 1)], sc_ref[...], ss_ref[...], pair_ref[...])
    packed = st_ref[0, :HD]
    lane = lax.broadcasted_iota(jnp.int32, (HD, LANES), 1)
    full = jnp.concatenate([jnp.where(lane < HD, packed, 0.0), jnp.where(lane < HD, 0.0, packed)], axis=0)
    state_hi, state_lo = split_hi_lo(full)
    rot_hi, rot_lo = split_hi_lo(rot)
    numerator = dot(rot_hi, state_hi) + dot(rot_lo, state_hi) + dot(rot_hi, state_lo)
    w_hi, w_lo = split_hi_lo(wide * st_ref[0, HD : HD + 1])
    denominator = dot(w_hi, same_ref[...]) + dot(w_lo, same_ref[...]) + EPSILON
    out_ref[...] = (numerator / denominator).astype(BF).reshape(height, 1, width, lanes)


def conv_kernel(count, idx, *refs):
    blocks = refs[: 2 * count]
    w_ref, send_ref, keep_ref = refs[2 * count :]
    rows = None
    for tap in range(3):
        lhs = jnp.concatenate([b[:, 2 - tap : 4 - tap].reshape(-1, LANES) for b in blocks], axis=0)
        part = dot(lhs, w_ref[tap])
        rows = part if rows is None else rows + part
    each = rows.shape[0] // (2 * count)
    shape = send_ref.shape[1:]
    for j in range(count):
        send_ref[j] = rows[2 * j * each : (2 * j + 1) * each].astype(BF).reshape(shape)
        keep_ref[j] = rows[(2 * j + 1) * each : (2 * j + 2) * each].reshape(shape)


def whole(shape):
    return pl.BlockSpec(shape, lambda *_: (0,) * len(shape))


def conv_group(extended, weight, index, count):
    _, frames, width, lanes = extended.shape
    c_out = weight.shape[-1]
    tile = 768
    steps = pl.cdiv(c_out, tile)

    def row_block(slot):
        return pl.BlockSpec((2, frames, width, lanes), lambda n, idx: (idx[slot], 0, 0, 0))

    out_block = pl.BlockSpec((count, 2, 2, width, tile), lambda n, idx: (0, 0, 0, 0, n))
    shape = (count, 2, 2, width, c_out)
    return pl.pallas_call(
        functools.partial(conv_kernel, count),
        grid_spec=pltpu.PrefetchScalarGridSpec(
            num_scalar_prefetch=1,
            grid=(steps,),
            in_specs=[row_block(s) for s in range(2 * count)]
            + [pl.BlockSpec((3, lanes, tile), lambda n, idx: (0, 0, n))],
            out_specs=[out_block, out_block],
        ),
        out_shape=[jax.ShapeDtypeStruct(shape, BF), jax.ShapeDtypeStruct(shape, F32)],
        name="conv",
    )(index, *([extended] * (2 * count)), weight)


def shifted(value, by):
    length = lax.axis_size("frame")
    return lax.ppermute(value, "frame", [(i, i + by) for i in range(length) if 0 <= i + by < length])


def moved(value, dy, dc):
    chips = lax.axis_size("head") // 2
    return lax.ppermute(
        value, "head", [(y * 2 + c, (y + dy) % chips * 2 + (c + dc) % 2) for y in range(chips) for c in range(2)]
    )


def angle_tables(positions, section):
    angles = positions.astype(F32)[:, None] * FREQ[None, :]
    mine = (SECTION == section)[None, :]
    return jnp.where(mine, jnp.cos(angles), 0.0), jnp.where(mine, jnp.sin(angles), 0.0)


def per_device(
    queries, key_vectors, value_vectors, frame_index, height_index, width_index, frame_block, conv_weight, conv_bias
):
    frames, height, width, lanes = queries.shape
    pairing = jnp.asarray(PAIRING, BF)
    same_head = jnp.asarray(SAME_HEAD, BF)
    time_cos, time_sin = angle_tables(frame_index, 0)
    row_cos, row_sin = angle_tables(height_index, 1)
    col_cos, col_sin = angle_tables(width_index, 2)
    side_cos = jnp.concatenate([row_cos, col_cos], axis=0)
    side_sin = jnp.concatenate([row_sin, col_sin], axis=0)
    frame_spec = pl.BlockSpec((1, height, width, lanes), lambda g, ids: (g, 0, 0, 0))
    packed = pl.pallas_call(
        state_kernel,
        grid_spec=pltpu.PrefetchScalarGridSpec(
            num_scalar_prefetch=1,
            grid=(frames,),
            in_specs=[frame_spec, frame_spec]
            + [whole((frames, lanes))] * 2
            + [whole((height + width, lanes))] * 2
            + [whole((lanes, lanes))],
            out_specs=pl.BlockSpec((1, ROWS, lanes), lambda g, ids: (g, 0, 0)),
        ),
        out_shape=jax.ShapeDtypeStruct((frames, ROWS, lanes), F32),
        name="frame_state",
    )(
        jnp.concatenate([frame_block, frame_index]),
        key_vectors, value_vectors, time_cos, time_sin, side_cos, side_sin, pairing,
    )
    first, second = packed[0], packed[1]
    is_id = lax.broadcasted_iota(jnp.int32, first.shape, 0) == HD + 1
    ids = frame_block.astype(F32)
    joined = ids[0] == ids[1]

    before = shifted(packed, 1)
    halo = shifted(queries, 1)
    previous = before[0] + before[1]
    running = first + second + previous
    earlier = jnp.zeros_like(first)
    length = lax.axis_size("frame")
    by = 2
    while by < length:
        arrived = shifted(running, by)
        earlier = earlier + arrived
        running = running + arrived
        by *= 2
    lead = jnp.where(is_id, first, first + jnp.where(joined, second, 0.0))
    next_lead = shifted(lead, -1)
    next_id = next_lead[HD + 1, 0]
    pair_lead = jnp.where(is_id, lead, lead + jnp.where(joined & (next_id == ids[0]), next_lead, 0.0))
    far_lead = shifted(pair_lead, -2)
    tail = jnp.where(next_id == ids[1], next_lead, 0.0) + jnp.where(far_lead[HD + 1, 0] == ids[1], far_lead, 0.0)

    upto = earlier + previous
    state_1 = upto + first + second + tail
    state_0 = jnp.where(joined, state_1, upto + first)
    id_a, id_b = before[0, HD + 1, 0], before[1, HD + 1, 0]
    state_b = jnp.where(id_b == ids[0], state_0, upto)
    state_a = jnp.where(id_a == id_b, state_b, earlier + before[0])
    states = jnp.stack([state_a, state_b, state_0, state_1])

    halo_cos, halo_sin = angle_tables(before[:, HD + 2, 0], 0)
    all_cos = jnp.concatenate([halo_cos, time_cos], axis=0)
    all_sin = jnp.concatenate([halo_sin, time_sin], axis=0)
    extended = pl.pallas_call(
        attend_kernel,
        grid=(2 * frames,),
        in_specs=[
            pl.BlockSpec((1, height, width, lanes), lambda e: (jnp.maximum(e - 2, 0), 0, 0, 0)),
            pl.BlockSpec((1, height, width, lanes), lambda e: (jnp.minimum(e, 1), 0, 0, 0)),
            pl.BlockSpec((1, ROWS, lanes), lambda e: (e, 0, 0)),
            whole((2 * frames, lanes)), whole((2 * frames, lanes)),
            whole((height + width, lanes)), whole((height + width, lanes)),
            whole((lanes, lanes)), whole((lanes, lanes)),
        ],
        out_specs=pl.BlockSpec((height, 1, width, lanes), lambda e: (0, e, 0, 0)),
        out_shape=jax.ShapeDtypeStruct((height, 2 * frames, width, lanes), BF),
        name="attend",
    )(queries, halo, states, all_cos, all_sin, side_cos, side_sin, pairing, same_head)

    head = lax.axis_index("head")
    chips = lax.axis_size("head") // 2
    chip, core = head // 2, head % 2

    def slots(relatives):
        return jnp.stack([(chip + j) % chips * 2 + c for j in relatives for c in (1 - core, core)]).astype(jnp.int32)

    def chip_sums(relatives):
        send, keep = conv_group(extended, conv_weight, slots(relatives), len(relatives))
        return keep + moved(send, 0, 1).astype(F32)

    far = chip_sums((2,))
    from_far = moved(far[0].astype(BF), 2, 0)
    near = chip_sums((1, 3))
    from_low = moved(near[0].astype(BF), 1, 0)
    from_high = moved(near[1].astype(BF), 3, 0)
    own = chip_sums((0,))
    summed = own[0] + from_far.astype(F32) + from_low.astype(F32) + from_high.astype(F32)
    return jax.nn.silu(summed + conv_bias).astype(BF)


def solution(mesh):
    placed = (
        P("frame", None, None, "head"),
        P("frame", None, None, "head"),
        P("frame", None, None, "head"),
        P("frame"),
        P(),
        P(),
        P("frame"),
        P(None, "head", None),
        P(),
    )
    return jax.shard_map(
        per_device,
        mesh=mesh,
        in_specs=placed,
        out_specs=P("head", "frame", None, None),
        check_vma=False,
    )
```

time: 443 us -> 129 us (0.29)
  blocking collectives: 132 us -> 0 us
  waiting for transfers between devices: 93.3 us -> 28.8 us
  loops' own time: 60.5 us -> 0 us
  other arithmetic: 72.5 us -> 14 us
  starting transfers between devices: 1.67 us -> 48.8 us
  local copies, waits for them, and re-layouts: 47.1 us -> 3.23 us
  Pallas kernels: 0 us -> 25.8 us
  matrix products: 19.6 us -> 0 us
  between operations: 13.5 us -> 7.62 us
    reduce_scatter x1 -> x0, waiting for transfers between devices: 89.7 us -> none  [per_device(): lax.psum_scatter(conv_taps(extended, conv_weight, frame_count), 'head', s...]
    all_gather x2 -> x0, blocking collectives: 67.5 us -> none  [prefix(): pieces = jax.tree.map(lambda part: lax.all_gather(part, axis), value)]
    unnamed x1 -> x0, blocking collectives: 64.5 us -> none
    another operation x2 -> x0, loops' own time: 60.5 us -> none  [prefix(): return lax.fori_loop(0, count - 1, step, so_far)]
    select_n x124 -> x5, other arithmetic: 59.6 us -> 3.32 us  [the longest x4 3.23 us: angle_tables(): jnp.where(mine, jnp.sin(angles), 0.0)]
    ppermute x1 -> x14, starting transfers between devices: 1.59 us -> 48.8 us  [the longest x8 41.2 us: shifted(): lax.ppermute(value, 'frame', [(i, i + by) for i in range(length) if 0 <=...]
    pallas_call x0 -> x5, Pallas kernels: none -> 25.8 us  [the longest x3 16.7 us: conv_group(): pl.pallas_call(functools.partial(conv_kernel, count), grid_spec=pltpu.Pre...]
    ppermute x1 -> x14, waiting for transfers between devices: 3.46 us -> 28.8 us  [the longest x6 24.6 us: moved(): lax.ppermute(value, 'head', [(y * 2 + c, (y + dy) % chips * 2 + (c + dc)...]
  transfers between devices with their start and end apart: 4 -> 14, of which waited for: 2 -> 5; matrix products, arithmetic and copies ran while one was open for 9% -> 12% of each run, Pallas kernels for 0% -> 12%
where the time goes in v1:
time: 129 us; the launch traced here: 128 us
  starting transfers between devices  48.8 us (38%)
  waiting for transfers between devices  28.8 us (22%)
  Pallas kernels  25.8 us (20%)
  other arithmetic  14 us (11%)
  between operations  7.62 us (6%)
  local copies, waits for them, and re-layouts  3.23 us (3%)
    ppermute x8, starting transfers between devices, shifted(): lax.ppermute(value, 'frame', [(i, i + by) for i in range(length) if 0 <=...  41.2 us
    ppermute x6, waiting for transfers between devices, moved(): lax.ppermute(value, 'head', [(y * 2 + c, (y + dy) % chips * 2 + (c + dc)...  24.6 us
    pallas_call x3, Pallas kernels, conv_group(): pl.pallas_call(functools.partial(conv_kernel, count), grid_spec=pltpu.Pre...  16.7 us
    ppermute x6, starting transfers between devices, moved(): lax.ppermute(value, 'head', [(y * 2 + c, (y + dy) % chips * 2 + (c + dc)...  7.68 us
    pallas_call x1, Pallas kernels, per_device(): pl.pallas_call(attend_kernel, grid=(2 * frames,), in_specs=[pl.BlockSpec(...  5.34 us
    ppermute x8, waiting for transfers between devices, shifted(): lax.ppermute(value, 'frame', [(i, i + by) for i in range(length) if 0 <=...  4.25 us
    pallas_call x1, Pallas kernels, per_device(): pl.pallas_call(state_kernel, grid_spec=pltpu.PrefetchScalarGridSpec(num_s...  3.74 us
    select_n x4, other arithmetic, angle_tables(): jnp.where(mine, jnp.sin(angles), 0.0)  3.23 us
  transfers between devices with their start and end apart: 14, of which 5 were waited for; matrix products, arithmetic and copies ran while one was open for 12% of the time, Pallas kernels for 12%

profile of v1, /device:TPU:1, one launch (start us, length us, event | category | flops | bytes accessed | tf_op | source)
XLA Modules:
  0.0 128.4 jit_solution(16313024650357070828)
XLA Ops:
  0.0 4.5 %collective-permute-start = (bf16[2,16,32,224]{3,2,1,0:T(8,128)(2,1)}, bf16[2,16,32,224]{3,2,1,0:T(8,128)(2,1)S(1)}, u32[]{:S(2)}, u32[]{:S(2)}) collective-permute-start(bf16[2,16,32,224]{3,2,1,0:T(8,128)(2,1)} %q_ref.1), channel_id=1, source_target_pairs={{0,8},{8,16},{16,24},{24,32},{32,40},{40,48},{48,56},{56,64},{64,7... | collective-permute-start | bytes 1376264 | tf_op jit(solution)/shard_map/ppermute | solution.py:144
  4.5 0.7 convert_element_type.47
  5.2 1.2 pad_add_fusion.1.ids
  6.4 0.7 convert_element_type.49
  7.1 0.7 convert_element_type.48
  7.7 1.4 %fusion.13 = (f32[2,224]{1,0:T(2,128)}, f32[2,224]{1,0:T(2,128)}) fusion(pred[224]{0:T(512)(128)(4,1)} %constant.90, f32[224]{0:T(256)} %constant.91, f32[2]{0:T(128)S(1)} %convert_element_type.47), kind=kLoop, calls=%fused_computation.44 | loop fusion | flops 1344 | bytes 4712 | tf_op jit(solution)/shard_map/jit(_where)/select_n | solution.py:157
  9.2 0.9 fusion.8
  10.0 0.8 fusion.11
  10.9 0.6 pad_maximum_fusion.1.sc_ref
  11.5 0.6 pad_maximum_fusion.2.ss_ref
  12.1 3.7 %frame_state.1 = f32[2,120,224]{2,1,0:T(8,128)} custom-call(s32[4]{0:T(128)} %pad_add_fusion.1.ids, bf16[2,16,32,224]{3,2,1,0:T(8,128)(2,1)} %k_ref.1, bf16[2,16,32,224]{3,2,1,0:T(8,128)(2,1)} %v_ref.1, f32[2,224]{1,0:T(2,128)} %get-tuple-element.36.tc_ref, f32[2,224]{1,0:T(2,128)} %get-tuple-element.35.ts_ref, f32[48,224]{1,0:T(8,128)} %pad_maximum_fusion.1.sc_ref, ...), custom_call_target="tpu_custom_call" | custom-call | tf_op jit(solution)/shard_map/frame_state/pallas_call | solution.py:172
  15.9 3.5 %collective-permute-start.1 = (f32[2,120,224]{2,1,0:T(8,128)}, f32[2,120,224]{2,1,0:T(8,128)S(1)}, u32[]{:S(2)}, u32[]{:S(2)}) collective-permute-start(f32[2,120,224]{2,1,0:T(8,128)} %frame_state.1), channel_id=1, source_target_pairs={{0,8},{8,16},{16,24},{24,32},{32,40},{40,48},{48,56},{56,64},{64,7... | collective-permute-start | bytes 645128 | tf_op jit(solution)/shard_map/ppermute | solution.py:144
  19.4 0.6 fusion.18
  21.2 0.6 pad_add_fusion.2.idx
  21.8 2.2 %collective-permute-done.1 = f32[2,120,224]{2,1,0:T(8,128)S(1)} collective-permute-done((f32[2,120,224]{2,1,0:T(8,128)}, f32[2,120,224]{2,1,0:T(8,128)S(1)}, u32[]{:S(2)}, u32[]{:S(2)}) %collective-permute-start.1) | collective-permute-done | bytes 215072 | tf_op jit(solution)/shard_map/ppermute | solution.py:144
  24.0 1.1 add_add_fusion.2
  25.1 1.3 %collective-permute-start.6 = (f32[120,224]{1,0:T(8,128)S(1)}, f32[120,224]{1,0:T(8,128)S(1)}, u32[]{:S(2)}, u32[]{:S(2)}) collective-permute-start(f32[120,224]{1,0:T(8,128)S(1)} %get-tuple-element.26), channel_id=1, source_target_pairs={{8,0},{16,8},{24,16},{32,24},{40,32},{48,40},{56,48},{64,56},{72,6... | collective-permute-start | bytes 322568 | tf_op jit(solution)/shard_map/ppermute | solution.py:144
  26.4 6.7 %collective-permute-start.2 = (f32[120,224]{1,0:T(8,128)S(1)}, f32[120,224]{1,0:T(8,128)S(1)}, u32[]{:S(2)}, u32[]{:S(2)}) collective-permute-start(f32[120,224]{1,0:T(8,128)S(1)} %get-tuple-element.20), channel_id=1, source_target_pairs={{0,16},{8,24},{16,32},{24,40},{32,48},{40,56},{48,64},{56,72},{64,... | collective-permute-start | bytes 322568 | tf_op jit(solution)/shard_map/ppermute | solution.py:144
  33.1 0.1 slice_reduce_fusion
  33.2 0.1 fusion.15
  33.3 1.6 %collective-permute-done.2 = f32[120,224]{1,0:T(8,128)S(1)} collective-permute-done((f32[120,224]{1,0:T(8,128)S(1)}, f32[120,224]{1,0:T(8,128)S(1)}, u32[]{:S(2)}, u32[]{:S(2)}) %collective-permute-start.2) | collective-permute-done | bytes 107552 | tf_op jit(solution)/shard_map/ppermute | solution.py:144
  35.0 10.2 %collective-permute-start.3 = (f32[120,224]{1,0:T(8,128)S(1)}, f32[120,224]{1,0:T(8,128)S(1)}, u32[]{:S(2)}, u32[]{:S(2)}) collective-permute-start(f32[120,224]{1,0:T(8,128)S(1)} %add.146), channel_id=1, source_target_pairs={{0,32},{8,40},{16,48},{24,56},{32,64},{40,72},{48,80},{56,88},{64,... | collective-permute-start | bytes 322568 | tf_op jit(solution)/shard_map/ppermute | solution.py:144
  45.2 0.5 fusion.17
  48.2 0.0 collective-permute-done.6
  48.2 0.5 slice.65
  49.9 0.0 collective-permute-done.3
  50.0 6.9 %collective-permute-start.4 = (f32[120,224]{1,0:T(8,128)S(1)}, f32[120,224]{1,0:T(8,128)S(1)}, u32[]{:S(2)}, u32[]{:S(2)}) collective-permute-start(f32[120,224]{1,0:T(8,128)S(1)} %add.148), channel_id=1, source_target_pairs={{0,64},{8,72},{16,80},{24,88},{32,96},{40,104},{48,112},{56,120},{... | collective-permute-start | bytes 322568 | tf_op jit(solution)/shard_map/ppermute | solution.py:144
  56.9 0.1 add_select_fusion
  57.0 1.3 %collective-permute-start.7 = (f32[120,224]{1,0:T(8,128)S(1)}, f32[120,224]{1,0:T(8,128)S(1)}, u32[]{:S(2)}, u32[]{:S(2)}) collective-permute-start(f32[120,224]{1,0:T(8,128)S(1)} %add_select_fusion), channel_id=1, source_target_pairs={{16,0},{24,8},{32,16},{40,24},{48,32},{56,40},{64,48},{72,56},{80,... | collective-permute-start | bytes 322568 | tf_op jit(solution)/shard_map/ppermute | solution.py:144
  58.3 0.4 collective-permute-done.4
  58.7 6.7 %collective-permute-start.5 = (f32[120,224]{1,0:T(8,128)S(1)}, f32[120,224]{1,0:T(8,128)S(1)}, u32[]{:S(2)}, u32[]{:S(2)}) collective-permute-start(f32[120,224]{1,0:T(8,128)S(1)} %add.150), channel_id=1, source_target_pairs={{0,128},{8,136},{16,144},{24,152},{32,160},{40,168},{48,176},{56,1... | collective-permute-start | bytes 322568 | tf_op jit(solution)/shard_map/ppermute | solution.py:144
  65.5 0.6 pad_maximum_fusion.3
  67.3 0.0 collective-permute-done.7
  67.3 0.6 slice.66
  69.1 0.0 collective-permute-done.5
  69.1 0.0 copy-done
  69.2 0.1 select_bitcast_fusion
  69.3 0.8 pad_maximum_fusion.st_ref
  70.1 0.0 collective-permute-done.halo_ref
  70.1 0.8 copy-done.4
  70.9 5.3 %attend.1.refs_0_.refs_1_.refs_2_.refs_3_ = bf16[16,4,32,224]{3,2,1,0:T(8,128)(2,1)} custom-call(bf16[2,16,32,224]{3,2,1,0:T(8,128)(2,1)} %q_ref.1, bf16[2,16,32,224]{3,2,1,0:T(8,128)(2,1)} %copy-done.4, f32[4,120,224]{2,1,0:T(8,128)} %pad_maximum_fusion.st_ref, f32[4,224]{1,0:T(4,128)} %get-tuple-element.39.tc_ref, f32[4,224]{1,0:T(4,128)} %get-tuple-element.40.ts_ref, ...), custom_call_target="tpu_custom_call" | custom-call | tf_op jit(solution)/shard_map/attend/pallas_call | solution.py:224
  76.3 5.2 %conv.4 = (bf16[1,2,2,32,2240]{4,3,2,1,0:T(8,128)(2,1)}, f32[1,2,2,32,2240]{4,3,2,1,0:T(8,128)}) custom-call(s32[2]{0:T(128)} %pad_add_fusion.2.idx, bf16[16,4,32,224]{3,2,1,0:T(8,128)(2,1)} %attend.1.refs_0_.refs_1_.refs_2_.refs_3_, bf16[16,4,32,224]{3,2,1,0:T(8,128)(2,1)} %attend.1.refs_0_.refs_1_.refs_2_.refs_3_, bf16[3,224,2240]{2,1,0:T(8,128)(2,1)} %refs_4_.1), custom_call_target="tpu_custom_call" | custom-call | tf_op jit(solution)/shard_map/conv/pallas_call | solution.py:128
  81.5 2.7 %collective-permute-start.9 = (bf16[1,2,2,32,2240]{4,3,2,1,0:T(8,128)(2,1)}, bf16[1,2,2,32,2240]{4,3,2,1,0:T(8,128)(2,1)S(1)}, u32[]{:S(2)}, u32[]{:S(2)}) collective-permute-start(bf16[1,2,2,32,2240]{4,3,2,1,0:T(8,128)(2,1)} %get-tuple-element.14), channel_id=1, source_target_pairs={{0,1},{1,0},{2,3},{3,2},{4,5},{5,4},{6,7},{7,6},{8,9},{9,8},{10,11... | collective-permute-start | bytes 1720328 | tf_op jit(solution)/shard_map/ppermute | solution.py:149
  84.1 0.6 pad_add_fusion.3.idx
  84.7 6.2 %conv.5 = (bf16[2,2,2,32,2240]{4,3,2,1,0:T(8,128)(2,1)}, f32[2,2,2,32,2240]{4,3,2,1,0:T(8,128)}) custom-call(s32[4]{0:T(128)} %pad_add_fusion.3.idx, bf16[16,4,32,224]{3,2,1,0:T(8,128)(2,1)} %attend.1.refs_0_.refs_1_.refs_2_.refs_3_, bf16[16,4,32,224]{3,2,1,0:T(8,128)(2,1)} %attend.1.refs_0_.refs_1_.refs_2_.refs_3_, ...), custom_call_target="tpu_custom_call" | custom-call | tf_op jit(solution)/shard_map/conv/pallas_call | solution.py:128
  91.0 0.0 collective-permute-start.11
  91.0 0.6 pad_add_fusion.idx
  91.6 5.3 %conv.3 = (bf16[1,2,2,32,2240]{4,3,2,1,0:T(8,128)(2,1)}, f32[1,2,2,32,2240]{4,3,2,1,0:T(8,128)}) custom-call(s32[2]{0:T(128)} %pad_add_fusion.idx, bf16[16,4,32,224]{3,2,1,0:T(8,128)(2,1)} %attend.1.refs_0_.refs_1_.refs_2_.refs_3_, bf16[16,4,32,224]{3,2,1,0:T(8,128)(2,1)} %attend.1.refs_0_.refs_1_.refs_2_.refs_3_, bf16[3,224,2240]{2,1,0:T(8,128)(2,1)} %refs_4_.1), custom_call_target="tpu_custom_call" | custom-call | tf_op jit(solution)/shard_map/conv/pallas_call | solution.py:128
  96.9 0.5 collective-permute-start.8
  97.4 0.0 collective-permute-done.9
  97.4 0.0 copy-done.3
  97.4 0.1 fusion.3
  97.5 3.0 %collective-permute-start.10 = (bf16[2,2,32,2240]{3,2,1,0:T(8,128)(2,1)S(1)}, bf16[2,2,32,2240]{3,2,1,0:T(8,128)(2,1)S(1)}, u32[]{:S(2)}, u32[]{:S(2)}) collective-permute-start(bf16[2,2,32,2240]{3,2,1,0:T(8,128)(2,1)S(1)} %fusion.3), channel_id=1, source_target_pairs={{0,4},{1,5},{2,6},{3,7},{4,0},{5,1},{6,2},{7,3},{8,12},{9,13},{10,... | collective-permute-start | bytes 1720328 | tf_op jit(solution)/shard_map/ppermute | solution.py:149
  100.5 0.0 collective-permute-done.11
  100.5 0.3 add_convert_fusion
  100.8 0.0 copy-start.8
  100.8 0.1 slice_bitcast_fusion.1
  100.9 1.4 %collective-permute-start.13 = (bf16[2,2,32,2240]{3,2,1,0:T(8,128)(2,1)S(1)}, bf16[2,2,32,2240]{3,2,1,0:T(8,128)(2,1)S(1)}, u32[]{:S(2)}, u32[]{:S(2)}) collective-permute-start(bf16[2,2,32,2240]{3,2,1,0:T(8,128)(2,1)S(1)} %get-tuple-element.23), channel_id=1, source_target_pairs={{0,6},{1,7},{2,0},{3,1},{4,2},{5,3},{6,4},{7,5},{8,14},{9,15},{10,... | collective-permute-start | bytes 1720328 | tf_op jit(solution)/shard_map/ppermute | solution.py:149
  102.2 0.2 collective-permute-start.12
  102.4 0.0 collective-permute-done.8
  102.4 11.5 %collective-permute-done.10 = bf16[2,2,32,2240]{3,2,1,0:T(8,128)(2,1)S(1)} collective-permute-done((bf16[2,2,32,2240]{3,2,1,0:T(8,128)(2,1)S(1)}, bf16[2,2,32,2240]{3,2,1,0:T(8,128)(2,1)S(1)}, u32[]{:S(2)}, u32[]{:S(2)}) %collective-permute-start.10) | collective-permute-done | bytes 573472 | tf_op jit(solution)/shard_map/ppermute | solution.py:149
  113.9 13.0 %collective-permute-done.13 = bf16[2,2,32,2240]{3,2,1,0:T(8,128)(2,1)S(1)} collective-permute-done((bf16[2,2,32,2240]{3,2,1,0:T(8,128)(2,1)S(1)}, bf16[2,2,32,2240]{3,2,1,0:T(8,128)(2,1)S(1)}, u32[]{:S(2)}, u32[]{:S(2)}) %collective-permute-start.13) | collective-permute-done | bytes 573472 | tf_op jit(solution)/shard_map/ppermute | solution.py:149
  126.9 0.0 collective-permute-done.12
  127.0 1.4 %multiply_convert_fusion = bf16[2,2,32,2240]{3,2,1,0:T(8,128)(2,1)} fusion(bf16[2,2,32,2240]{3,2,1,0:T(8,128)(2,1)S(1)} %collective-permute-done.13, bf16[2,2,32,2240]{3,2,1,0:T(8,128)(2,1)S(1)} %collective-permute-done.12, bf16[2,2,32,2240]{3,2,1,0:T(8,128)(2,1)S(1)} %collective-permute-done.10, f32[1,2,2,32,2240]{4,3,2,1,0:T(8,128)S(1)} %copy-done.2, ...), kind=kLoop, calls=%fused_computation.5 | loop fusion | flops 4014080 | bytes 4023040 | tf_op jit(solution)/shard_map/convert_element_type | solution.py:258
  (24 shorter events, 0.1 us)
Async XLA Ops:
  0.0 19.4 %copy-start.10 = (s32[2]{0:T(128)S(1)}, s32[2]{0:T(128)}, u32[]{:S(2)}) copy-start(s32[2]{0:T(128)} %param.25) | copy-start | bytes 28
  0.0 70.1 %collective-permute-start = (bf16[2,16,32,224]{3,2,1,0:T(8,128)(2,1)}, bf16[2,16,32,224]{3,2,1,0:T(8,128)(2,1)S(1)}, u32[]{:S(2)}, u32[]{:S(2)}) collective-permute-start(bf16[2,16,32,224]{3,2,1,0:T(8,128)(2,1)} %q_ref.1), channel_id=1, source_target_pairs={{0,8},{8,16},{16,24},{24,32},{32,40},{40,48},{48,56},{56,64},{64,7... | collective-permute-start | bytes 1376264 | tf_op jit(solution)/shard_map/ppermute | solution.py:144
  12.1 21.1 %copy-start.7 = (f32[224]{0:T(256)S(1)}, f32[224]{0:T(256)}, u32[]{:S(2)}) copy-start(f32[224]{0:T(256)} %constant.91) | copy-start | bytes 2692
  12.1 21.1 %copy-start.9 = (pred[224]{0:T(512)(128)(4,1)S(1)}, pred[224]{0:T(512)(128)(4,1)}, u32[]{:S(2)}) copy-start(pred[224]{0:T(512)(128)(4,1)} %constant.90) | copy-start | bytes 676
  15.9 8.2 %collective-permute-start.1 = (f32[2,120,224]{2,1,0:T(8,128)}, f32[2,120,224]{2,1,0:T(8,128)S(1)}, u32[]{:S(2)}, u32[]{:S(2)}) collective-permute-start(f32[2,120,224]{2,1,0:T(8,128)} %frame_state.1), channel_id=1, source_target_pairs={{0,8},{8,16},{16,24},{24,32},{32,40},{40,48},{48,56},{56,64},{64,7... | collective-permute-start | bytes 645128 | tf_op jit(solution)/shard_map/ppermute | solution.py:144
  21.8 43.7 %copy-start.5 = (f32[2,224]{1,0:T(2,128)S(1)}, f32[2,224]{1,0:T(2,128)}, u32[]{:S(2)}) copy-start(f32[2,224]{1,0:T(2,128)} %get-tuple-element.35.ts_ref) | copy-start | bytes 5380
  21.8 43.7 %copy-start.6 = (f32[2,224]{1,0:T(2,128)S(1)}, f32[2,224]{1,0:T(2,128)}, u32[]{:S(2)}) copy-start(f32[2,224]{1,0:T(2,128)} %get-tuple-element.36.tc_ref) | copy-start | bytes 5380
  21.8 47.3 %copy-start = (f32[2,120,224]{2,1,0:T(8,128)S(1)}, f32[2,120,224]{2,1,0:T(8,128)}, u32[]{:S(2)}) copy-start(f32[2,120,224]{2,1,0:T(8,128)} %frame_state.1) | copy-start | bytes 645124
  25.1 23.1 %collective-permute-start.6 = (f32[120,224]{1,0:T(8,128)S(1)}, f32[120,224]{1,0:T(8,128)S(1)}, u32[]{:S(2)}, u32[]{:S(2)}) collective-permute-start(f32[120,224]{1,0:T(8,128)S(1)} %get-tuple-element.26), channel_id=1, source_target_pairs={{8,0},{16,8},{24,16},{32,24},{40,32},{48,40},{56,48},{64,56},{72,6... | collective-permute-start | bytes 322568 | tf_op jit(solution)/shard_map/ppermute | solution.py:144
  26.4 8.6 %collective-permute-start.2 = (f32[120,224]{1,0:T(8,128)S(1)}, f32[120,224]{1,0:T(8,128)S(1)}, u32[]{:S(2)}, u32[]{:S(2)}) collective-permute-start(f32[120,224]{1,0:T(8,128)S(1)} %get-tuple-element.20), channel_id=1, source_target_pairs={{0,16},{8,24},{16,32},{24,40},{32,48},{40,56},{48,64},{56,72},{64,... | collective-permute-start | bytes 322568 | tf_op jit(solution)/shard_map/ppermute | solution.py:144
  35.0 15.0 %collective-permute-start.3 = (f32[120,224]{1,0:T(8,128)S(1)}, f32[120,224]{1,0:T(8,128)S(1)}, u32[]{:S(2)}, u32[]{:S(2)}) collective-permute-start(f32[120,224]{1,0:T(8,128)S(1)} %add.146), channel_id=1, source_target_pairs={{0,32},{8,40},{16,48},{24,56},{32,64},{40,72},{48,80},{56,88},{64,... | collective-permute-start | bytes 322568 | tf_op jit(solution)/shard_map/ppermute | solution.py:144
  50.0 8.7 %collective-permute-start.4 = (f32[120,224]{1,0:T(8,128)S(1)}, f32[120,224]{1,0:T(8,128)S(1)}, u32[]{:S(2)}, u32[]{:S(2)}) collective-permute-start(f32[120,224]{1,0:T(8,128)S(1)} %add.148), channel_id=1, source_target_pairs={{0,64},{8,72},{16,80},{24,88},{32,96},{40,104},{48,112},{56,120},{... | collective-permute-start | bytes 322568 | tf_op jit(solution)/shard_map/ppermute | solution.py:144
  57.0 10.3 %collective-permute-start.7 = (f32[120,224]{1,0:T(8,128)S(1)}, f32[120,224]{1,0:T(8,128)S(1)}, u32[]{:S(2)}, u32[]{:S(2)}) collective-permute-start(f32[120,224]{1,0:T(8,128)S(1)} %add_select_fusion), channel_id=1, source_target_pairs={{16,0},{24,8},{32,16},{40,24},{48,32},{56,40},{64,48},{72,56},{80,... | collective-permute-start | bytes 322568 | tf_op jit(solution)/shard_map/ppermute | solution.py:144
  58.7 10.4 %collective-permute-start.5 = (f32[120,224]{1,0:T(8,128)S(1)}, f32[120,224]{1,0:T(8,128)S(1)}, u32[]{:S(2)}, u32[]{:S(2)}) collective-permute-start(f32[120,224]{1,0:T(8,128)S(1)} %add.150), channel_id=1, source_target_pairs={{0,128},{8,136},{16,144},{24,152},{32,160},{40,168},{48,176},{56,1... | collective-permute-start | bytes 322568 | tf_op jit(solution)/shard_map/ppermute | solution.py:144
  70.1 0.8 copy-start.4
  81.5 15.9 %collective-permute-start.9 = (bf16[1,2,2,32,2240]{4,3,2,1,0:T(8,128)(2,1)}, bf16[1,2,2,32,2240]{4,3,2,1,0:T(8,128)(2,1)S(1)}, u32[]{:S(2)}, u32[]{:S(2)}) collective-permute-start(bf16[1,2,2,32,2240]{4,3,2,1,0:T(8,128)(2,1)} %get-tuple-element.14), channel_id=1, source_target_pairs={{0,1},{1,0},{2,3},{3,2},{4,5},{5,4},{6,7},{7,6},{8,9},{9,8},{10,11... | collective-permute-start | bytes 1720328 | tf_op jit(solution)/shard_map/ppermute | solution.py:149
  91.0 9.5 %collective-permute-start.11 = (bf16[2,2,2,32,2240]{4,3,2,1,0:T(8,128)(2,1)}, bf16[2,2,2,32,2240]{4,3,2,1,0:T(8,128)(2,1)S(1)}, u32[]{:S(2)}, u32[]{:S(2)}) collective-permute-start(bf16[2,2,2,32,2240]{4,3,2,1,0:T(8,128)(2,1)} %get-tuple-element.16), channel_id=1, source_target_pairs={{0,1},{1,0},{2,3},{3,2},{4,5},{5,4},{6,7},{7,6},{8,9},{9,8},{10,11... | collective-permute-start | bytes 3440648 | tf_op jit(solution)/shard_map/ppermute | solution.py:149
  91.6 5.8 %copy-start.3 = (f32[1,2,2,32,2240]{4,3,2,1,0:T(8,128)S(1)}, f32[1,2,2,32,2240]{4,3,2,1,0:T(8,128)}, u32[]{:S(2)}) copy-start(f32[1,2,2,32,2240]{4,3,2,1,0:T(8,128)} %get-tuple-element.13) | copy-start | bytes 3440644
  96.9 5.5 %collective-permute-start.8 = (bf16[1,2,2,32,2240]{4,3,2,1,0:T(8,128)(2,1)}, bf16[1,2,2,32,2240]{4,3,2,1,0:T(8,128)(2,1)S(1)}, u32[]{:S(2)}, u32[]{:S(2)}) collective-permute-start(bf16[1,2,2,32,2240]{4,3,2,1,0:T(8,128)(2,1)} %get-tuple-element.12), channel_id=1, source_target_pairs={{0,1},{1,0},{2,3},{3,2},{4,5},{5,4},{6,7},{7,6},{8,9},{9,8},{10,11... | collective-permute-start | bytes 1720328 | tf_op jit(solution)/shard_map/ppermute | solution.py:149
  97.4 3.1 %copy-start.1 = (f32[2,2,2,32,2240]{4,3,2,1,0:T(8,128)S(1)}, f32[2,2,2,32,2240]{4,3,2,1,0:T(8,128)}, u32[]{:S(2)}) copy-start(f32[2,2,2,32,2240]{4,3,2,1,0:T(8,128)} %get-tuple-element.15) | copy-start | bytes 6881284
  97.5 16.5 %collective-permute-start.10 = (bf16[2,2,32,2240]{3,2,1,0:T(8,128)(2,1)S(1)}, bf16[2,2,32,2240]{3,2,1,0:T(8,128)(2,1)S(1)}, u32[]{:S(2)}, u32[]{:S(2)}) collective-permute-start(bf16[2,2,32,2240]{3,2,1,0:T(8,128)(2,1)S(1)} %fusion.3), channel_id=1, source_target_pairs={{0,4},{1,5},{2,6},{3,7},{4,0},{5,1},{6,2},{7,3},{8,12},{9,13},{10,... | collective-permute-start | bytes 1720328 | tf_op jit(solution)/shard_map/ppermute | solution.py:149
  100.8 26.2 %copy-start.2 = (f32[1,2,2,32,2240]{4,3,2,1,0:T(8,128)S(1)}, f32[1,2,2,32,2240]{4,3,2,1,0:T(8,128)}, u32[]{:S(2)}) copy-start(f32[1,2,2,32,2240]{4,3,2,1,0:T(8,128)} %get-tuple-element.11) | copy-start | bytes 3440644
  100.8 26.2 %copy-start.8 = (f32[2240]{0:T(1024)S(1)}, f32[2240]{0:T(1024)}, u32[]{:S(2)}) copy-start(f32[2240]{0:T(1024)} %param.27) | copy-start | bytes 26884
  100.9 26.1 %collective-permute-start.13 = (bf16[2,2,32,2240]{3,2,1,0:T(8,128)(2,1)S(1)}, bf16[2,2,32,2240]{3,2,1,0:T(8,128)(2,1)S(1)}, u32[]{:S(2)}, u32[]{:S(2)}) collective-permute-start(bf16[2,2,32,2240]{3,2,1,0:T(8,128)(2,1)S(1)} %get-tuple-element.23), channel_id=1, source_target_pairs={{0,6},{1,7},{2,0},{3,1},{4,2},{5,3},{6,4},{7,5},{8,14},{9,15},{10,... | collective-permute-start | bytes 1720328 | tf_op jit(solution)/shard_map/ppermute | solution.py:149
  102.2 24.7 %collective-permute-start.12 = (bf16[2,2,32,2240]{3,2,1,0:T(8,128)(2,1)S(1)}, bf16[2,2,32,2240]{3,2,1,0:T(8,128)(2,1)S(1)}, u32[]{:S(2)}, u32[]{:S(2)}) collective-permute-start(bf16[2,2,32,2240]{3,2,1,0:T(8,128)(2,1)S(1)} %get-tuple-element.22), channel_id=1, source_target_pairs={{0,2},{1,3},{2,4},{3,5},{4,6},{5,7},{6,0},{7,1},{8,10},{9,11},{10,... | collective-permute-start | bytes 1720328 | tf_op jit(solution)/shard_map/ppermute | solution.py:149

commit v2 on v1

v2 whole, which is shorter than its diff:
```python
import functools

import jax
import jax.numpy as jnp
import numpy as np
from jax import lax
from jax.experimental import pallas as pl
from jax.experimental.pallas import tpu as pltpu
from jax.sharding import PartitionSpec as P


HD = 112
LANES = 2 * HD
SIDE = HD * 5 // 14 // 2 * 2
ROWS = 120
EPSILON = 1e-06
BF = jnp.bfloat16
F32 = jnp.float32


def lane_tables():
    first = HD - 2 * SIDE
    freq = np.zeros(LANES, np.float64)
    section = np.zeros(LANES, np.int32)
    pairing = np.zeros((LANES, LANES), np.float32)
    for head in range(2):
        start = head * HD
        for number, size in enumerate((first, SIDE, SIDE)):
            half = size // 2
            for j in range(half):
                low, high = start + j, start + j + half
                freq[low] = freq[high] = 10000.0 ** (-2.0 * j / size)
                section[low] = section[high] = number
                pairing[high, low] = -1.0
                pairing[low, high] = 1.0
            start += size
    same_head = (np.arange(LANES)[:, None] // HD == np.arange(LANES)[None, :] // HD).astype(np.float32)
    return freq.astype(np.float32), section, pairing, same_head


FREQ, _, PAIRING, SAME_HEAD = lane_tables()


def split_hi_lo(value):
    hi = value.astype(BF)
    return hi, (value - hi.astype(F32)).astype(BF)


def dot(a, b):
    return jnp.dot(a, b, preferred_element_type=F32)


def dot_t(a, b):
    return lax.dot_general(a, b, (((0,), (0,)), ((), ())), preferred_element_type=F32)


def side_angles(heights, widths, freq, cos_ref, sin_ref):
    rows, cols = heights.shape[0], widths.shape[0]
    positions = [heights[i] for i in range(rows)] + [widths[i] for i in range(cols)]
    lane = lax.broadcasted_iota(jnp.int32, (rows + cols, LANES), 1)
    lane = jnp.where(lane < HD, lane, lane - HD)
    row = lax.broadcasted_iota(jnp.int32, lane.shape, 0)
    first = HD - 2 * SIDE
    section = (lane >= first).astype(jnp.int32) + (lane >= first + SIDE).astype(jnp.int32)
    mine = section == jnp.where(row < rows, 1, 2)
    for i, position in enumerate(positions):
        cos_ref[i : i + 1] = freq * position.astype(F32)
    angles = cos_ref[...]
    sin_ref[...] = jnp.where(mine, jnp.sin(angles), 0.0)
    cos_ref[...] = jnp.where(mine, jnp.cos(angles), 0.0)


def time_tables(angle):
    lane = lax.broadcasted_iota(jnp.int32, angle.shape, 1)
    mine = jnp.where(lane < HD, lane, lane - HD) < HD - 2 * SIDE
    return jnp.where(mine, jnp.cos(angle), 0.0), jnp.where(mine, jnp.sin(angle), 0.0)


def rotated(positive, angle, side_cos, side_sin, pairing, height):
    _, width, lanes = positive.shape
    flat = positive.reshape(height * width, lanes)
    partner = dot(flat, pairing)
    time_cos, time_sin = time_tables(angle)
    cos = (side_cos[:height] + time_cos)[:, None, :] + side_cos[height:][None, :, :]
    sin = (side_sin[:height] + time_sin)[:, None, :] + side_sin[height:][None, :, :]
    wide = flat.astype(F32)
    return wide, wide * cos.reshape(height * width, lanes) + partner * sin.reshape(height * width, lanes)


def state_kernel(
    blocks, frames, heights, widths, k_ref, v_ref, freq_ref, pair_ref,
    first_ref, second_ref, total_ref, lead_ref, cos_ref, sin_ref,
):
    g = pl.program_id(0)
    height = k_ref.shape[1]

    @pl.when(g == 0)
    def _():
        side_angles(heights, widths, freq_ref[...], cos_ref, sin_ref)

    key = jnp.maximum(k_ref[0], 0)
    angle = freq_ref[...] * frames[g].astype(F32)
    wide, rot = rotated(key, angle, cos_ref[...], sin_ref[...], pair_ref[...], height)
    value = v_ref[0].reshape(wide.shape)
    hi, lo = split_hi_lo(rot)
    outer = dot_t(hi, value) + dot_t(lo, value)
    lane = lax.broadcasted_iota(jnp.int32, (HD, LANES), 1)
    state = jnp.where(lane < HD, outer[:HD], outer[HD:])
    row = lax.broadcasted_iota(jnp.int32, (ROWS - HD, LANES), 0)
    total = jnp.broadcast_to(jnp.sum(wide, axis=0, keepdims=True), row.shape)
    joined = (blocks[0] == blocks[1]).astype(F32)
    marks = [blocks[g], frames[g], None, frames[1 - g]]
    extra = jnp.where(row == 0, total, 0.0)
    for i, mark in enumerate(marks):
        extra = jnp.where(row == i + 1, joined if mark is None else mark.astype(F32), extra)

    @pl.when(g == 0)
    def _():
        first_ref[:HD] = state
        first_ref[HD:] = extra

    @pl.when(g == 1)
    def _():
        second_ref[:HD] = state
        second_ref[HD:] = extra
        total_ref[:HD] = first_ref[:HD] + state
        total_ref[HD:] = first_ref[HD:] + extra
        lead_ref[:HD] = first_ref[:HD] + joined * state
        lead_ref[HD:] = first_ref[HD:] + jnp.where(row == 0, joined * extra, 0.0)


def query_kernel(q_ref, halo_ref, prev_ref, own_ref, freq_ref, cos_ref, sin_ref, pair_ref, qp_ref, hi_ref, lo_ref):
    e = pl.program_id(0)
    query = jnp.maximum(jnp.where(e < 2, halo_ref[0], q_ref[0]), 0)
    height, _, _ = query.shape
    here, other = HD + 2, HD + 4
    rows = [prev_ref[other : other + 1], prev_ref[here : here + 1], own_ref[other : other + 1], own_ref[here : here + 1]]
    position = jnp.where(e < 2, jnp.where(e == 0, rows[0], rows[1]), jnp.where(e == 2, rows[2], rows[3]))
    _, rot = rotated(query, freq_ref[...] * position, cos_ref[...], sin_ref[...], pair_ref[...], height)
    hi, lo = split_hi_lo(rot)
    qp_ref[...] = query.reshape(qp_ref.shape)
    hi_ref[...] = hi.reshape(hi_ref.shape)
    lo_ref[...] = lo.reshape(lo_ref.shape)


def finish_states(first, second, prev, upto, next_lead, far_lead, same_head, sh_ref, sl_ref, kh_ref, kl_ref):
    mark = slice(HD + 1, HD + 2)
    joint = slice(HD + 3, HD + 4)
    tail = jnp.where(next_lead[mark] == second[mark], next_lead, 0.0)
    tail = tail + jnp.where(far_lead[mark] == second[mark], far_lead, 0.0)
    state_1 = upto + first + second + tail
    state_0 = jnp.where(second[joint] > 0.5, state_1, upto + first)
    state_b = jnp.where(prev[mark] == first[mark], state_0, upto)
    state_a = jnp.where(prev[joint] > 0.5, state_b, upto - prev)
    lane = lax.broadcasted_iota(jnp.int32, (HD, LANES), 1)
    square = (LANES, LANES)
    eye = lax.broadcasted_iota(jnp.int32, square, 0) == lax.broadcasted_iota(jnp.int32, square, 1)
    for e, state in enumerate((state_a, state_b, state_0, state_1)):
        packed = state[:HD]
        full = jnp.concatenate([jnp.where(lane < HD, packed, 0.0), jnp.where(lane < HD, 0.0, packed)], axis=0)
        sh_ref[e], sl_ref[e] = split_hi_lo(full)
        d_hi, d_lo = split_hi_lo(jnp.where(eye, state[HD : HD + 1], 0.0))
        kh_ref[e], kl_ref[e] = split_hi_lo(dot(d_hi, same_head) + dot(d_lo, same_head))


def conv_kernel(count, idx, *refs):
    groups = [refs[i * 2 * count : (i + 1) * 2 * count] for i in range(3)]
    records = refs[6 * count : 6 * count + 6]
    same_ref, w_ref, send_ref, keep_ref, lhs_ref, sh_ref, sl_ref, kh_ref, kl_ref = refs[6 * count + 6 :]
    width = groups[0][0].shape[2]
    each = 2 * width
    half = 2 * count * each

    def rows(blocks, e):
        return jnp.concatenate([b[:, e].reshape(each, LANES) for b in blocks], axis=0)

    finish_states(*(r[...] for r in records), same_ref[...], sh_ref, sl_ref, kh_ref, kl_ref)
    for e in range(4):
        query, hi, lo = (rows(blocks, e) for blocks in groups)
        numerator = dot(hi, sh_ref[e]) + dot(lo, sh_ref[e]) + dot(hi, sl_ref[e])
        denominator = dot(query, kh_ref[e]) + dot(query, kl_ref[e]) + EPSILON
        lhs_ref[e * half : (e + 1) * half] = (numerator / denominator).astype(BF)
    c_out = w_ref.shape[-1]
    tile = 768
    for col in range(0, c_out, tile):
        cols = slice(col, min(col + tile, c_out))
        part = dot(lhs_ref[2 * half :], w_ref[0, :, cols])
        part = part + dot(lhs_ref[half : 3 * half], w_ref[1, :, cols])
        part = part + dot(lhs_ref[: 2 * half], w_ref[2, :, cols])
        for t in range(2):
            for s in range(2 * count):
                at = (t * 2 * count + s) * each
                piece = part[at : at + each].reshape(2, width, -1)
                if s % 2 == 0:
                    send_ref[s // 2, :, t, :, cols] = piece.astype(BF)
                else:
                    keep_ref[s // 2, :, t, :, cols] = piece


LIMIT = pltpu.CompilerParams(vmem_limit_bytes=24 << 20)


def off_chip(*values):
    return [pltpu.with_memory_space_constraint(v, pltpu.HBM) for v in values]


def whole(shape):
    return pl.BlockSpec(shape, lambda *_: (0,) * len(shape))


def conv_group(index, queries, records, same_head, weight, count):
    _, frames, width, lanes = queries[0].shape

    def row_block(slot):
        return pl.BlockSpec((2, frames, width, lanes), lambda n, idx: (idx[slot], 0, 0, 0))

    in_vmem = pl.BlockSpec(memory_space=pltpu.VMEM)
    shape = (count, 2, 2, width, weight.shape[-1])
    return pl.pallas_call(
        functools.partial(conv_kernel, count),
        grid_spec=pltpu.PrefetchScalarGridSpec(
            num_scalar_prefetch=1,
            grid=(1,),
            in_specs=[row_block(s) for _ in queries for s in range(2 * count)]
            + [whole((ROWS, lanes))] * 6
            + [whole((lanes, lanes)), in_vmem],
            out_specs=[whole(shape)] * 2,
            scratch_shapes=[pltpu.VMEM((frames * 2 * count * 2 * width, lanes), BF)]
            + [pltpu.VMEM((frames, lanes, lanes), BF)] * 4,
        ),
        out_shape=[pltpu.HBM(shape, BF), pltpu.HBM(shape, F32)],
        compiler_params=LIMIT,
        name="conv",
    )(index, *[q for q in queries for _ in range(2 * count)], *records, same_head, weight)


def shifted(value, by):
    length = lax.axis_size("frame")
    return lax.ppermute(value, "frame", [(i, i + by) for i in range(length) if 0 <= i + by < length])


def swapped(value, mask):
    return lax.ppermute(value, "frame", [(i, i ^ mask) for i in range(lax.axis_size("frame"))])


def moved(value, dy, dc):
    chips = lax.axis_size("head") // 2
    return lax.ppermute(
        value, "head", [(y * 2 + c, (y + dy) % chips * 2 + (c + dc) % 2) for y in range(chips) for c in range(2)]
    )


def block(
    queries, key_vectors, value_vectors, frame_index, height_index, width_index, frame_block, conv_weight, conv_bias
):
    frames, height, width, lanes = queries.shape
    pairing = jnp.asarray(PAIRING, BF)
    same_head = jnp.asarray(SAME_HEAD, BF)
    freq = jnp.asarray(FREQ)[None, :]
    frame_spec = pl.BlockSpec((1, height, width, lanes), lambda g, *_: (g, 0, 0, 0))
    record = (ROWS, lanes)
    table = (height + width, lanes)
    first, second, total, lead, side_cos, side_sin = pl.pallas_call(
        state_kernel,
        grid_spec=pltpu.PrefetchScalarGridSpec(
            num_scalar_prefetch=4,
            grid=(frames,),
            in_specs=[frame_spec, frame_spec, whole((1, lanes)), whole((lanes, lanes))],
            out_specs=[whole(record)] * 4 + [whole(table)] * 2,
        ),
        out_shape=[pltpu.HBM(record, F32)] * 2
        + [jax.ShapeDtypeStruct(record, F32)] * 2
        + [pltpu.HBM(table, F32)] * 2,
        compiler_params=LIMIT,
        name="frame_state",
    )(*off_chip(frame_block, frame_index, height_index, width_index, key_vectors, value_vectors, freq, pairing))

    device = lax.axis_index("frame")
    depth = 8
    upto = jnp.zeros_like(total)
    running = total
    mask = 1
    while mask < depth:
        arrived = swapped(running, mask)
        upto = upto + jnp.where(device & mask != 0, arrived, 0.0)
        running = running + arrived
        mask *= 2
    across = []
    while mask < lax.axis_size("frame"):
        across.append((mask, swapped(running, mask)))
        mask += depth

    halo = shifted(queries, 1)
    prev = shifted(second, 1)
    next_lead = shifted(lead, -1)
    sums = lax.broadcasted_iota(jnp.int32, (ROWS, 1), 0) <= HD
    mark = slice(HD + 1, HD + 2)
    chained = (next_lead[mark] == lead[mark]) & (lead[HD + 3 : HD + 4] > 0.5)
    pair_lead = lead + jnp.where(sums & chained, next_lead, 0.0)
    far_lead = shifted(pair_lead, -2)

    query_block = pl.BlockSpec((height, 1, width, lanes), lambda e: (0, e, 0, 0))
    query_shape = pltpu.HBM((height, 2 * frames, width, lanes), BF)
    query_call = pl.pallas_call(
        query_kernel,
        grid=(2 * frames,),
        in_specs=[
            pl.BlockSpec((1, height, width, lanes), lambda e: (jnp.maximum(e - 2, 0), 0, 0, 0)),
            pl.BlockSpec((1, height, width, lanes), lambda e: (jnp.minimum(e, 1), 0, 0, 0)),
            whole(record), whole(record), whole((1, lanes)), whole(table), whole(table), whole((lanes, lanes)),
        ],
        out_specs=[query_block] * 3,
        out_shape=[query_shape] * 3,
        compiler_params=LIMIT,
        name="queries",
    )
    positive, rot_hi, rot_lo = query_call(
        *off_chip(queries, halo, prev, second, freq, side_cos, side_sin, pairing)
    )

    positive, rot_hi, rot_lo, across = lax.optimization_barrier((positive, rot_hi, rot_lo, across))
    for mask, arrived in across:
        upto = upto + jnp.where(device ^ mask < device, arrived, 0.0)
    records = off_chip(first, second, prev, upto, next_lead, far_lead)

    head = lax.axis_index("head")
    chips = lax.axis_size("head") // 2
    chip, core = head // 2, head % 2
    weight = pltpu.with_memory_space_constraint(conv_weight, pltpu.VMEM)
    (same,) = off_chip(same_head)
    rotated_queries = off_chip(positive, rot_hi, rot_lo)

    def slots(*relatives):
        return jnp.stack([(chip + j) % chips * 2 + c for j in relatives for c in (1 - core, core)]).astype(jnp.int32)

    def conv(index):
        return conv_group(index, rotated_queries, records, same, weight, index.shape[0] // 2)

    send, keep = conv(slots(2))
    far = (keep[0] + moved(send[0], 0, 1).astype(F32)).astype(BF)
    from_far = moved(far, 2, 0)
    far, near_index = lax.optimization_barrier((far, slots(1, 3)))
    send, keep = conv(near_index)
    swap = moved(send, 0, 1)
    near = (keep + swap.astype(F32)).astype(BF)
    from_low = moved(near[0], 1, 0)
    from_high = moved(near[1], 3, 0)
    near, own_index = lax.optimization_barrier((near, slots(0)))
    own_send, own = conv(own_index)
    own = own[0] + moved(own_send[0], 0, 1).astype(F32)
    summed = own + from_far.astype(F32) + from_low.astype(F32) + from_high.astype(F32)
    return jax.nn.silu(summed + conv_bias).astype(BF)


def solution(mesh):
    placed = (
        P("frame", None, None, "head"),
        P("frame", None, None, "head"),
        P("frame", None, None, "head"),
        P("frame"),
        P(),
        P(),
        P("frame"),
        P(None, "head", None),
        P(),
    )
    return jax.shard_map(
        block,
        mesh=mesh,
        in_specs=placed,
        out_specs=P("head", "frame", None, None),
        check_vma=False,
    )
```

time: 129 us -> 107 us (0.83)
  the two profiles are of different devices: /device:TPU:1 before, /device:TPU:38 now
where the time goes in v2:
time: 107 us; the launch traced here: 106 us
  starting transfers between devices  42.3 us (40%)
  waiting for transfers between devices  27.4 us (26%)
  Pallas kernels  25.7 us (24%)
  other arithmetic  10.1 us (9%)
    ppermute x4, starting transfers between devices, shifted(): lax.ppermute(value, 'frame', [(i, i + by) for i in range(length) if 0 <=...  20.9 us
    ppermute x6, waiting for transfers between devices, moved(): lax.ppermute(value, 'head', [(y * 2 + c, (y + dy) % chips * 2 + (c + dc)...  18.8 us
    pallas_call x3, Pallas kernels, conv_group(): pl.pallas_call(functools.partial(conv_kernel, count), grid_spec=pltpu.Pre...  17 us
    ppermute x6, starting transfers between devices, swapped(): lax.ppermute(value, 'frame', [(i, i ^ mask) for i in range(lax.axis_size(...  14.6 us
    ppermute x6, waiting for transfers between devices, swapped(): lax.ppermute(value, 'frame', [(i, i ^ mask) for i in range(lax.axis_size(...  8.61 us
    ppermute x6, starting transfers between devices, moved(): lax.ppermute(value, 'head', [(y * 2 + c, (y + dy) % chips * 2 + (c + dc)...  6.87 us
    pallas_call x1, Pallas kernels, block(): query_call(*off_chip(queries, halo, prev, second, freq, side_cos, side_si...  4.73 us
    pallas_call x1, Pallas kernels, block(): pl.pallas_call(state_kernel, grid_spec=pltpu.PrefetchScalarGridSpec(num_s...  3.94 us
  transfers between devices with their start and end apart: 16, of which 7 were waited for; matrix products, arithmetic and copies ran while one was open for 5% of the time, Pallas kernels for 13%

profile of v2, /device:TPU:38, one launch (start us, length us, event | category | flops | bytes accessed | tf_op | source)
XLA Modules:
  0.0 106.4 jit_solution(6325731134915767653)
XLA Ops:
  0.0 3.8 %collective-permute-start = (bf16[2,16,32,224]{3,2,1,0:T(8,128)(2,1)}, bf16[2,16,32,224]{3,2,1,0:T(8,128)(2,1)}, u32[]{:S(2)}, u32[]{:S(2)}) collective-permute-start(bf16[2,16,32,224]{3,2,1,0:T(8,128)(2,1)} %q_ref.1), channel_id=1, source_target_pairs={{0,8},{8,16},{16,24},{24,32},{32,40},{40,48},{48,56},{56,64},{64,7... | collective-permute-start | bytes 1376264 | tf_op jit(solution)/shard_map/ppermute | solution.py:239
  3.8 3.9 %frame_state.1 = (f32[120,224]{1,0:T(8,128)}, f32[120,224]{1,0:T(8,128)}, f32[120,224]{1,0:T(8,128)S(1)}, f32[120,224]{1,0:T(8,128)S(1)}, f32[48,224]{1,0:T(8,128)}, /*index=5*/f32[48,224]{1,0:T(8,128)}) custom-call(s32[2]{0:T(128)} %blocks.1, s32[2]{0:T(128)} %frames.1, s32[16]{0:T(128)} %heights.1, s32[32]{0:T(128)} %widths.1, ...), custom_call_target="tpu_custom_call" | custom-call | tf_op jit(solution)/shard_map/frame_state/pallas_call | solution.py:263
  7.8 0.1 collective-permute-start.2
  7.9 3.8 %collective-permute-start.8 = (f32[120,224]{1,0:T(8,128)S(1)}, f32[120,224]{1,0:T(8,128)S(1)}, u32[]{:S(2)}, u32[]{:S(2)}) collective-permute-start(f32[120,224]{1,0:T(8,128)S(1)} %get-tuple-element.48), channel_id=1, source_target_pairs={{8,0},{16,8},{24,16},{32,24},{40,32},{48,40},{56,48},{64,56},{72,6... | collective-permute-start | bytes 322568 | tf_op jit(solution)/shard_map/ppermute | solution.py:239
  11.7 4.9 %collective-permute-start.1 = (f32[120,224]{1,0:T(8,128)}, f32[120,224]{1,0:T(8,128)S(1)}, u32[]{:S(2)}, u32[]{:S(2)}) collective-permute-start(f32[120,224]{1,0:T(8,128)} %get-tuple-element.31.own_ref.refs_7_.refs_13_), channel_id=1, source_target_pairs={{0,8},{8,16},{16,24},{24,32},{32,40},{40,48},{48,56},{56,64},{64,7... | collective-permute-start | bytes 322568 | tf_op jit(solution)/shard_map/ppermute | solution.py:239
  16.7 2.1 %collective-permute-done.2 = f32[120,224]{1,0:T(8,128)S(1)} collective-permute-done((f32[120,224]{1,0:T(8,128)S(1)}, f32[120,224]{1,0:T(8,128)S(1)}, u32[]{:S(2)}, u32[]{:S(2)}) %collective-permute-start.2) | collective-permute-done | bytes 107552 | tf_op jit(solution)/shard_map/ppermute | solution.py:243
  18.8 0.0 copy-start.4
  18.8 4.1 %collective-permute-start.3 = (f32[120,224]{1,0:T(8,128)S(1)}, f32[120,224]{1,0:T(8,128)S(1)}, u32[]{:S(2)}, u32[]{:S(2)}) collective-permute-start(f32[120,224]{1,0:T(8,128)S(1)} %add.119), channel_id=1, source_target_pairs={{0,16},{8,24},{16,0},{24,8},{32,48},{40,56},{48,32},{56,40},{64,80... | collective-permute-start | bytes 322568 | tf_op jit(solution)/shard_map/ppermute | solution.py:243
  22.9 0.1 pad_add_fusion.idx
  23.0 2.8 %collective-permute-done.3 = f32[120,224]{1,0:T(8,128)S(1)} collective-permute-done((f32[120,224]{1,0:T(8,128)S(1)}, f32[120,224]{1,0:T(8,128)S(1)}, u32[]{:S(2)}, u32[]{:S(2)}) %collective-permute-start.3) | collective-permute-done | bytes 107552 | tf_op jit(solution)/shard_map/ppermute | solution.py:243
  25.8 0.0 copy-start.5
  25.8 6.2 %collective-permute-start.4 = (f32[120,224]{1,0:T(8,128)S(1)}, f32[120,224]{1,0:T(8,128)S(1)}, u32[]{:S(2)}, u32[]{:S(2)}) collective-permute-start(f32[120,224]{1,0:T(8,128)S(1)} %add.120), channel_id=1, source_target_pairs={{0,32},{8,40},{16,48},{24,56},{32,0},{40,8},{48,16},{56,24},{64,96... | collective-permute-start | bytes 322568 | tf_op jit(solution)/shard_map/ppermute | solution.py:243
  32.0 0.0 collective-permute-done.8.refs_10_.refs_16_
  32.0 0.0 copy-start.1
  32.0 0.0 copy-done.4
  32.0 0.0 copy-done.5
  32.0 3.7 %collective-permute-done.4 = f32[120,224]{1,0:T(8,128)S(1)} collective-permute-done((f32[120,224]{1,0:T(8,128)S(1)}, f32[120,224]{1,0:T(8,128)S(1)}, u32[]{:S(2)}, u32[]{:S(2)}) %collective-permute-start.4) | collective-permute-done | bytes 107552 | tf_op jit(solution)/shard_map/ppermute | solution.py:243
  35.7 0.0 copy-start.6
  35.7 0.0 copy-start
  35.8 0.6 collective-permute-start.7
  36.3 2.4 %collective-permute-start.6 = (f32[120,224]{1,0:T(8,128)S(1)}, f32[120,224]{1,0:T(8,128)}, u32[]{:S(2)}, u32[]{:S(2)}) collective-permute-start(f32[120,224]{1,0:T(8,128)S(1)} %add.121), channel_id=1, source_target_pairs={{0,128},{8,136},{16,144},{24,152},{32,160},{40,168},{48,176},{56,1... | collective-permute-start | bytes 322568 | tf_op jit(solution)/shard_map/ppermute | solution.py:243
  38.8 1.2 %collective-permute-start.5 = (f32[120,224]{1,0:T(8,128)S(1)}, f32[120,224]{1,0:T(8,128)}, u32[]{:S(2)}, u32[]{:S(2)}) collective-permute-start(f32[120,224]{1,0:T(8,128)S(1)} %add.121), channel_id=1, source_target_pairs={{0,64},{8,72},{16,80},{24,88},{32,96},{40,104},{48,112},{56,120},{... | collective-permute-start | bytes 322568 | tf_op jit(solution)/shard_map/ppermute | solution.py:243
  39.9 0.7 select_add_fusion
  40.7 0.0 collective-permute-done.1.prev_ref.refs_8_.refs_14_
  40.7 0.0 copy-done.6
  40.7 0.0 copy-start.2
  40.7 8.3 %collective-permute-start.9 = (f32[120,224]{1,0:T(8,128)}, f32[120,224]{1,0:T(8,128)S(1)}, u32[]{:S(2)}, u32[]{:S(2)}) collective-permute-start(f32[120,224]{1,0:T(8,128)} %select_add_fusion), channel_id=1, source_target_pairs={{16,0},{24,8},{32,16},{40,24},{48,32},{56,40},{64,48},{72,56},{80,... | collective-permute-start | bytes 322568 | tf_op jit(solution)/shard_map/ppermute | solution.py:239
  49.0 0.0 collective-permute-done.halo_ref
  49.0 0.0 copy-done.2
  49.0 4.7 %queries.1 = (bf16[16,4,32,224]{3,2,1,0:T(8,128)(2,1)}, bf16[16,4,32,224]{3,2,1,0:T(8,128)(2,1)}, bf16[16,4,32,224]{3,2,1,0:T(8,128)(2,1)}) custom-call(bf16[2,16,32,224]{3,2,1,0:T(8,128)(2,1)} %q_ref.1, bf16[2,16,32,224]{3,2,1,0:T(8,128)(2,1)} %collective-permute-done.halo_ref, f32[120,224]{1,0:T(8,128)} %copy-done.2, ...), custom_call_target="tpu_custom_call" | custom-call | tf_op jit(solution)/shard_map/queries/pallas_call | solution.py:317
  53.7 0.0 collective-permute-done.7
  53.7 0.0 collective-permute-done.6
  53.8 0.0 collective-permute-done.5
  53.8 1.8 %select_add_fusion.1.refs_9_.refs_15_ = f32[120,224]{1,0:T(8,128)} fusion(f32[120,224]{1,0:T(8,128)} %collective-permute-done.7, f32[120,224]{1,0:T(8,128)} %collective-permute-done.6, f32[120,224]{1,0:T(8,128)} %collective-permute-done.5, f32[120,224]{1,0:T(8,128)} %copy-done.6, f32[120,224]{1,0:T(8,128)} %copy-done.5, f32[120,224]{1,0:T(8,128)} %copy-done.4, ...), kind=kLoop, calls=%fused_computation.12 | loop fusion | flops 295680 | bytes 752646 | tf_op jit(solution)/shard_map/add | solution.py:323
  55.6 0.0 copy-done.1
  55.6 0.0 collective-permute-done.9.refs_11_.refs_17_
  55.6 0.0 copy-start.3
  55.6 0.6 copy-done.3
  56.2 0.0 copy-done
  56.2 5.0 %conv.3 = (bf16[1,2,2,32,2240]{4,3,2,1,0:T(8,128)(2,1)}, f32[1,2,2,32,2240]{4,3,2,1,0:T(8,128)}) custom-call(s32[2]{0:T(128)S(1)} %pad_add_fusion.idx, bf16[16,4,32,224]{3,2,1,0:T(8,128)(2,1)} %get-tuple-element.38.refs_0_.refs_1_.refs_2_.refs_3_, bf16[16,4,32,224]{3,2,1,0:T(8,128)(2,1)} %get-tuple-element.38.refs_0_.refs_1_.refs_2_.refs_3_, ...), custom_call_target="tpu_custom_call" | custom-call | tf_op jit(solution)/shard_map/conv/pallas_call | solution.py:219
  61.2 0.0 collective-permute-start.10
  61.2 0.1 pad_add_fusion.1.idx
  61.3 2.3 %collective-permute-done.10 = bf16[2,2,32,2240]{3,2,1,0:T(8,128)(2,1)} collective-permute-done((bf16[2,2,32,2240]{3,2,1,0:T(8,128)(2,1)}, bf16[2,2,32,2240]{3,2,1,0:T(8,128)(2,1)}, u32[]{:S(2)}, u32[]{:S(2)}) %collective-permute-start.10) | collective-permute-done | bytes 573472 | tf_op jit(solution)/shard_map/ppermute | solution.py:248
  63.6 2.4 %fusion.4 = bf16[2,2,32,2240]{3,2,1,0:T(8,128)(2,1)} fusion(f32[1,2,2,32,2240]{4,3,2,1,0:T(8,128)} %get-tuple-element.49, bf16[2,2,32,2240]{3,2,1,0:T(8,128)(2,1)} %collective-permute-done.10), kind=kLoop, calls=%fused_computation.7 | loop fusion | flops 860160 | bytes 2293760 | tf_op jit(solution)/shard_map/convert_element_type | solution.py:340
  66.0 7.0 %conv.4 = (bf16[2,2,2,32,2240]{4,3,2,1,0:T(8,128)(2,1)}, f32[2,2,2,32,2240]{4,3,2,1,0:T(8,128)}) custom-call(s32[4]{0:T(128)S(1)} %pad_add_fusion.1.idx, bf16[16,4,32,224]{3,2,1,0:T(8,128)(2,1)} %get-tuple-element.38.refs_0_.refs_1_.refs_2_.refs_3_, bf16[16,4,32,224]{3,2,1,0:T(8,128)(2,1)} %get-tuple-element.38.refs_0_.refs_1_.refs_2_.refs_3_, ...), custom_call_target="tpu_custom_call" | custom-call | tf_op jit(solution)/shard_map/conv/pallas_call | solution.py:219
  73.0 0.1 collective-permute-start.11
  73.1 0.1 pad_add_fusion.2.idx
  73.2 3.4 %collective-permute-start.13 = (bf16[2,2,32,2240]{3,2,1,0:T(8,128)(2,1)}, bf16[2,2,32,2240]{3,2,1,0:T(8,128)(2,1)S(1)}, u32[]{:S(2)}, u32[]{:S(2)}) collective-permute-start(bf16[2,2,32,2240]{3,2,1,0:T(8,128)(2,1)} %fusion.4), channel_id=1, source_target_pairs={{0,4},{1,5},{2,6},{3,7},{4,0},{5,1},{6,2},{7,3},{8,12},{9,13},{10,... | collective-permute-start | bytes 1720328 | tf_op jit(solution)/shard_map/ppermute | solution.py:248
  76.6 0.0 collective-permute-done.11
  76.6 2.2 %add_convert_fusion = bf16[2,2,2,32,2240]{4,3,2,1,0:T(8,128)(2,1)S(1)} fusion(f32[2,2,2,32,2240]{4,3,2,1,0:T(8,128)} %get-tuple-element.52, bf16[2,2,2,32,2240]{4,3,2,1,0:T(8,128)(2,1)} %collective-permute-done.11), kind=kLoop, calls=%fused_computation | loop fusion | flops 1720320 | bytes 4587520 | tf_op jit(solution)/shard_map/convert_element_type | solution.py:345
  78.8 0.1 slice_bitcast_fusion.1
  78.9 0.0 copy-start.7
  78.9 5.0 %conv.5 = (bf16[1,2,2,32,2240]{4,3,2,1,0:T(8,128)(2,1)}, f32[1,2,2,32,2240]{4,3,2,1,0:T(8,128)}) custom-call(s32[2]{0:T(128)S(1)} %pad_add_fusion.2.idx, bf16[16,4,32,224]{3,2,1,0:T(8,128)(2,1)} %get-tuple-element.38.refs_0_.refs_1_.refs_2_.refs_3_, bf16[16,4,32,224]{3,2,1,0:T(8,128)(2,1)} %get-tuple-element.38.refs_0_.refs_1_.refs_2_.refs_3_, ...), custom_call_target="tpu_custom_call" | custom-call | tf_op jit(solution)/shard_map/conv/pallas_call | solution.py:219
  83.9 0.1 collective-permute-start.12
  84.0 1.2 %collective-permute-start.14 = (bf16[2,2,32,2240]{3,2,1,0:T(8,128)(2,1)S(1)}, bf16[2,2,32,2240]{3,2,1,0:T(8,128)(2,1)S(1)}, u32[]{:S(2)}, u32[]{:S(2)}) collective-permute-start(bf16[2,2,32,2240]{3,2,1,0:T(8,128)(2,1)S(1)} %get-tuple-element.57), channel_id=1, source_target_pairs={{0,2},{1,3},{2,4},{3,5},{4,6},{5,7},{6,0},{7,1},{8,10},{9,11},{10,... | collective-permute-start | bytes 1720328 | tf_op jit(solution)/shard_map/ppermute | solution.py:248
  85.2 2.0 %collective-permute-start.15 = (bf16[2,2,32,2240]{3,2,1,0:T(8,128)(2,1)S(1)}, bf16[2,2,32,2240]{3,2,1,0:T(8,128)(2,1)S(1)}, u32[]{:S(2)}, u32[]{:S(2)}) collective-permute-start(bf16[2,2,32,2240]{3,2,1,0:T(8,128)(2,1)S(1)} %get-tuple-element.58), channel_id=1, source_target_pairs={{0,6},{1,7},{2,0},{3,1},{4,2},{5,3},{6,4},{7,5},{8,14},{9,15},{10,... | collective-permute-start | bytes 1720328 | tf_op jit(solution)/shard_map/ppermute | solution.py:248
  87.2 4.1 %collective-permute-done.13 = bf16[2,2,32,2240]{3,2,1,0:T(8,128)(2,1)S(1)} collective-permute-done((bf16[2,2,32,2240]{3,2,1,0:T(8,128)(2,1)}, bf16[2,2,32,2240]{3,2,1,0:T(8,128)(2,1)S(1)}, u32[]{:S(2)}, u32[]{:S(2)}) %collective-permute-start.13) | collective-permute-done | bytes 573472 | tf_op jit(solution)/shard_map/ppermute | solution.py:248
  91.3 0.0 collective-permute-done.12
  91.3 12.0 %collective-permute-done.14 = bf16[2,2,32,2240]{3,2,1,0:T(8,128)(2,1)S(1)} collective-permute-done((bf16[2,2,32,2240]{3,2,1,0:T(8,128)(2,1)S(1)}, bf16[2,2,32,2240]{3,2,1,0:T(8,128)(2,1)S(1)}, u32[]{:S(2)}, u32[]{:S(2)}) %collective-permute-start.14) | collective-permute-done | bytes 573472 | tf_op jit(solution)/shard_map/ppermute | solution.py:248
  103.3 0.4 collective-permute-done.15
  103.7 0.0 copy-done.7
  103.7 2.7 %multiply_convert_fusion = bf16[2,2,32,2240]{3,2,1,0:T(8,128)(2,1)} fusion(f32[1,2,2,32,2240]{4,3,2,1,0:T(8,128)} %get-tuple-element.55, bf16[2,2,32,2240]{3,2,1,0:T(8,128)(2,1)S(1)} %collective-permute-done.15, bf16[2,2,32,2240]{3,2,1,0:T(8,128)(2,1)S(1)} %collective-permute-done.14, bf16[2,2,32,2240]{3,2,1,0:T(8,128)(2,1)S(1)} %collective-permute-done.13, ...), kind=kLoop, calls=%fused_computation.8 | loop fusion | flops 4014080 | bytes 4023040 | tf_op jit(solution)/shard_map/convert_element_type | solution.py:352
  (5 shorter events, 0.1 us)
Async XLA Ops:
  0.0 49.0 %collective-permute-start = (bf16[2,16,32,224]{3,2,1,0:T(8,128)(2,1)}, bf16[2,16,32,224]{3,2,1,0:T(8,128)(2,1)}, u32[]{:S(2)}, u32[]{:S(2)}) collective-permute-start(bf16[2,16,32,224]{3,2,1,0:T(8,128)(2,1)} %q_ref.1), channel_id=1, source_target_pairs={{0,8},{8,16},{16,24},{24,32},{32,40},{40,48},{48,56},{56,64},{64,7... | collective-permute-start | bytes 1376264 | tf_op jit(solution)/shard_map/ppermute | solution.py:239
  7.8 11.1 %collective-permute-start.2 = (f32[120,224]{1,0:T(8,128)S(1)}, f32[120,224]{1,0:T(8,128)S(1)}, u32[]{:S(2)}, u32[]{:S(2)}) collective-permute-start(f32[120,224]{1,0:T(8,128)S(1)} %get-tuple-element.37), channel_id=1, source_target_pairs={{0,8},{8,0},{16,24},{24,16},{32,40},{40,32},{48,56},{56,48},{64,72... | collective-permute-start | bytes 322568 | tf_op jit(solution)/shard_map/ppermute | solution.py:243
  7.9 24.1 %collective-permute-start.8 = (f32[120,224]{1,0:T(8,128)S(1)}, f32[120,224]{1,0:T(8,128)S(1)}, u32[]{:S(2)}, u32[]{:S(2)}) collective-permute-start(f32[120,224]{1,0:T(8,128)S(1)} %get-tuple-element.48), channel_id=1, source_target_pairs={{8,0},{16,8},{24,16},{32,24},{40,32},{48,40},{56,48},{64,56},{72,6... | collective-permute-start | bytes 322568 | tf_op jit(solution)/shard_map/ppermute | solution.py:239
  11.7 29.0 %collective-permute-start.1 = (f32[120,224]{1,0:T(8,128)}, f32[120,224]{1,0:T(8,128)S(1)}, u32[]{:S(2)}, u32[]{:S(2)}) collective-permute-start(f32[120,224]{1,0:T(8,128)} %get-tuple-element.31.own_ref.refs_7_.refs_13_), channel_id=1, source_target_pairs={{0,8},{8,16},{16,24},{24,32},{32,40},{40,48},{48,56},{56,64},{64,7... | collective-permute-start | bytes 322568 | tf_op jit(solution)/shard_map/ppermute | solution.py:239
  18.8 13.2 %copy-start.4 = (f32[120,224]{1,0:T(8,128)}, f32[120,224]{1,0:T(8,128)S(1)}, u32[]{:S(2)}) copy-start(f32[120,224]{1,0:T(8,128)S(1)} %collective-permute-done.2) | copy-start | bytes 322564
  18.8 6.9 %collective-permute-start.3 = (f32[120,224]{1,0:T(8,128)S(1)}, f32[120,224]{1,0:T(8,128)S(1)}, u32[]{:S(2)}, u32[]{:S(2)}) collective-permute-start(f32[120,224]{1,0:T(8,128)S(1)} %add.119), channel_id=1, source_target_pairs={{0,16},{8,24},{16,0},{24,8},{32,48},{40,56},{48,32},{56,40},{64,80... | collective-permute-start | bytes 322568 | tf_op jit(solution)/shard_map/ppermute | solution.py:243
  25.8 6.3 %copy-start.5 = (f32[120,224]{1,0:T(8,128)}, f32[120,224]{1,0:T(8,128)S(1)}, u32[]{:S(2)}) copy-start(f32[120,224]{1,0:T(8,128)S(1)} %collective-permute-done.3) | copy-start | bytes 322564
  25.8 10.0 %collective-permute-start.4 = (f32[120,224]{1,0:T(8,128)S(1)}, f32[120,224]{1,0:T(8,128)S(1)}, u32[]{:S(2)}, u32[]{:S(2)}) collective-permute-start(f32[120,224]{1,0:T(8,128)S(1)} %add.120), channel_id=1, source_target_pairs={{0,32},{8,40},{16,48},{24,56},{32,0},{40,8},{48,16},{56,24},{64,96... | collective-permute-start | bytes 322568 | tf_op jit(solution)/shard_map/ppermute | solution.py:243
  32.0 23.6 %copy-start.1 = (f32[120,224]{1,0:T(8,128)}, f32[120,224]{1,0:T(8,128)S(1)}, u32[]{:S(2)}) copy-start(f32[120,224]{1,0:T(8,128)S(1)} %collective-permute-done.8.refs_10_.refs_16_) | copy-start | bytes 322564
  35.7 4.9 %copy-start.6 = (f32[120,224]{1,0:T(8,128)}, f32[120,224]{1,0:T(8,128)S(1)}, u32[]{:S(2)}) copy-start(f32[120,224]{1,0:T(8,128)S(1)} %collective-permute-done.4) | copy-start | bytes 322564
  35.7 20.5 %copy-start = (bf16[3,224,2240]{2,1,0:T(8,128)(2,1)S(1)}, bf16[3,224,2240]{2,1,0:T(8,128)(2,1)}, u32[]{:S(2)}) copy-start(bf16[3,224,2240]{2,1,0:T(8,128)(2,1)} %refs_13_.3) | copy-start | bytes 9031684
  35.8 18.0 %collective-permute-start.7 = (f32[120,224]{1,0:T(8,128)S(1)}, f32[120,224]{1,0:T(8,128)}, u32[]{:S(2)}, u32[]{:S(2)}) collective-permute-start(f32[120,224]{1,0:T(8,128)S(1)} %add.121), channel_id=1, source_target_pairs={{0,192},{8,200},{16,208},{24,216},{32,224},{40,232},{48,240},{56,2... | collective-permute-start | bytes 322568 | tf_op jit(solution)/shard_map/ppermute | solution.py:243
  36.3 17.4 %collective-permute-start.6 = (f32[120,224]{1,0:T(8,128)S(1)}, f32[120,224]{1,0:T(8,128)}, u32[]{:S(2)}, u32[]{:S(2)}) collective-permute-start(f32[120,224]{1,0:T(8,128)S(1)} %add.121), channel_id=1, source_target_pairs={{0,128},{8,136},{16,144},{24,152},{32,160},{40,168},{48,176},{56,1... | collective-permute-start | bytes 322568 | tf_op jit(solution)/shard_map/ppermute | solution.py:243
  38.8 15.0 %collective-permute-start.5 = (f32[120,224]{1,0:T(8,128)S(1)}, f32[120,224]{1,0:T(8,128)}, u32[]{:S(2)}, u32[]{:S(2)}) collective-permute-start(f32[120,224]{1,0:T(8,128)S(1)} %add.121), channel_id=1, source_target_pairs={{0,64},{8,72},{16,80},{24,88},{32,96},{40,104},{48,112},{56,120},{... | collective-permute-start | bytes 322568 | tf_op jit(solution)/shard_map/ppermute | solution.py:243
  40.7 8.3 %copy-start.2 = (f32[120,224]{1,0:T(8,128)}, f32[120,224]{1,0:T(8,128)S(1)}, u32[]{:S(2)}) copy-start(f32[120,224]{1,0:T(8,128)S(1)} %collective-permute-done.1.prev_ref.refs_8_.refs_14_) | copy-start | bytes 322564
  40.7 14.9 %collective-permute-start.9 = (f32[120,224]{1,0:T(8,128)}, f32[120,224]{1,0:T(8,128)S(1)}, u32[]{:S(2)}, u32[]{:S(2)}) collective-permute-start(f32[120,224]{1,0:T(8,128)} %select_add_fusion), channel_id=1, source_target_pairs={{16,0},{24,8},{32,16},{40,24},{48,32},{56,40},{64,48},{72,56},{80,... | collective-permute-start | bytes 322568 | tf_op jit(solution)/shard_map/ppermute | solution.py:239
  55.6 0.6 copy-start.3
  61.2 2.3 %collective-permute-start.10 = (bf16[2,2,32,2240]{3,2,1,0:T(8,128)(2,1)}, bf16[2,2,32,2240]{3,2,1,0:T(8,128)(2,1)}, u32[]{:S(2)}, u32[]{:S(2)}) collective-permute-start(bf16[2,2,32,2240]{3,2,1,0:T(8,128)(2,1)} %bitcast.30), channel_id=1, source_target_pairs={{0,1},{1,0},{2,3},{3,2},{4,5},{5,4},{6,7},{7,6},{8,9},{9,8},{10,11... | collective-permute-start | bytes 1720328 | tf_op jit(solution)/shard_map/ppermute | solution.py:248
  73.0 3.6 %collective-permute-start.11 = (bf16[2,2,2,32,2240]{4,3,2,1,0:T(8,128)(2,1)}, bf16[2,2,2,32,2240]{4,3,2,1,0:T(8,128)(2,1)}, u32[]{:S(2)}, u32[]{:S(2)}) collective-permute-start(bf16[2,2,2,32,2240]{4,3,2,1,0:T(8,128)(2,1)} %get-tuple-element.53), channel_id=1, source_target_pairs={{0,1},{1,0},{2,3},{3,2},{4,5},{5,4},{6,7},{7,6},{8,9},{9,8},{10,11... | collective-permute-start | bytes 3440648 | tf_op jit(solution)/shard_map/ppermute | solution.py:248
  73.2 18.2 %collective-permute-start.13 = (bf16[2,2,32,2240]{3,2,1,0:T(8,128)(2,1)}, bf16[2,2,32,2240]{3,2,1,0:T(8,128)(2,1)S(1)}, u32[]{:S(2)}, u32[]{:S(2)}) collective-permute-start(bf16[2,2,32,2240]{3,2,1,0:T(8,128)(2,1)} %fusion.4), channel_id=1, source_target_pairs={{0,4},{1,5},{2,6},{3,7},{4,0},{5,1},{6,2},{7,3},{8,12},{9,13},{10,... | collective-permute-start | bytes 1720328 | tf_op jit(solution)/shard_map/ppermute | solution.py:248
  78.9 24.9 %copy-start.7 = (f32[2240]{0:T(1024)S(1)}, f32[2240]{0:T(1024)}, u32[]{:S(2)}) copy-start(f32[2240]{0:T(1024)} %param.20) | copy-start | bytes 26884
  83.9 7.4 %collective-permute-start.12 = (bf16[2,2,32,2240]{3,2,1,0:T(8,128)(2,1)}, bf16[2,2,32,2240]{3,2,1,0:T(8,128)(2,1)S(1)}, u32[]{:S(2)}, u32[]{:S(2)}) collective-permute-start(bf16[2,2,32,2240]{3,2,1,0:T(8,128)(2,1)} %bitcast.31), channel_id=1, source_target_pairs={{0,1},{1,0},{2,3},{3,2},{4,5},{5,4},{6,7},{7,6},{8,9},{9,8},{10,11... | collective-permute-start | bytes 1720328 | tf_op jit(solution)/shard_map/ppermute | solution.py:248
  84.0 19.3 %collective-permute-start.14 = (bf16[2,2,32,2240]{3,2,1,0:T(8,128)(2,1)S(1)}, bf16[2,2,32,2240]{3,2,1,0:T(8,128)(2,1)S(1)}, u32[]{:S(2)}, u32[]{:S(2)}) collective-permute-start(bf16[2,2,32,2240]{3,2,1,0:T(8,128)(2,1)S(1)} %get-tuple-element.57), channel_id=1, source_target_pairs={{0,2},{1,3},{2,4},{3,5},{4,6},{5,7},{6,0},{7,1},{8,10},{9,11},{10,... | collective-permute-start | bytes 1720328 | tf_op jit(solution)/shard_map/ppermute | solution.py:248
  85.2 18.5 %collective-permute-start.15 = (bf16[2,2,32,2240]{3,2,1,0:T(8,128)(2,1)S(1)}, bf16[2,2,32,2240]{3,2,1,0:T(8,128)(2,1)S(1)}, u32[]{:S(2)}, u32[]{:S(2)}) collective-permute-start(bf16[2,2,32,2240]{3,2,1,0:T(8,128)(2,1)S(1)} %get-tuple-element.58), channel_id=1, source_target_pairs={{0,6},{1,7},{2,0},{3,1},{4,2},{5,3},{6,4},{7,5},{8,14},{9,15},{10,... | collective-permute-start | bytes 1720328 | tf_op jit(solution)/shard_map/ppermute | solution.py:248

commit v3 on v2

--- a/solution.py
+++ b/solution.py
@@ -163,40 +163,59 @@
         kh_ref[e], kl_ref[e] = split_hi_lo(dot(d_hi, same_head) + dot(d_lo, same_head))
 
 
-def conv_kernel(count, idx, *refs):
-    groups = [refs[i * 2 * count : (i + 1) * 2 * count] for i in range(3)]
-    records = refs[6 * count : 6 * count + 6]
-    same_ref, w_ref, send_ref, keep_ref, lhs_ref, sh_ref, sl_ref, kh_ref, kl_ref = refs[6 * count + 6 :]
-    width = groups[0][0].shape[2]
-    each = 2 * width
-    half = 2 * count * each
-
-    def rows(blocks, e):
-        return jnp.concatenate([b[:, e].reshape(each, LANES) for b in blocks], axis=0)
-
-    finish_states(*(r[...] for r in records), same_ref[...], sh_ref, sl_ref, kh_ref, kl_ref)
-    for e in range(4):
-        query, hi, lo = (rows(blocks, e) for blocks in groups)
+def attend_kernel(
+    flags, qp_ref, hi_ref, lo_ref, first_ref, second_ref, prev_ref, next_ref, far_ref, upto_ref, a_ref, b_ref, c_ref,
+    same_ref, mine_ref, other_ref, rows_ref, sh_ref, sl_ref, kh_ref, kl_ref,
+):
+    height, frames, width, lanes = qp_ref.shape
+    upto = upto_ref[...]
+    for i, arrived in enumerate((a_ref, b_ref, c_ref)):
+        upto = upto + jnp.where(flags[i + 1] != 0, arrived[...], 0.0)
+    records = (first_ref[...], second_ref[...], prev_ref[...], upto, next_ref[...], far_ref[...])
+    finish_states(*records, same_ref[...], sh_ref, sl_ref, kh_ref, kl_ref)
+    mine = flags[0]
+    for e in range(frames):
+        query, hi, lo = (r[:, e].reshape(height * width, lanes) for r in (qp_ref, hi_ref, lo_ref))
         numerator = dot(hi, sh_ref[e]) + dot(lo, sh_ref[e]) + dot(hi, sl_ref[e])
         denominator = dot(query, kh_ref[e]) + dot(query, kl_ref[e]) + EPSILON
-        lhs_ref[e * half : (e + 1) * half] = (numerator / denominator).astype(BF)
-    c_out = w_ref.shape[-1]
-    tile = 768
-    for col in range(0, c_out, tile):
-        cols = slice(col, min(col + tile, c_out))
-        part = dot(lhs_ref[2 * half :], w_ref[0, :, cols])
-        part = part + dot(lhs_ref[half : 3 * half], w_ref[1, :, cols])
-        part = part + dot(lhs_ref[: 2 * half], w_ref[2, :, cols])
-        for t in range(2):
-            for s in range(2 * count):
-                at = (t * 2 * count + s) * each
-                piece = part[at : at + each].reshape(2, width, -1)
-                if s % 2 == 0:
-                    send_ref[s // 2, :, t, :, cols] = piece.astype(BF)
-                else:
-                    keep_ref[s // 2, :, t, :, cols] = piece
-
-
+        rows_ref[...] = (numerator / denominator).astype(BF).reshape(height, width, lanes)
+        for chip in range(height // 4):
+            out = slice(2 * chip, 2 * chip + 2)
+            mine_ref[out, e] = rows_ref[pl.ds(4 * chip + 2 * mine, 2)]
+            other_ref[out, e] = rows_ref[pl.ds(4 * chip + 2 - 2 * mine, 2)]
+
+
+def conv_kernel(count, idx, *refs):
+    parts = (refs[:count], refs[count : 2 * count])
+    weights = refs[2 * count : 2 * count + 2]
+    outs = refs[2 * count + 2 :]
+    width = parts[0][0].shape[2]
+    each = 2 * width
+    lhs = [
+        [
+            jnp.concatenate([b[:, 2 - tap + t].reshape(each, LANES) for b in blocks for t in range(2)], axis=0)
+            for tap in range(3)
+        ]
+        for blocks in parts
+    ]
+
+    def columns(col, size):
+        total = None
+        for blocks, w_ref in zip(lhs, weights):
+            for tap in range(3):
+                part = dot(blocks[tap], w_ref[tap, :, col : col + size])
+                total = part if total is None else total + part
+        for j in range(count):
+            for t in range(2):
+                at = (2 * j + t) * each
+                outs[j][:, t, :, :size] = total[at : at + each].reshape(2, width, size).astype(outs[j].dtype)
+
+    c_out = weights[0].shape[-1]
+    for number, col in enumerate(range(0, c_out, TILE)):
+        pl.when(pl.program_id(0) == number)(functools.partial(columns, col, min(TILE, c_out - col)))
+
+
+TILE = 768
 LIMIT = pltpu.CompilerParams(vmem_limit_bytes=24 << 20)
 
 
@@ -208,30 +227,46 @@
     return pl.BlockSpec(shape, lambda *_: (0,) * len(shape))
 
 
-def conv_group(index, queries, records, same_head, weight, count):
-    _, frames, width, lanes = queries[0].shape
+def attend(flags, queries, records, same_head):
+    height, frames, width, lanes = queries[0].shape
+    half = (height // 2, frames, width, lanes)
+    square = pltpu.VMEM((frames, lanes, lanes), BF)
+    in_vmem = pl.BlockSpec(memory_space=pltpu.VMEM)
+    return pl.pallas_call(
+        attend_kernel,
+        grid_spec=pltpu.PrefetchScalarGridSpec(
+            num_scalar_prefetch=1,
+            grid=(1,),
+            in_specs=[in_vmem] * 3 + [whole((ROWS, lanes))] * 9 + [whole((lanes, lanes))],
+            out_specs=[in_vmem] * 2,
+            scratch_shapes=[pltpu.VMEM((height, width, lanes), BF)] + [square] * 4,
+        ),
+        out_shape=[pltpu.VMEM(half, BF)] * 2,
+        compiler_params=LIMIT,
+        name="attend",
+    )(flags, *queries, *records, same_head)
+
+
+def conv_group(index, slots, attended, weights, dtype):
+    _, frames, width, lanes = attended[0].shape
+    count = len(slots)
+    c_out = weights[0].shape[-1]
 
     def row_block(slot):
         return pl.BlockSpec((2, frames, width, lanes), lambda n, idx: (idx[slot], 0, 0, 0))
 
-    in_vmem = pl.BlockSpec(memory_space=pltpu.VMEM)
-    shape = (count, 2, 2, width, weight.shape[-1])
     return pl.pallas_call(
         functools.partial(conv_kernel, count),
         grid_spec=pltpu.PrefetchScalarGridSpec(
             num_scalar_prefetch=1,
-            grid=(1,),
-            in_specs=[row_block(s) for _ in queries for s in range(2 * count)]
-            + [whole((ROWS, lanes))] * 6
-            + [whole((lanes, lanes)), in_vmem],
-            out_specs=[whole(shape)] * 2,
-            scratch_shapes=[pltpu.VMEM((frames * 2 * count * 2 * width, lanes), BF)]
-            + [pltpu.VMEM((frames, lanes, lanes), BF)] * 4,
+            grid=(pl.cdiv(c_out, TILE),),
+            in_specs=[row_block(s) for _ in attended for s in slots] + [pl.BlockSpec(memory_space=pltpu.VMEM)] * 2,
+            out_specs=[pl.BlockSpec((2, 2, width, TILE), lambda n, idx: (0, 0, 0, n))] * count,
         ),
-        out_shape=[pltpu.HBM(shape, BF), pltpu.HBM(shape, F32)],
+        out_shape=[pltpu.HBM((2, 2, width, c_out), dtype)] * count,
         compiler_params=LIMIT,
         name="conv",
-    )(index, *[q for q in queries for _ in range(2 * count)], *records, same_head, weight)
+    )(index, *[a for a in attended for _ in slots], *weights)
 
 
 def shifted(value, by):
@@ -260,7 +295,7 @@
     frame_spec = pl.BlockSpec((1, height, width, lanes), lambda g, *_: (g, 0, 0, 0))
     record = (ROWS, lanes)
     table = (height + width, lanes)
-    first, second, total, lead, side_cos, side_sin = pl.pallas_call(
+    state_call = pl.pallas_call(
         state_kernel,
         grid_spec=pltpu.PrefetchScalarGridSpec(
             num_scalar_prefetch=4,
@@ -273,7 +308,8 @@
         + [pltpu.HBM(table, F32)] * 2,
         compiler_params=LIMIT,
         name="frame_state",
-    )(*off_chip(frame_block, frame_index, height_index, width_index, key_vectors, value_vectors, freq, pairing))
+    )
+    first, second, total, lead, side_cos, side_sin = state_call(*off_chip(frame_block, frame_index, height_index, width_index, key_vectors, value_vectors, freq, pairing))
 
     device = lax.axis_index("frame")
     depth = 8
@@ -281,15 +317,16 @@
     running = total
     mask = 1
     while mask < depth:
-        arrived = swapped(running, mask)
+        arrived = swapped(running, depth - 1 if 2 * mask == depth else mask)
         upto = upto + jnp.where(device & mask != 0, arrived, 0.0)
         running = running + arrived
         mask *= 2
     across = []
     while mask < lax.axis_size("frame"):
-        across.append((mask, swapped(running, mask)))
+        across.append(swapped(running, mask))
         mask += depth
 
+    their_weight = moved(conv_weight, 0, 1)
     halo = shifted(queries, 1)
     prev = shifted(second, 1)
     next_lead = shifted(lead, -1)
@@ -300,7 +337,7 @@
     far_lead = shifted(pair_lead, -2)
 
     query_block = pl.BlockSpec((height, 1, width, lanes), lambda e: (0, e, 0, 0))
-    query_shape = pltpu.HBM((height, 2 * frames, width, lanes), BF)
+    query_shape = pltpu.VMEM((height, 2 * frames, width, lanes), BF)
     query_call = pl.pallas_call(
         query_kernel,
         grid=(2 * frames,),
@@ -319,36 +356,26 @@
     )
 
     positive, rot_hi, rot_lo, across = lax.optimization_barrier((positive, rot_hi, rot_lo, across))
-    for mask, arrived in across:
-        upto = upto + jnp.where(device ^ mask < device, arrived, 0.0)
-    records = off_chip(first, second, prev, upto, next_lead, far_lead)
+    records = (*off_chip(first, second, prev), next_lead, far_lead, upto, *across)
 
     head = lax.axis_index("head")
     chips = lax.axis_size("head") // 2
     chip, core = head // 2, head % 2
-    weight = pltpu.with_memory_space_constraint(conv_weight, pltpu.VMEM)
     (same,) = off_chip(same_head)
-    rotated_queries = off_chip(positive, rot_hi, rot_lo)
-
-    def slots(*relatives):
-        return jnp.stack([(chip + j) % chips * 2 + c for j in relatives for c in (1 - core, core)]).astype(jnp.int32)
-
-    def conv(index):
-        return conv_group(index, rotated_queries, records, same, weight, index.shape[0] // 2)
-
-    send, keep = conv(slots(2))
-    far = (keep[0] + moved(send[0], 0, 1).astype(F32)).astype(BF)
+    owners = [(chip + j) % chips for j in (2, 1, 3, 0)]
+    flags = jnp.stack([core] + [(device ^ m < device).astype(jnp.int32) for m in (8, 16, 24)] + owners).astype(jnp.int32)
+    mine, other = attend(flags, (positive, rot_hi, rot_lo), records, same)
+    theirs = moved(other, 0, 1)
+    attended = (mine, theirs)
+    weights = [pltpu.with_memory_space_constraint(w, pltpu.VMEM) for w in (conv_weight, their_weight)]
+    (far,) = conv_group(flags, (4,), attended, weights, BF)
     from_far = moved(far, 2, 0)
-    far, near_index = lax.optimization_barrier((far, slots(1, 3)))
-    send, keep = conv(near_index)
-    swap = moved(send, 0, 1)
-    near = (keep + swap.astype(F32)).astype(BF)
+    near = conv_group(flags, (5, 6), attended, weights, BF)
     from_low = moved(near[0], 1, 0)
     from_high = moved(near[1], 3, 0)
-    near, own_index = lax.optimization_barrier((near, slots(0)))
-    own_send, own = conv(own_index)
-    own = own[0] + moved(own_send[0], 0, 1).astype(F32)
-    summed = own + from_far.astype(F32) + from_low.astype(F32) + from_high.astype(F32)
+    (own,) = conv_group(flags, (7,), attended, weights, F32)
+    own = own + from_far.astype(F32)
+    summed = lax.optimization_barrier(own) + from_low.astype(F32) + from_high.astype(F32)
     return jax.nn.silu(summed + conv_bias).astype(BF)
 
 

time: 107 us -> 96.6 us (0.903)
  the two profiles are of different devices: /device:TPU:38 before, /device:TPU:1 now
where the time goes in v3:
time: 96.6 us; the launch traced here: 96.2 us
  starting transfers between devices  36.3 us (38%)
  waiting for transfers between devices  33.5 us (35%)
  Pallas kernels  21.1 us (22%)
  other arithmetic  5.03 us (5%)
    ppermute x5, waiting for transfers between devices, moved(): lax.ppermute(value, 'head', [(y * 2 + c, (y + dy) % chips * 2 + (c + dc)...  17.1 us
    ppermute x6, waiting for transfers between devices, swapped(): lax.ppermute(value, 'frame', [(i, i ^ mask) for i in range(lax.axis_size(...  15.6 us
    ppermute x6, starting transfers between devices, swapped(): lax.ppermute(value, 'frame', [(i, i ^ mask) for i in range(lax.axis_size(...  14.6 us
    ppermute x5, starting transfers between devices, moved(): lax.ppermute(value, 'head', [(y * 2 + c, (y + dy) % chips * 2 + (c + dc)...  11.3 us
    ppermute x4, starting transfers between devices, shifted(): lax.ppermute(value, 'frame', [(i, i + by) for i in range(length) if 0 <=...  10.4 us
    pallas_call x3, Pallas kernels, conv_group(): pl.pallas_call(functools.partial(conv_kernel, count), grid_spec=pltpu.Pre...  9.92 us
    pallas_call x1, Pallas kernels, attend(): pl.pallas_call(attend_kernel, grid_spec=pltpu.PrefetchScalarGridSpec(num_...  4 us
    pallas_call x1, Pallas kernels, block(): state_call(*off_chip(frame_block, frame_index, height_index, width_index,...  3.9 us
  transfers between devices with their start and end apart: 15, of which 7 were waited for; matrix products, arithmetic and copies ran while one was open for 4% of the time, Pallas kernels for 19%

profile of v3, /device:TPU:1, one launch (start us, length us, event | category | flops | bytes accessed | tf_op | source)
XLA Modules:
  0.0 96.2 jit_solution(4713356410567301847)
XLA Ops:
  0.0 3.2 %collective-permute-start.11 = (bf16[3,224,2240]{2,1,0:T(8,128)(2,1)}, bf16[3,224,2240]{2,1,0:T(8,128)(2,1)S(1)}, u32[]{:S(2)}, u32[]{:S(2)}) collective-permute-start(bf16[3,224,2240]{2,1,0:T(8,128)(2,1)} %refs_4_.1), channel_id=1, source_target_pairs={{0,1},{1,0},{2,3},{3,2},{4,5},{5,4},{6,7},{7,6},{8,9},{9,8},{10,11... | collective-permute-start | bytes 9031688 | tf_op jit(solution)/shard_map/ppermute | solution.py:283
  3.2 3.9 %frame_state.1 = (f32[120,224]{1,0:T(8,128)}, f32[120,224]{1,0:T(8,128)}, f32[120,224]{1,0:T(8,128)S(1)}, f32[120,224]{1,0:T(8,128)S(1)}, f32[48,224]{1,0:T(8,128)}, /*index=5*/f32[48,224]{1,0:T(8,128)}) custom-call(s32[2]{0:T(128)} %blocks.1, s32[2]{0:T(128)} %frames.1, s32[16]{0:T(128)} %heights.1, s32[32]{0:T(128)} %widths.1, ...), custom_call_target="tpu_custom_call" | custom-call | tf_op jit(solution)/shard_map/frame_state/pallas_call | solution.py:312
  7.1 0.0 collective-permute-start.2
  7.1 4.0 %collective-permute-start.1 = (f32[120,224]{1,0:T(8,128)}, f32[120,224]{1,0:T(8,128)}, u32[]{:S(2)}, u32[]{:S(2)}) collective-permute-start(f32[120,224]{1,0:T(8,128)} %get-tuple-element.24.own_ref.second_ref), channel_id=1, source_target_pairs={{0,8},{8,16},{16,24},{24,32},{32,40},{40,48},{48,56},{56,64},{64,7... | collective-permute-start | bytes 322568 | tf_op jit(solution)/shard_map/ppermute | solution.py:274
  11.1 3.8 %collective-permute-start = (bf16[2,16,32,224]{3,2,1,0:T(8,128)(2,1)}, bf16[2,16,32,224]{3,2,1,0:T(8,128)(2,1)}, u32[]{:S(2)}, u32[]{:S(2)}) collective-permute-start(bf16[2,16,32,224]{3,2,1,0:T(8,128)(2,1)} %q_ref.1), channel_id=1, source_target_pairs={{0,8},{8,16},{16,24},{24,32},{32,40},{40,48},{48,56},{56,64},{64,7... | collective-permute-start | bytes 1376264 | tf_op jit(solution)/shard_map/ppermute | solution.py:274
  14.9 1.3 %collective-permute-start.8 = (f32[120,224]{1,0:T(8,128)S(1)}, f32[120,224]{1,0:T(8,128)S(1)}, u32[]{:S(2)}, u32[]{:S(2)}) collective-permute-start(f32[120,224]{1,0:T(8,128)S(1)} %get-tuple-element.35), channel_id=1, source_target_pairs={{8,0},{16,8},{24,16},{32,24},{40,32},{48,40},{56,48},{64,56},{72,6... | collective-permute-start | bytes 322568 | tf_op jit(solution)/shard_map/ppermute | solution.py:274
  16.2 0.0 collective-permute-done.2
  16.2 0.9 add.73
  17.2 3.2 %collective-permute-start.3 = (f32[120,224]{1,0:T(8,128)S(1)}, f32[120,224]{1,0:T(8,128)S(1)}, u32[]{:S(2)}, u32[]{:S(2)}) collective-permute-start(f32[120,224]{1,0:T(8,128)S(1)} %add.73), channel_id=1, source_target_pairs={{0,16},{8,24},{16,0},{24,8},{32,48},{40,56},{48,32},{56,40},{64,80... | collective-permute-start | bytes 322568 | tf_op jit(solution)/shard_map/ppermute | solution.py:278
  20.4 7.3 %collective-permute-done.3 = f32[120,224]{1,0:T(8,128)S(1)} collective-permute-done((f32[120,224]{1,0:T(8,128)S(1)}, f32[120,224]{1,0:T(8,128)S(1)}, u32[]{:S(2)}, u32[]{:S(2)}) %collective-permute-start.3) | collective-permute-done | bytes 107552 | tf_op jit(solution)/shard_map/ppermute | solution.py:278
  27.7 7.5 %collective-permute-start.4 = (f32[120,224]{1,0:T(8,128)S(1)}, f32[120,224]{1,0:T(8,128)S(1)}, u32[]{:S(2)}, u32[]{:S(2)}) collective-permute-start(f32[120,224]{1,0:T(8,128)S(1)} %add.74), channel_id=1, source_target_pairs={{0,56},{8,48},{16,40},{24,32},{32,24},{40,16},{48,8},{56,0},{64,12... | collective-permute-start | bytes 322568 | tf_op jit(solution)/shard_map/ppermute | solution.py:278
  35.2 0.0 collective-permute-done.8.next_ref
  35.2 5.8 %collective-permute-done.4 = f32[120,224]{1,0:T(8,128)S(1)} collective-permute-done((f32[120,224]{1,0:T(8,128)S(1)}, f32[120,224]{1,0:T(8,128)S(1)}, u32[]{:S(2)}, u32[]{:S(2)}) %collective-permute-start.4) | collective-permute-done | bytes 107552 | tf_op jit(solution)/shard_map/ppermute | solution.py:278
  41.0 0.7 select_add_fusion
  41.7 1.2 %collective-permute-start.5 = (f32[120,224]{1,0:T(8,128)}, f32[120,224]{1,0:T(8,128)}, u32[]{:S(2)}, u32[]{:S(2)}) collective-permute-start(f32[120,224]{1,0:T(8,128)} %get-tuple-element.44), channel_id=1, source_target_pairs={{0,64},{8,72},{16,80},{24,88},{32,96},{40,104},{48,112},{56,120},{... | collective-permute-start | bytes 322568 | tf_op jit(solution)/shard_map/ppermute | solution.py:278
  42.9 2.4 %collective-permute-start.6 = (f32[120,224]{1,0:T(8,128)}, f32[120,224]{1,0:T(8,128)}, u32[]{:S(2)}, u32[]{:S(2)}) collective-permute-start(f32[120,224]{1,0:T(8,128)} %get-tuple-element.44), channel_id=1, source_target_pairs={{0,128},{8,136},{16,144},{24,152},{32,160},{40,168},{48,176},{56,1... | collective-permute-start | bytes 322568 | tf_op jit(solution)/shard_map/ppermute | solution.py:278
  45.3 0.0 collective-permute-done.1.prev_ref
  45.3 0.2 collective-permute-start.7
  45.5 0.7 select_add_fusion.1
  46.3 0.0 collective-permute-done.halo_ref
  46.3 1.3 %collective-permute-start.9 = (f32[120,224]{1,0:T(8,128)}, f32[120,224]{1,0:T(8,128)S(1)}, u32[]{:S(2)}, u32[]{:S(2)}) collective-permute-start(f32[120,224]{1,0:T(8,128)} %select_add_fusion.1), channel_id=1, source_target_pairs={{16,0},{24,8},{32,16},{40,24},{48,32},{56,40},{64,48},{72,56},{80,... | collective-permute-start | bytes 322568 | tf_op jit(solution)/shard_map/ppermute | solution.py:274
  47.7 0.1 stack.47.flags.idx
  47.7 3.3 %queries.1 = (bf16[16,4,32,224]{3,2,1,0:T(8,128)(2,1)S(1)}, bf16[16,4,32,224]{3,2,1,0:T(8,128)(2,1)S(1)}, bf16[16,4,32,224]{3,2,1,0:T(8,128)(2,1)S(1)}) custom-call(bf16[2,16,32,224]{3,2,1,0:T(8,128)(2,1)} %q_ref.1, bf16[2,16,32,224]{3,2,1,0:T(8,128)(2,1)} %collective-permute-done.halo_ref, f32[120,224]{1,0:T(8,128)} %collective-permute-done.1.prev_ref, ...), custom_call_target="tpu_custom_call" | custom-call | tf_op jit(solution)/shard_map/queries/pallas_call | solution.py:354
  51.1 0.0 collective-permute-done.5.a_ref
  51.1 0.0 collective-permute-done.6.b_ref
  51.1 2.6 %collective-permute-done.7.c_ref = f32[120,224]{1,0:T(8,128)} collective-permute-done((f32[120,224]{1,0:T(8,128)}, f32[120,224]{1,0:T(8,128)}, u32[]{:S(2)}, u32[]{:S(2)}) %collective-permute-start.7) | collective-permute-done | bytes 107552 | tf_op jit(solution)/shard_map/ppermute | solution.py:278
  53.7 0.7 collective-permute-done.9.far_ref
  54.4 0.0 copy-start
  54.4 4.0 %attend.1 = (bf16[8,4,32,224]{3,2,1,0:T(8,128)(2,1)S(1)}, bf16[8,4,32,224]{3,2,1,0:T(8,128)(2,1)S(1)}) custom-call(s32[8]{0:T(128)S(1)} %stack.47.flags.idx, bf16[16,4,32,224]{3,2,1,0:T(8,128)(2,1)S(1)} %get-tuple-element.31.qp_ref, bf16[16,4,32,224]{3,2,1,0:T(8,128)(2,1)S(1)} %get-tuple-element.32.hi_ref, ...), custom_call_target="tpu_custom_call" | custom-call | tf_op jit(solution)/shard_map/attend/pallas_call | solution.py:235
  58.4 2.5 %collective-permute-start.10 = (bf16[8,4,32,224]{3,2,1,0:T(8,128)(2,1)S(1)}, bf16[8,4,32,224]{3,2,1,0:T(8,128)(2,1)S(1)}, u32[]{:S(2)}, u32[]{:S(2)}) collective-permute-start(bf16[8,4,32,224]{3,2,1,0:T(8,128)(2,1)S(1)} %get-tuple-element.40), channel_id=1, source_target_pairs={{0,1},{1,0},{2,3},{3,2},{4,5},{5,4},{6,7},{7,6},{8,9},{9,8},{10,11... | collective-permute-start | bytes 1376264 | tf_op jit(solution)/shard_map/ppermute | solution.py:283
  60.9 1.5 %collective-permute-done.10.refs_1_.refs_2_.refs_3_ = bf16[8,4,32,224]{3,2,1,0:T(8,128)(2,1)S(1)} collective-permute-done((bf16[8,4,32,224]{3,2,1,0:T(8,128)(2,1)S(1)}, bf16[8,4,32,224]{3,2,1,0:T(8,128)(2,1)S(1)}, u32[]{:S(2)}, u32[]{:S(2)}) %collective-permute-start.10) | collective-permute-done | bytes 458784 | tf_op jit(solution)/shard_map/ppermute | solution.py:283
  62.5 0.0 collective-permute-done.11.refs_3_.refs_5_
  62.5 0.0 copy-done
  62.5 2.9 %conv.4 = bf16[2,2,32,2240]{3,2,1,0:T(8,128)(2,1)} custom-call(s32[8]{0:T(128)S(1)} %stack.47.flags.idx, bf16[8,4,32,224]{3,2,1,0:T(8,128)(2,1)S(1)} %get-tuple-element.39.refs_0_.refs_1_, bf16[8,4,32,224]{3,2,1,0:T(8,128)(2,1)S(1)} %collective-permute-done.10.refs_1_.refs_2_.refs_3_, bf16[3,224,2240]{2,1,0:T(8,128)(2,1)S(1)} %copy-done, ...), custom_call_target="tpu_custom_call" | custom-call | tf_op jit(solution)/shard_map/conv/pallas_call | solution.py:258
  65.4 2.9 %collective-permute-start.12 = (bf16[2,2,32,2240]{3,2,1,0:T(8,128)(2,1)}, bf16[2,2,32,2240]{3,2,1,0:T(8,128)(2,1)S(1)}, u32[]{:S(2)}, u32[]{:S(2)}) collective-permute-start(bf16[2,2,32,2240]{3,2,1,0:T(8,128)(2,1)} %conv.4), channel_id=1, source_target_pairs={{0,4},{1,5},{2,6},{3,7},{4,0},{5,1},{6,2},{7,3},{8,12},{9,13},{10,... | collective-permute-start | bytes 1720328 | tf_op jit(solution)/shard_map/ppermute | solution.py:283
  68.3 3.8 %conv.5 = (bf16[2,2,32,2240]{3,2,1,0:T(8,128)(2,1)}, bf16[2,2,32,2240]{3,2,1,0:T(8,128)(2,1)}) custom-call(s32[8]{0:T(128)S(1)} %stack.47.flags.idx, bf16[8,4,32,224]{3,2,1,0:T(8,128)(2,1)S(1)} %get-tuple-element.39.refs_0_.refs_1_, bf16[8,4,32,224]{3,2,1,0:T(8,128)(2,1)S(1)} %get-tuple-element.39.refs_0_.refs_1_, ...), custom_call_target="tpu_custom_call" | custom-call | tf_op jit(solution)/shard_map/conv/pallas_call | solution.py:258
  72.1 0.4 collective-permute-start.13
  72.5 2.3 %collective-permute-start.14 = (bf16[2,2,32,2240]{3,2,1,0:T(8,128)(2,1)}, bf16[2,2,32,2240]{3,2,1,0:T(8,128)(2,1)S(1)}, u32[]{:S(2)}, u32[]{:S(2)}) collective-permute-start(bf16[2,2,32,2240]{3,2,1,0:T(8,128)(2,1)} %get-tuple-element.42), channel_id=1, source_target_pairs={{0,6},{1,7},{2,0},{3,1},{4,2},{5,3},{6,4},{7,5},{8,14},{9,15},{10,... | collective-permute-start | bytes 1720328 | tf_op jit(solution)/shard_map/ppermute | solution.py:283
  74.8 3.2 %conv.3 = f32[2,2,32,2240]{3,2,1,0:T(8,128)} custom-call(s32[8]{0:T(128)S(1)} %stack.47.flags.idx, bf16[8,4,32,224]{3,2,1,0:T(8,128)(2,1)S(1)} %get-tuple-element.39.refs_0_.refs_1_, bf16[8,4,32,224]{3,2,1,0:T(8,128)(2,1)S(1)} %collective-permute-done.10.refs_1_.refs_2_.refs_3_, bf16[3,224,2240]{2,1,0:T(8,128)(2,1)S(1)} %copy-done, ...), custom_call_target="tpu_custom_call" | custom-call | tf_op jit(solution)/shard_map/conv/pallas_call | solution.py:258
  78.0 0.0 copy-start.1
  78.0 3.7 %collective-permute-done.12 = bf16[2,2,32,2240]{3,2,1,0:T(8,128)(2,1)S(1)} collective-permute-done((bf16[2,2,32,2240]{3,2,1,0:T(8,128)(2,1)}, bf16[2,2,32,2240]{3,2,1,0:T(8,128)(2,1)S(1)}, u32[]{:S(2)}, u32[]{:S(2)}) %collective-permute-start.12) | collective-permute-done | bytes 573472 | tf_op jit(solution)/shard_map/ppermute | solution.py:283
  81.7 1.4 %convert_add_fusion = f32[2,2,32,2240]{3,2,1,0:T(8,128)S(1)} fusion(f32[2,2,32,2240]{3,2,1,0:T(8,128)} %conv.3, bf16[2,2,32,2240]{3,2,1,0:T(8,128)(2,1)S(1)} %collective-permute-done.12), kind=kLoop, calls=%fused_computation.1 | loop fusion | flops 573440 | bytes 2867200 | tf_op jit(solution)/shard_map/add | solution.py:377
  83.1 11.9 %collective-permute-done.13 = bf16[2,2,32,2240]{3,2,1,0:T(8,128)(2,1)S(1)} collective-permute-done((bf16[2,2,32,2240]{3,2,1,0:T(8,128)(2,1)}, bf16[2,2,32,2240]{3,2,1,0:T(8,128)(2,1)S(1)}, u32[]{:S(2)}, u32[]{:S(2)}) %collective-permute-start.13) | collective-permute-done | bytes 573472 | tf_op jit(solution)/shard_map/ppermute | solution.py:283
  95.0 0.0 collective-permute-done.14
  95.0 0.0 copy-done.1
  95.0 1.2 %multiply_convert_fusion = bf16[2,2,32,2240]{3,2,1,0:T(8,128)(2,1)} fusion(bf16[2,2,32,2240]{3,2,1,0:T(8,128)(2,1)S(1)} %collective-permute-done.14, f32[2,2,32,2240]{3,2,1,0:T(8,128)S(1)} %convert_add_fusion, bf16[2,2,32,2240]{3,2,1,0:T(8,128)(2,1)S(1)} %collective-permute-done.13, f32[2240]{0:T(1024)S(1)} %copy-done.1), kind=kLoop, calls=%fused_computation | loop fusion | flops 2867200 | bytes 2876160 | tf_op jit(solution)/shard_map/convert_element_type | solution.py:379
  (3 shorter events, 0.0 us)
Async XLA Ops:
  0.0 62.5 %collective-permute-start.11 = (bf16[3,224,2240]{2,1,0:T(8,128)(2,1)}, bf16[3,224,2240]{2,1,0:T(8,128)(2,1)S(1)}, u32[]{:S(2)}, u32[]{:S(2)}) collective-permute-start(bf16[3,224,2240]{2,1,0:T(8,128)(2,1)} %refs_4_.1), channel_id=1, source_target_pairs={{0,1},{1,0},{2,3},{3,2},{4,5},{5,4},{6,7},{7,6},{8,9},{9,8},{10,11... | collective-permute-start | bytes 9031688 | tf_op jit(solution)/shard_map/ppermute | solution.py:283
  7.1 9.1 %collective-permute-start.2 = (f32[120,224]{1,0:T(8,128)S(1)}, f32[120,224]{1,0:T(8,128)}, u32[]{:S(2)}, u32[]{:S(2)}) collective-permute-start(f32[120,224]{1,0:T(8,128)S(1)} %get-tuple-element.30), channel_id=1, source_target_pairs={{0,8},{8,0},{16,24},{24,16},{32,40},{40,32},{48,56},{56,48},{64,72... | collective-permute-start | bytes 322568 | tf_op jit(solution)/shard_map/ppermute | solution.py:278
  7.1 38.2 %collective-permute-start.1 = (f32[120,224]{1,0:T(8,128)}, f32[120,224]{1,0:T(8,128)}, u32[]{:S(2)}, u32[]{:S(2)}) collective-permute-start(f32[120,224]{1,0:T(8,128)} %get-tuple-element.24.own_ref.second_ref), channel_id=1, source_target_pairs={{0,8},{8,16},{16,24},{24,32},{32,40},{40,48},{48,56},{56,64},{64,7... | collective-permute-start | bytes 322568 | tf_op jit(solution)/shard_map/ppermute | solution.py:274
  11.1 35.2 %collective-permute-start = (bf16[2,16,32,224]{3,2,1,0:T(8,128)(2,1)}, bf16[2,16,32,224]{3,2,1,0:T(8,128)(2,1)}, u32[]{:S(2)}, u32[]{:S(2)}) collective-permute-start(bf16[2,16,32,224]{3,2,1,0:T(8,128)(2,1)} %q_ref.1), channel_id=1, source_target_pairs={{0,8},{8,16},{16,24},{24,32},{32,40},{40,48},{48,56},{56,64},{64,7... | collective-permute-start | bytes 1376264 | tf_op jit(solution)/shard_map/ppermute | solution.py:274
  14.9 20.3 %collective-permute-start.8 = (f32[120,224]{1,0:T(8,128)S(1)}, f32[120,224]{1,0:T(8,128)S(1)}, u32[]{:S(2)}, u32[]{:S(2)}) collective-permute-start(f32[120,224]{1,0:T(8,128)S(1)} %get-tuple-element.35), channel_id=1, source_target_pairs={{8,0},{16,8},{24,16},{32,24},{40,32},{48,40},{56,48},{64,56},{72,6... | collective-permute-start | bytes 322568 | tf_op jit(solution)/shard_map/ppermute | solution.py:274
  17.2 10.5 %collective-permute-start.3 = (f32[120,224]{1,0:T(8,128)S(1)}, f32[120,224]{1,0:T(8,128)S(1)}, u32[]{:S(2)}, u32[]{:S(2)}) collective-permute-start(f32[120,224]{1,0:T(8,128)S(1)} %add.73), channel_id=1, source_target_pairs={{0,16},{8,24},{16,0},{24,8},{32,48},{40,56},{48,32},{56,40},{64,80... | collective-permute-start | bytes 322568 | tf_op jit(solution)/shard_map/ppermute | solution.py:278
  27.7 13.3 %collective-permute-start.4 = (f32[120,224]{1,0:T(8,128)S(1)}, f32[120,224]{1,0:T(8,128)S(1)}, u32[]{:S(2)}, u32[]{:S(2)}) collective-permute-start(f32[120,224]{1,0:T(8,128)S(1)} %add.74), channel_id=1, source_target_pairs={{0,56},{8,48},{16,40},{24,32},{32,24},{40,16},{48,8},{56,0},{64,12... | collective-permute-start | bytes 322568 | tf_op jit(solution)/shard_map/ppermute | solution.py:278
  41.7 9.4 %collective-permute-start.5 = (f32[120,224]{1,0:T(8,128)}, f32[120,224]{1,0:T(8,128)}, u32[]{:S(2)}, u32[]{:S(2)}) collective-permute-start(f32[120,224]{1,0:T(8,128)} %get-tuple-element.44), channel_id=1, source_target_pairs={{0,64},{8,72},{16,80},{24,88},{32,96},{40,104},{48,112},{56,120},{... | collective-permute-start | bytes 322568 | tf_op jit(solution)/shard_map/ppermute | solution.py:278
  42.9 8.2 %collective-permute-start.6 = (f32[120,224]{1,0:T(8,128)}, f32[120,224]{1,0:T(8,128)}, u32[]{:S(2)}, u32[]{:S(2)}) collective-permute-start(f32[120,224]{1,0:T(8,128)} %get-tuple-element.44), channel_id=1, source_target_pairs={{0,128},{8,136},{16,144},{24,152},{32,160},{40,168},{48,176},{56,1... | collective-permute-start | bytes 322568 | tf_op jit(solution)/shard_map/ppermute | solution.py:278
  45.3 8.3 %collective-permute-start.7 = (f32[120,224]{1,0:T(8,128)}, f32[120,224]{1,0:T(8,128)}, u32[]{:S(2)}, u32[]{:S(2)}) collective-permute-start(f32[120,224]{1,0:T(8,128)} %get-tuple-element.44), channel_id=1, source_target_pairs={{0,192},{8,200},{16,208},{24,216},{32,224},{40,232},{48,240},{56,2... | collective-permute-start | bytes 322568 | tf_op jit(solution)/shard_map/ppermute | solution.py:278
  46.3 8.1 %collective-permute-start.9 = (f32[120,224]{1,0:T(8,128)}, f32[120,224]{1,0:T(8,128)S(1)}, u32[]{:S(2)}, u32[]{:S(2)}) collective-permute-start(f32[120,224]{1,0:T(8,128)} %select_add_fusion.1), channel_id=1, source_target_pairs={{16,0},{24,8},{32,16},{40,24},{48,32},{56,40},{64,48},{72,56},{80,... | collective-permute-start | bytes 322568 | tf_op jit(solution)/shard_map/ppermute | solution.py:274
  54.4 8.1 %copy-start = (bf16[3,224,2240]{2,1,0:T(8,128)(2,1)S(1)}, bf16[3,224,2240]{2,1,0:T(8,128)(2,1)}, u32[]{:S(2)}) copy-start(bf16[3,224,2240]{2,1,0:T(8,128)(2,1)} %refs_4_.1) | copy-start | bytes 9031684
  58.4 4.0 %collective-permute-start.10 = (bf16[8,4,32,224]{3,2,1,0:T(8,128)(2,1)S(1)}, bf16[8,4,32,224]{3,2,1,0:T(8,128)(2,1)S(1)}, u32[]{:S(2)}, u32[]{:S(2)}) collective-permute-start(bf16[8,4,32,224]{3,2,1,0:T(8,128)(2,1)S(1)} %get-tuple-element.40), channel_id=1, source_target_pairs={{0,1},{1,0},{2,3},{3,2},{4,5},{5,4},{6,7},{7,6},{8,9},{9,8},{10,11... | collective-permute-start | bytes 1376264 | tf_op jit(solution)/shard_map/ppermute | solution.py:283
  65.4 16.3 %collective-permute-start.12 = (bf16[2,2,32,2240]{3,2,1,0:T(8,128)(2,1)}, bf16[2,2,32,2240]{3,2,1,0:T(8,128)(2,1)S(1)}, u32[]{:S(2)}, u32[]{:S(2)}) collective-permute-start(bf16[2,2,32,2240]{3,2,1,0:T(8,128)(2,1)} %conv.4), channel_id=1, source_target_pairs={{0,4},{1,5},{2,6},{3,7},{4,0},{5,1},{6,2},{7,3},{8,12},{9,13},{10,... | collective-permute-start | bytes 1720328 | tf_op jit(solution)/shard_map/ppermute | solution.py:283
  72.1 22.9 %collective-permute-start.13 = (bf16[2,2,32,2240]{3,2,1,0:T(8,128)(2,1)}, bf16[2,2,32,2240]{3,2,1,0:T(8,128)(2,1)S(1)}, u32[]{:S(2)}, u32[]{:S(2)}) collective-permute-start(bf16[2,2,32,2240]{3,2,1,0:T(8,128)(2,1)} %get-tuple-element.41), channel_id=1, source_target_pairs={{0,2},{1,3},{2,4},{3,5},{4,6},{5,7},{6,0},{7,1},{8,10},{9,11},{10,... | collective-permute-start | bytes 1720328 | tf_op jit(solution)/shard_map/ppermute | solution.py:283
  72.5 22.5 %collective-permute-start.14 = (bf16[2,2,32,2240]{3,2,1,0:T(8,128)(2,1)}, bf16[2,2,32,2240]{3,2,1,0:T(8,128)(2,1)S(1)}, u32[]{:S(2)}, u32[]{:S(2)}) collective-permute-start(bf16[2,2,32,2240]{3,2,1,0:T(8,128)(2,1)} %get-tuple-element.42), channel_id=1, source_target_pairs={{0,6},{1,7},{2,0},{3,1},{4,2},{5,3},{6,4},{7,5},{8,14},{9,15},{10,... | collective-permute-start | bytes 1720328 | tf_op jit(solution)/shard_map/ppermute | solution.py:283
  78.0 17.0 %copy-start.1 = (f32[2240]{0:T(1024)S(1)}, f32[2240]{0:T(1024)}, u32[]{:S(2)}) copy-start(f32[2240]{0:T(1024)} %param.20) | copy-start | bytes 26884

commit v4 on v3

--- a/solution.py
+++ b/solution.py
@@ -129,7 +129,7 @@
         lead_ref[HD:] = first_ref[HD:] + jnp.where(row == 0, joined * extra, 0.0)
 
 
-def query_kernel(q_ref, halo_ref, prev_ref, own_ref, freq_ref, cos_ref, sin_ref, pair_ref, qp_ref, hi_ref, lo_ref):
+def query_kernel(q_ref, halo_ref, prev_ref, own_ref, freq_ref, cos_ref, sin_ref, pair_ref, _, qp_ref, hi_ref, lo_ref, __):
     e = pl.program_id(0)
     query = jnp.maximum(jnp.where(e < 2, halo_ref[0], q_ref[0]), 0)
     height, _, _ = query.shape
@@ -208,7 +208,10 @@
         for j in range(count):
             for t in range(2):
                 at = (2 * j + t) * each
-                outs[j][:, t, :, :size] = total[at : at + each].reshape(2, width, size).astype(outs[j].dtype)
+                piece = total[at : at + each].reshape(2, width, size)
+                for row in range(2):
+                    out = outs[2 * j + row]
+                    out[t, :, :size] = piece[row].astype(out.dtype)
 
     c_out = weights[0].shape[-1]
     for number, col in enumerate(range(0, c_out, TILE)):
@@ -247,7 +250,20 @@
     )(flags, *queries, *records, same_head)
 
 
-def conv_group(index, slots, attended, weights, dtype):
+def add_kernel(a_ref, b_ref, c_ref, d_ref, first_ref, second_ref):
+    first_ref[...] = (a_ref[...] + b_ref[...].astype(F32)).astype(BF)
+    second_ref[...] = (c_ref[...] + d_ref[...].astype(F32)).astype(BF)
+
+
+def final_kernel(*refs):
+    bias_ref, out_ref = refs[-2:]
+    for row in range(2):
+        own, low, high = (r[...].astype(F32) for r in refs[3 * row : 3 * row + 3])
+        total = own + low + high + bias_ref[...][None]
+        out_ref[row] = (total / (1.0 + jnp.exp(-total))).astype(BF)
+
+
+def conv_group(index, slots, attended, weights, dtypes):
     _, frames, width, lanes = attended[0].shape
     count = len(slots)
     c_out = weights[0].shape[-1]
@@ -261,9 +277,9 @@
             num_scalar_prefetch=1,
             grid=(pl.cdiv(c_out, TILE),),
             in_specs=[row_block(s) for _ in attended for s in slots] + [pl.BlockSpec(memory_space=pltpu.VMEM)] * 2,
-            out_specs=[pl.BlockSpec((2, 2, width, TILE), lambda n, idx: (0, 0, 0, n))] * count,
+            out_specs=[pl.BlockSpec((2, width, TILE), lambda n, idx: (0, 0, n))] * (2 * count),
         ),
-        out_shape=[pltpu.HBM((2, 2, width, c_out), dtype)] * count,
+        out_shape=[pltpu.HBM((2, width, c_out), dtype) for dtype in dtypes],
         compiler_params=LIMIT,
         name="conv",
     )(index, *[a for a in attended for _ in slots], *weights)
@@ -289,6 +305,7 @@
     queries, key_vectors, value_vectors, frame_index, height_index, width_index, frame_block, conv_weight, conv_bias
 ):
     frames, height, width, lanes = queries.shape
+    c_out = conv_weight.shape[-1]
     pairing = jnp.asarray(PAIRING, BF)
     same_head = jnp.asarray(SAME_HEAD, BF)
     freq = jnp.asarray(FREQ)[None, :]
@@ -336,6 +353,7 @@
     pair_lead = lead + jnp.where(sums & chained, next_lead, 0.0)
     far_lead = shifted(pair_lead, -2)
 
+    anywhere = pl.BlockSpec(memory_space=pl.ANY)
     query_block = pl.BlockSpec((height, 1, width, lanes), lambda e: (0, e, 0, 0))
     query_shape = pltpu.VMEM((height, 2 * frames, width, lanes), BF)
     query_call = pl.pallas_call(
@@ -344,15 +362,16 @@
         in_specs=[
             pl.BlockSpec((1, height, width, lanes), lambda e: (jnp.maximum(e - 2, 0), 0, 0, 0)),
             pl.BlockSpec((1, height, width, lanes), lambda e: (jnp.minimum(e, 1), 0, 0, 0)),
-            whole(record), whole(record), whole((1, lanes)), whole(table), whole(table), whole((lanes, lanes)),
+            whole(record), whole(record), whole((1, lanes)), whole(table), whole(table), whole((lanes, lanes)), anywhere,
         ],
-        out_specs=[query_block] * 3,
-        out_shape=[query_shape] * 3,
+        out_specs=[query_block] * 3 + [anywhere],
+        out_shape=[query_shape] * 3 + [pltpu.HBM(conv_weight.shape, BF)],
+        input_output_aliases={8: 3},
         compiler_params=LIMIT,
         name="queries",
     )
-    positive, rot_hi, rot_lo = query_call(
-        *off_chip(queries, halo, prev, second, freq, side_cos, side_sin, pairing)
+    positive, rot_hi, rot_lo, their_weight = query_call(
+        *off_chip(queries, halo, prev, second, freq, side_cos, side_sin, pairing, their_weight)
     )
 
     positive, rot_hi, rot_lo, across = lax.optimization_barrier((positive, rot_hi, rot_lo, across))
@@ -368,15 +387,33 @@
     theirs = moved(other, 0, 1)
     attended = (mine, theirs)
     weights = [pltpu.with_memory_space_constraint(w, pltpu.VMEM) for w in (conv_weight, their_weight)]
-    (far,) = conv_group(flags, (4,), attended, weights, BF)
-    from_far = moved(far, 2, 0)
-    near = conv_group(flags, (5, 6), attended, weights, BF)
-    from_low = moved(near[0], 1, 0)
-    from_high = moved(near[1], 3, 0)
-    (own,) = conv_group(flags, (7,), attended, weights, F32)
-    own = own + from_far.astype(F32)
-    summed = lax.optimization_barrier(own) + from_low.astype(F32) + from_high.astype(F32)
-    return jax.nn.silu(summed + conv_bias).astype(BF)
+    far = conv_group(flags, (4,), attended, weights, (BF, BF))
+    up = moved(far[0], 1, 0)
+    down = moved(far[1], 3, 0)
+    near = conv_group(flags, (5, 6), attended, weights, (F32, BF, BF, F32))
+    low_1 = moved(near[1], 1, 0)
+    high_0 = moved(near[2], 3, 0)
+    row = (frames, width, c_out)
+    in_vmem = pl.BlockSpec(memory_space=pltpu.VMEM)
+    joined_low, joined_high = pl.pallas_call(
+        add_kernel,
+        in_specs=[whole(row), in_vmem, whole(row), in_vmem],
+        out_specs=[whole(row)] * 2,
+        out_shape=[pltpu.HBM(row, BF)] * 2,
+        compiler_params=LIMIT,
+        name="join",
+    )(*off_chip(near[0]), up, *off_chip(near[3]), down)
+    low_0 = moved(joined_low, 1, 0)
+    high_1 = moved(joined_high, 3, 0)
+    own = conv_group(flags, (7,), attended, weights, (F32, F32))
+    return pl.pallas_call(
+        final_kernel,
+        in_specs=[whole(row), in_vmem, in_vmem] * 2 + [whole((1, c_out))],
+        out_specs=whole((2, *row)),
+        out_shape=jax.ShapeDtypeStruct((2, *row), BF),
+        compiler_params=LIMIT,
+        name="silu",
+    )(*off_chip(own[0]), low_0, high_0, *off_chip(own[1]), low_1, high_1, conv_bias[None])
 
 
 def solution(mesh):

time: 96.6 us -> 93.1 us (0.964)
  the two profiles are of different devices: /device:TPU:1 before, /device:TPU:34 now
where the time goes in v4:
time: 93.1 us; the launch traced here: 92.7 us
  starting transfers between devices  38.7 us (42%)
  Pallas kernels  25.9 us (28%)
  waiting for transfers between devices  22.8 us (24%)
  other arithmetic  3.31 us (4%)
  local copies, waits for them, and re-layouts  1.72 us (2%)
    ppermute x4, starting transfers between devices, shifted(): lax.ppermute(value, 'frame', [(i, i + by) for i in range(length) if 0 <=...  19.4 us
    ppermute x6, waiting for transfers between devices, swapped(): lax.ppermute(value, 'frame', [(i, i ^ mask) for i in range(lax.axis_size(...  13.6 us
    ppermute x6, starting transfers between devices, swapped(): lax.ppermute(value, 'frame', [(i, i ^ mask) for i in range(lax.axis_size(...  10.8 us
    pallas_call x3, Pallas kernels, conv_group(): pl.pallas_call(functools.partial(conv_kernel, count), grid_spec=pltpu.Pre...  9.98 us
    ppermute x8, waiting for transfers between devices, moved(): lax.ppermute(value, 'head', [(y * 2 + c, (y + dy) % chips * 2 + (c + dc)...  9.12 us
    ppermute x8, starting transfers between devices, moved(): lax.ppermute(value, 'head', [(y * 2 + c, (y + dy) % chips * 2 + (c + dc)...  8.6 us
    pallas_call x1, Pallas kernels, attend(): pl.pallas_call(attend_kernel, grid_spec=pltpu.PrefetchScalarGridSpec(num_...  3.97 us
    pallas_call x1, Pallas kernels, block(): state_call(*off_chip(frame_block, frame_index, height_index, width_index,...  3.9 us
  transfers between devices with their start and end apart: 18, of which 7 were waited for; matrix products, arithmetic and copies ran while one was open for 4% of the time, Pallas kernels for 18%

profile of v4, /device:TPU:34, one launch (start us, length us, event | category | flops | bytes accessed | tf_op | source)
XLA Modules:
  0.0 92.7 jit_solution(5705053404376636214)
XLA Ops:
  0.0 0.0 collective-permute-start.2
  0.0 3.9 %frame_state.1 = (f32[120,224]{1,0:T(8,128)}, f32[120,224]{1,0:T(8,128)}, f32[120,224]{1,0:T(8,128)S(1)}, f32[120,224]{1,0:T(8,128)S(1)}, f32[48,224]{1,0:T(8,128)}, /*index=5*/f32[48,224]{1,0:T(8,128)}) custom-call(s32[2]{0:T(128)} %blocks.1, s32[2]{0:T(128)} %frames.1, s32[16]{0:T(128)} %heights.1, s32[32]{0:T(128)} %widths.1, ...), custom_call_target="tpu_custom_call" | custom-call | tf_op jit(solution)/shard_map/frame_state/pallas_call | solution.py:329
  3.9 0.1 collective-permute-start.3
  4.0 5.6 %collective-permute-start = (bf16[2,16,32,224]{3,2,1,0:T(8,128)(2,1)}, bf16[2,16,32,224]{3,2,1,0:T(8,128)(2,1)}, u32[]{:S(2)}, u32[]{:S(2)}) collective-permute-start(bf16[2,16,32,224]{3,2,1,0:T(8,128)(2,1)} %q_ref.1), channel_id=1, source_target_pairs={{0,8},{8,16},{16,24},{24,32},{32,40},{40,48},{48,56},{56,64},{64,7... | collective-permute-start | bytes 1376264 | tf_op jit(solution)/shard_map/ppermute | solution.py:290
  9.6 2.0 %collective-permute-start.1 = (f32[120,224]{1,0:T(8,128)}, f32[120,224]{1,0:T(8,128)}, u32[]{:S(2)}, u32[]{:S(2)}) collective-permute-start(f32[120,224]{1,0:T(8,128)} %get-tuple-element.33.own_ref.second_ref), channel_id=1, source_target_pairs={{0,8},{8,16},{16,24},{24,32},{32,40},{40,48},{48,56},{56,64},{64,7... | collective-permute-start | bytes 322568 | tf_op jit(solution)/shard_map/ppermute | solution.py:290
  11.7 3.8 %collective-permute-start.9 = (f32[120,224]{1,0:T(8,128)S(1)}, f32[120,224]{1,0:T(8,128)S(1)}, u32[]{:S(2)}, u32[]{:S(2)}) collective-permute-start(f32[120,224]{1,0:T(8,128)S(1)} %get-tuple-element.44), channel_id=1, source_target_pairs={{8,0},{16,8},{24,16},{32,24},{40,32},{48,40},{56,48},{64,56},{72,6... | collective-permute-start | bytes 322568 | tf_op jit(solution)/shard_map/ppermute | solution.py:290
  15.5 0.0 collective-permute-done.3
  15.5 0.9 add.52
  16.5 3.7 %collective-permute-start.4 = (f32[120,224]{1,0:T(8,128)S(1)}, f32[120,224]{1,0:T(8,128)S(1)}, u32[]{:S(2)}, u32[]{:S(2)}) collective-permute-start(f32[120,224]{1,0:T(8,128)S(1)} %add.52), channel_id=1, source_target_pairs={{0,16},{8,24},{16,0},{24,8},{32,48},{40,56},{48,32},{56,40},{64,80... | collective-permute-start | bytes 322568 | tf_op jit(solution)/shard_map/ppermute | solution.py:294
  20.1 9.2 %collective-permute-done.4 = f32[120,224]{1,0:T(8,128)S(1)} collective-permute-done((f32[120,224]{1,0:T(8,128)S(1)}, f32[120,224]{1,0:T(8,128)S(1)}, u32[]{:S(2)}, u32[]{:S(2)}) %collective-permute-start.4) | collective-permute-done | bytes 107552 | tf_op jit(solution)/shard_map/ppermute | solution.py:294
  29.3 3.5 %collective-permute-start.5 = (f32[120,224]{1,0:T(8,128)S(1)}, f32[120,224]{1,0:T(8,128)S(1)}, u32[]{:S(2)}, u32[]{:S(2)}) collective-permute-start(f32[120,224]{1,0:T(8,128)S(1)} %add.53), channel_id=1, source_target_pairs={{0,56},{8,48},{16,40},{24,32},{32,24},{40,16},{48,8},{56,0},{64,12... | collective-permute-start | bytes 322568 | tf_op jit(solution)/shard_map/ppermute | solution.py:294
  32.8 0.0 collective-permute-done.9.next_ref
  32.9 4.4 %collective-permute-done.5 = f32[120,224]{1,0:T(8,128)S(1)} collective-permute-done((f32[120,224]{1,0:T(8,128)S(1)}, f32[120,224]{1,0:T(8,128)S(1)}, u32[]{:S(2)}, u32[]{:S(2)}) %collective-permute-start.5) | collective-permute-done | bytes 107552 | tf_op jit(solution)/shard_map/ppermute | solution.py:294
  37.3 1.6 %select_add_fusion = (f32[120,224]{1,0:T(8,128)S(1)}, f32[120,224]{1,0:T(8,128)}) fusion(f32[120,224]{1,0:T(8,128)S(1)} %collective-permute-done.5, f32[120,224]{1,0:T(8,128)S(1)} %collective-permute-done.4, f32[120,224]{1,0:T(8,128)} %collective-permute-done.3, pred[]{:T(512)S(6)} %ne.45, pred[]{:T(512)S(6)} %ne.44, pred[]{:T(512)S(6)} %ne.43, ...), kind=kLoop, calls=%fused_computation | loop fusion | flops 161280 | bytes 645123 | tf_op jit(solution)/shard_map/add | solution.py:338
  38.9 0.5 collective-permute-start.6
  39.4 2.4 %collective-permute-start.7 = (f32[120,224]{1,0:T(8,128)}, f32[120,224]{1,0:T(8,128)}, u32[]{:S(2)}, u32[]{:S(2)}) collective-permute-start(f32[120,224]{1,0:T(8,128)} %get-tuple-element.62), channel_id=1, source_target_pairs={{0,128},{8,136},{16,144},{24,152},{32,160},{40,168},{48,176},{56,1... | collective-permute-start | bytes 322568 | tf_op jit(solution)/shard_map/ppermute | solution.py:294
  41.9 0.0 collective-permute-done.1.prev_ref
  41.9 0.5 collective-permute-start.8
  42.4 0.7 select_add_fusion.1
  43.1 0.0 collective-permute-done.halo_ref
  43.2 7.9 %collective-permute-start.10 = (f32[120,224]{1,0:T(8,128)}, f32[120,224]{1,0:T(8,128)S(1)}, u32[]{:S(2)}, u32[]{:S(2)}) collective-permute-start(f32[120,224]{1,0:T(8,128)} %select_add_fusion.1), channel_id=1, source_target_pairs={{16,0},{24,8},{32,16},{40,24},{48,32},{56,40},{64,48},{72,56},{80,... | collective-permute-start | bytes 322568 | tf_op jit(solution)/shard_map/ppermute | solution.py:290
  51.1 0.1 stack.47.flags.idx
  51.2 0.0 collective-permute-done.2._
  51.2 0.0 copy-start
  51.2 1.6 %copy-done = bf16[3,224,2240]{2,1,0:T(8,128)(2,1)} copy-done((bf16[3,224,2240]{2,1,0:T(8,128)(2,1)}, bf16[3,224,2240]{2,1,0:T(8,128)(2,1)S(1)}, u32[]{:S(2)}) %copy-start) | copy-done | bytes 3010584
  52.8 0.0 copy-start.2
  52.8 3.4 %queries.1 = (bf16[16,4,32,224]{3,2,1,0:T(8,128)(2,1)S(1)}, bf16[16,4,32,224]{3,2,1,0:T(8,128)(2,1)S(1)}, bf16[16,4,32,224]{3,2,1,0:T(8,128)(2,1)S(1)}, bf16[3,224,2240]{2,1,0:T(8,128)(2,1)}) custom-call(bf16[2,16,32,224]{3,2,1,0:T(8,128)(2,1)} %q_ref.1, bf16[2,16,32,224]{3,2,1,0:T(8,128)(2,1)} %collective-permute-done.halo_ref, ...), custom_call_target="tpu_custom_call", output_to_operand_aliasing={{3}: (8, {})} | custom-call | tf_op jit(solution)/shard_map/queries/pallas_call | solution.py:373
  56.3 0.0 copy-start.1
  56.3 0.0 collective-permute-done.6.a_ref
  56.3 0.0 collective-permute-done.7.b_ref
  56.3 0.0 collective-permute-done.8.c_ref
  56.3 0.0 collective-permute-done.10.far_ref
  56.3 4.0 %attend.1 = (bf16[8,4,32,224]{3,2,1,0:T(8,128)(2,1)S(1)}, bf16[8,4,32,224]{3,2,1,0:T(8,128)(2,1)S(1)}) custom-call(s32[8]{0:T(128)S(1)} %stack.47.flags.idx, bf16[16,4,32,224]{3,2,1,0:T(8,128)(2,1)S(1)} %get-tuple-element.40.qp_ref, bf16[16,4,32,224]{3,2,1,0:T(8,128)(2,1)S(1)} %get-tuple-element.41.hi_ref, ...), custom_call_target="tpu_custom_call" | custom-call | tf_op jit(solution)/shard_map/attend/pallas_call | solution.py:238
  60.3 0.1 collective-permute-start.11
  60.4 1.9 %collective-permute-done.11.refs_1_.refs_2_.refs_3_ = bf16[8,4,32,224]{3,2,1,0:T(8,128)(2,1)S(1)} collective-permute-done((bf16[8,4,32,224]{3,2,1,0:T(8,128)(2,1)S(1)}, bf16[8,4,32,224]{3,2,1,0:T(8,128)(2,1)S(1)}, u32[]{:S(2)}, u32[]{:S(2)}) %collective-permute-start.11) | collective-permute-done | bytes 458784 | tf_op jit(solution)/shard_map/ppermute | solution.py:299
  62.3 0.0 copy-done.2
  62.3 0.0 copy-done.1
  62.3 3.0 %conv.5 = (bf16[2,32,2240]{2,1,0:T(8,128)(2,1)}, bf16[2,32,2240]{2,1,0:T(8,128)(2,1)}) custom-call(s32[8]{0:T(128)S(1)} %stack.47.flags.idx, bf16[8,4,32,224]{3,2,1,0:T(8,128)(2,1)S(1)} %get-tuple-element.48.refs_0_.refs_1_, bf16[8,4,32,224]{3,2,1,0:T(8,128)(2,1)S(1)} %collective-permute-done.11.refs_1_.refs_2_.refs_3_, bf16[3,224,2240]{2,1,0:T(8,128)(2,1)S(1)} %copy-done.2, ...), custom_call_target="tpu_custom_call" | custom-call | tf_op jit(solution)/shard_map/conv/pallas_call | solution.py:274
  65.3 1.6 %collective-permute-start.12 = (bf16[2,32,2240]{2,1,0:T(8,128)(2,1)}, bf16[2,32,2240]{2,1,0:T(8,128)(2,1)S(1)}, u32[]{:S(2)}, u32[]{:S(2)}) collective-permute-start(bf16[2,32,2240]{2,1,0:T(8,128)(2,1)} %get-tuple-element.53), channel_id=1, source_target_pairs={{0,2},{1,3},{2,4},{3,5},{4,6},{5,7},{6,0},{7,1},{8,10},{9,11},{10,... | collective-permute-start | bytes 860168 | tf_op jit(solution)/shard_map/ppermute | solution.py:299
  66.9 0.0 copy-start.3
  66.9 1.7 %collective-permute-start.13 = (bf16[2,32,2240]{2,1,0:T(8,128)(2,1)}, bf16[2,32,2240]{2,1,0:T(8,128)(2,1)S(1)}, u32[]{:S(2)}, u32[]{:S(2)}) collective-permute-start(bf16[2,32,2240]{2,1,0:T(8,128)(2,1)} %get-tuple-element.55), channel_id=1, source_target_pairs={{0,6},{1,7},{2,0},{3,1},{4,2},{5,3},{6,4},{7,5},{8,14},{9,15},{10,... | collective-permute-start | bytes 860168 | tf_op jit(solution)/shard_map/ppermute | solution.py:299
  68.5 3.9 %conv.4 = (f32[2,32,2240]{2,1,0:T(8,128)}, bf16[2,32,2240]{2,1,0:T(8,128)(2,1)}, bf16[2,32,2240]{2,1,0:T(8,128)(2,1)}, f32[2,32,2240]{2,1,0:T(8,128)}) custom-call(s32[8]{0:T(128)S(1)} %stack.47.flags.idx, bf16[8,4,32,224]{3,2,1,0:T(8,128)(2,1)S(1)} %get-tuple-element.48.refs_0_.refs_1_, bf16[8,4,32,224]{3,2,1,0:T(8,128)(2,1)S(1)} %get-tuple-element.48.refs_0_.refs_1_, ...), custom_call_target="tpu_custom_call" | custom-call | tf_op jit(solution)/shard_map/conv/pallas_call | solution.py:274
  72.5 1.8 %collective-permute-start.15 = (bf16[2,32,2240]{2,1,0:T(8,128)(2,1)}, bf16[2,32,2240]{2,1,0:T(8,128)(2,1)S(1)}, u32[]{:S(2)}, u32[]{:S(2)}) collective-permute-start(bf16[2,32,2240]{2,1,0:T(8,128)(2,1)} %get-tuple-element.57), channel_id=1, source_target_pairs={{0,6},{1,7},{2,0},{3,1},{4,2},{5,3},{6,4},{7,5},{8,14},{9,15},{10,... | collective-permute-start | bytes 860168 | tf_op jit(solution)/shard_map/ppermute | solution.py:299
  74.2 0.2 collective-permute-start.16
  74.5 1.3 %collective-permute-done.12.b_ref = bf16[2,32,2240]{2,1,0:T(8,128)(2,1)S(1)} collective-permute-done((bf16[2,32,2240]{2,1,0:T(8,128)(2,1)}, bf16[2,32,2240]{2,1,0:T(8,128)(2,1)S(1)}, u32[]{:S(2)}, u32[]{:S(2)}) %collective-permute-start.12) | collective-permute-done | bytes 286752 | tf_op jit(solution)/shard_map/ppermute | solution.py:299
  75.8 0.8 collective-permute-done.13.d_ref
  76.6 2.1 %join.1 = (bf16[2,32,2240]{2,1,0:T(8,128)(2,1)}, bf16[2,32,2240]{2,1,0:T(8,128)(2,1)}) custom-call(f32[2,32,2240]{2,1,0:T(8,128)} %get-tuple-element.52.a_ref, bf16[2,32,2240]{2,1,0:T(8,128)(2,1)S(1)} %collective-permute-done.12.b_ref, f32[2,32,2240]{2,1,0:T(8,128)} %get-tuple-element.54.c_ref, bf16[2,32,2240]{2,1,0:T(8,128)(2,1)S(1)} %collective-permute-done.13.d_ref), custom_call_target="tpu_custom_call" | custom-call | tf_op jit(solution)/shard_map/join/pallas_call | solution.py:398
  78.7 1.9 %collective-permute-start.14 = (bf16[2,32,2240]{2,1,0:T(8,128)(2,1)}, bf16[2,32,2240]{2,1,0:T(8,128)(2,1)S(1)}, u32[]{:S(2)}, u32[]{:S(2)}) collective-permute-start(bf16[2,32,2240]{2,1,0:T(8,128)(2,1)} %get-tuple-element.56), channel_id=1, source_target_pairs={{0,2},{1,3},{2,4},{3,5},{4,6},{5,7},{6,0},{7,1},{8,10},{9,11},{10,... | collective-permute-start | bytes 860168 | tf_op jit(solution)/shard_map/ppermute | solution.py:299
  80.7 1.3 %collective-permute-start.17 = (bf16[2,32,2240]{2,1,0:T(8,128)(2,1)}, bf16[2,32,2240]{2,1,0:T(8,128)(2,1)S(1)}, u32[]{:S(2)}, u32[]{:S(2)}) collective-permute-start(bf16[2,32,2240]{2,1,0:T(8,128)(2,1)} %get-tuple-element.60), channel_id=1, source_target_pairs={{0,6},{1,7},{2,0},{3,1},{4,2},{5,3},{6,4},{7,5},{8,14},{9,15},{10,... | collective-permute-start | bytes 860168 | tf_op jit(solution)/shard_map/ppermute | solution.py:299
  82.0 0.0 copy-done.3
  82.0 3.1 %conv.3 = (f32[2,32,2240]{2,1,0:T(8,128)}, f32[2,32,2240]{2,1,0:T(8,128)}) custom-call(s32[8]{0:T(128)S(1)} %stack.47.flags.idx, bf16[8,4,32,224]{3,2,1,0:T(8,128)(2,1)S(1)} %get-tuple-element.48.refs_0_.refs_1_, bf16[8,4,32,224]{3,2,1,0:T(8,128)(2,1)S(1)} %collective-permute-done.11.refs_1_.refs_2_.refs_3_, bf16[3,224,2240]{2,1,0:T(8,128)(2,1)S(1)} %copy-done.2, ...), custom_call_target="tpu_custom_call" | custom-call | tf_op jit(solution)/shard_map/conv/pallas_call | solution.py:274
  85.1 0.0 collective-permute-done.15.refs_2_
  85.1 0.5 collective-permute-done.16.refs_4_
  85.5 4.6 %collective-permute-done.14.refs_1_ = bf16[2,32,2240]{2,1,0:T(8,128)(2,1)S(1)} collective-permute-done((bf16[2,32,2240]{2,1,0:T(8,128)(2,1)}, bf16[2,32,2240]{2,1,0:T(8,128)(2,1)S(1)}, u32[]{:S(2)}, u32[]{:S(2)}) %collective-permute-start.14) | collective-permute-done | bytes 286752 | tf_op jit(solution)/shard_map/ppermute | solution.py:299
  90.2 0.0 collective-permute-done.17.refs_5_
  90.2 2.5 %silu.1 = bf16[2,2,32,2240]{3,2,1,0:T(8,128)(2,1)} custom-call(f32[2,32,2240]{2,1,0:T(8,128)} %get-tuple-element.51.refs_0_, bf16[2,32,2240]{2,1,0:T(8,128)(2,1)S(1)} %collective-permute-done.14.refs_1_, bf16[2,32,2240]{2,1,0:T(8,128)(2,1)S(1)} %collective-permute-done.15.refs_2_, f32[2,32,2240]{2,1,0:T(8,128)} %get-tuple-element.58.refs_3_, ...), custom_call_target="tpu_custom_call" | custom-call | tf_op jit(solution)/shard_map/silu/pallas_call | solution.py:409
  (4 shorter events, 0.1 us)
Async XLA Ops:
  0.0 51.2 %collective-permute-start.2 = (bf16[3,224,2240]{2,1,0:T(8,128)(2,1)}, bf16[3,224,2240]{2,1,0:T(8,128)(2,1)S(1)}, u32[]{:S(2)}, u32[]{:S(2)}) collective-permute-start(bf16[3,224,2240]{2,1,0:T(8,128)(2,1)} %refs_2_.3), channel_id=1, source_target_pairs={{0,1},{1,0},{2,3},{3,2},{4,5},{5,4},{6,7},{7,6},{8,9},{9,8},{10,11... | collective-permute-start | bytes 9031688 | tf_op jit(solution)/shard_map/ppermute | solution.py:299
  3.9 11.6 %collective-permute-start.3 = (f32[120,224]{1,0:T(8,128)S(1)}, f32[120,224]{1,0:T(8,128)}, u32[]{:S(2)}, u32[]{:S(2)}) collective-permute-start(f32[120,224]{1,0:T(8,128)S(1)} %get-tuple-element.39), channel_id=1, source_target_pairs={{0,8},{8,0},{16,24},{24,16},{32,40},{40,32},{48,56},{56,48},{64,72... | collective-permute-start | bytes 322568 | tf_op jit(solution)/shard_map/ppermute | solution.py:294
  4.0 39.1 %collective-permute-start = (bf16[2,16,32,224]{3,2,1,0:T(8,128)(2,1)}, bf16[2,16,32,224]{3,2,1,0:T(8,128)(2,1)}, u32[]{:S(2)}, u32[]{:S(2)}) collective-permute-start(bf16[2,16,32,224]{3,2,1,0:T(8,128)(2,1)} %q_ref.1), channel_id=1, source_target_pairs={{0,8},{8,16},{16,24},{24,32},{32,40},{40,48},{48,56},{56,64},{64,7... | collective-permute-start | bytes 1376264 | tf_op jit(solution)/shard_map/ppermute | solution.py:290
  9.6 32.2 %collective-permute-start.1 = (f32[120,224]{1,0:T(8,128)}, f32[120,224]{1,0:T(8,128)}, u32[]{:S(2)}, u32[]{:S(2)}) collective-permute-start(f32[120,224]{1,0:T(8,128)} %get-tuple-element.33.own_ref.second_ref), channel_id=1, source_target_pairs={{0,8},{8,16},{16,24},{24,32},{32,40},{40,48},{48,56},{56,64},{64,7... | collective-permute-start | bytes 322568 | tf_op jit(solution)/shard_map/ppermute | solution.py:290
  11.7 21.2 %collective-permute-start.9 = (f32[120,224]{1,0:T(8,128)S(1)}, f32[120,224]{1,0:T(8,128)S(1)}, u32[]{:S(2)}, u32[]{:S(2)}) collective-permute-start(f32[120,224]{1,0:T(8,128)S(1)} %get-tuple-element.44), channel_id=1, source_target_pairs={{8,0},{16,8},{24,16},{32,24},{40,32},{48,40},{56,48},{64,56},{72,6... | collective-permute-start | bytes 322568 | tf_op jit(solution)/shard_map/ppermute | solution.py:290
  16.5 12.9 %collective-permute-start.4 = (f32[120,224]{1,0:T(8,128)S(1)}, f32[120,224]{1,0:T(8,128)S(1)}, u32[]{:S(2)}, u32[]{:S(2)}) collective-permute-start(f32[120,224]{1,0:T(8,128)S(1)} %add.52), channel_id=1, source_target_pairs={{0,16},{8,24},{16,0},{24,8},{32,48},{40,56},{48,32},{56,40},{64,80... | collective-permute-start | bytes 322568 | tf_op jit(solution)/shard_map/ppermute | solution.py:294
  29.3 8.0 %collective-permute-start.5 = (f32[120,224]{1,0:T(8,128)S(1)}, f32[120,224]{1,0:T(8,128)S(1)}, u32[]{:S(2)}, u32[]{:S(2)}) collective-permute-start(f32[120,224]{1,0:T(8,128)S(1)} %add.53), channel_id=1, source_target_pairs={{0,56},{8,48},{16,40},{24,32},{32,24},{40,16},{48,8},{56,0},{64,12... | collective-permute-start | bytes 322568 | tf_op jit(solution)/shard_map/ppermute | solution.py:294
  38.9 17.4 %collective-permute-start.6 = (f32[120,224]{1,0:T(8,128)}, f32[120,224]{1,0:T(8,128)}, u32[]{:S(2)}, u32[]{:S(2)}) collective-permute-start(f32[120,224]{1,0:T(8,128)} %get-tuple-element.62), channel_id=1, source_target_pairs={{0,64},{8,72},{16,80},{24,88},{32,96},{40,104},{48,112},{56,120},{... | collective-permute-start | bytes 322568 | tf_op jit(solution)/shard_map/ppermute | solution.py:294
  39.4 16.9 %collective-permute-start.7 = (f32[120,224]{1,0:T(8,128)}, f32[120,224]{1,0:T(8,128)}, u32[]{:S(2)}, u32[]{:S(2)}) collective-permute-start(f32[120,224]{1,0:T(8,128)} %get-tuple-element.62), channel_id=1, source_target_pairs={{0,128},{8,136},{16,144},{24,152},{32,160},{40,168},{48,176},{56,1... | collective-permute-start | bytes 322568 | tf_op jit(solution)/shard_map/ppermute | solution.py:294
  41.9 14.5 %collective-permute-start.8 = (f32[120,224]{1,0:T(8,128)}, f32[120,224]{1,0:T(8,128)}, u32[]{:S(2)}, u32[]{:S(2)}) collective-permute-start(f32[120,224]{1,0:T(8,128)} %get-tuple-element.62), channel_id=1, source_target_pairs={{0,192},{8,200},{16,208},{24,216},{32,224},{40,232},{48,240},{56,2... | collective-permute-start | bytes 322568 | tf_op jit(solution)/shard_map/ppermute | solution.py:294
  43.2 13.2 %collective-permute-start.10 = (f32[120,224]{1,0:T(8,128)}, f32[120,224]{1,0:T(8,128)S(1)}, u32[]{:S(2)}, u32[]{:S(2)}) collective-permute-start(f32[120,224]{1,0:T(8,128)} %select_add_fusion.1), channel_id=1, source_target_pairs={{16,0},{24,8},{32,16},{40,24},{48,32},{56,40},{64,48},{72,56},{80,... | collective-permute-start | bytes 322568 | tf_op jit(solution)/shard_map/ppermute | solution.py:290
  51.2 1.6 %copy-start = (bf16[3,224,2240]{2,1,0:T(8,128)(2,1)}, bf16[3,224,2240]{2,1,0:T(8,128)(2,1)S(1)}, u32[]{:S(2)}) copy-start(bf16[3,224,2240]{2,1,0:T(8,128)(2,1)S(1)} %collective-permute-done.2._) | copy-start | bytes 9031684
  52.8 9.5 %copy-start.2 = (bf16[3,224,2240]{2,1,0:T(8,128)(2,1)S(1)}, bf16[3,224,2240]{2,1,0:T(8,128)(2,1)}, u32[]{:S(2)}) copy-start(bf16[3,224,2240]{2,1,0:T(8,128)(2,1)} %refs_2_.3) | copy-start | bytes 9031684
  56.3 6.0 %copy-start.1 = (bf16[3,224,2240]{2,1,0:T(8,128)(2,1)S(1)}, bf16[3,224,2240]{2,1,0:T(8,128)(2,1)}, u32[]{:S(2)}) copy-start(bf16[3,224,2240]{2,1,0:T(8,128)(2,1)} %get-tuple-element.50.refs_3_.refs_5_) | copy-start | bytes 9031684
  60.3 2.0 %collective-permute-start.11 = (bf16[8,4,32,224]{3,2,1,0:T(8,128)(2,1)S(1)}, bf16[8,4,32,224]{3,2,1,0:T(8,128)(2,1)S(1)}, u32[]{:S(2)}, u32[]{:S(2)}) collective-permute-start(bf16[8,4,32,224]{3,2,1,0:T(8,128)(2,1)S(1)} %get-tuple-element.49), channel_id=1, source_target_pairs={{0,1},{1,0},{2,3},{3,2},{4,5},{5,4},{6,7},{7,6},{8,9},{9,8},{10,11... | collective-permute-start | bytes 1376264 | tf_op jit(solution)/shard_map/ppermute | solution.py:299
  65.3 10.5 %collective-permute-start.12 = (bf16[2,32,2240]{2,1,0:T(8,128)(2,1)}, bf16[2,32,2240]{2,1,0:T(8,128)(2,1)S(1)}, u32[]{:S(2)}, u32[]{:S(2)}) collective-permute-start(bf16[2,32,2240]{2,1,0:T(8,128)(2,1)} %get-tuple-element.53), channel_id=1, source_target_pairs={{0,2},{1,3},{2,4},{3,5},{4,6},{5,7},{6,0},{7,1},{8,10},{9,11},{10,... | collective-permute-start | bytes 860168 | tf_op jit(solution)/shard_map/ppermute | solution.py:299
  66.9 15.1 %copy-start.3 = (f32[2240]{0:T(1024)S(1)}, f32[2240]{0:T(1024)}, u32[]{:S(2)}) copy-start(f32[2240]{0:T(1024)} %param.20) | copy-start | bytes 26884
  66.9 9.7 %collective-permute-start.13 = (bf16[2,32,2240]{2,1,0:T(8,128)(2,1)}, bf16[2,32,2240]{2,1,0:T(8,128)(2,1)S(1)}, u32[]{:S(2)}, u32[]{:S(2)}) collective-permute-start(bf16[2,32,2240]{2,1,0:T(8,128)(2,1)} %get-tuple-element.55), channel_id=1, source_target_pairs={{0,6},{1,7},{2,0},{3,1},{4,2},{5,3},{6,4},{7,5},{8,14},{9,15},{10,... | collective-permute-start | bytes 860168 | tf_op jit(solution)/shard_map/ppermute | solution.py:299
  72.5 12.6 %collective-permute-start.15 = (bf16[2,32,2240]{2,1,0:T(8,128)(2,1)}, bf16[2,32,2240]{2,1,0:T(8,128)(2,1)S(1)}, u32[]{:S(2)}, u32[]{:S(2)}) collective-permute-start(bf16[2,32,2240]{2,1,0:T(8,128)(2,1)} %get-tuple-element.57), channel_id=1, source_target_pairs={{0,6},{1,7},{2,0},{3,1},{4,2},{5,3},{6,4},{7,5},{8,14},{9,15},{10,... | collective-permute-start | bytes 860168 | tf_op jit(solution)/shard_map/ppermute | solution.py:299
  74.2 11.3 %collective-permute-start.16 = (bf16[2,32,2240]{2,1,0:T(8,128)(2,1)}, bf16[2,32,2240]{2,1,0:T(8,128)(2,1)S(1)}, u32[]{:S(2)}, u32[]{:S(2)}) collective-permute-start(bf16[2,32,2240]{2,1,0:T(8,128)(2,1)} %get-tuple-element.59), channel_id=1, source_target_pairs={{0,2},{1,3},{2,4},{3,5},{4,6},{5,7},{6,0},{7,1},{8,10},{9,11},{10,... | collective-permute-start | bytes 860168 | tf_op jit(solution)/shard_map/ppermute | solution.py:299
  78.7 11.5 %collective-permute-start.14 = (bf16[2,32,2240]{2,1,0:T(8,128)(2,1)}, bf16[2,32,2240]{2,1,0:T(8,128)(2,1)S(1)}, u32[]{:S(2)}, u32[]{:S(2)}) collective-permute-start(bf16[2,32,2240]{2,1,0:T(8,128)(2,1)} %get-tuple-element.56), channel_id=1, source_target_pairs={{0,2},{1,3},{2,4},{3,5},{4,6},{5,7},{6,0},{7,1},{8,10},{9,11},{10,... | collective-permute-start | bytes 860168 | tf_op jit(solution)/shard_map/ppermute | solution.py:299
  80.7 9.5 %collective-permute-start.17 = (bf16[2,32,2240]{2,1,0:T(8,128)(2,1)}, bf16[2,32,2240]{2,1,0:T(8,128)(2,1)S(1)}, u32[]{:S(2)}, u32[]{:S(2)}) collective-permute-start(bf16[2,32,2240]{2,1,0:T(8,128)(2,1)} %get-tuple-element.60), channel_id=1, source_target_pairs={{0,6},{1,7},{2,0},{3,1},{4,2},{5,3},{6,4},{7,5},{8,14},{9,15},{10,... | collective-permute-start | bytes 860168 | tf_op jit(solution)/shard_map/ppermute | solution.py:299

commit v5 on v4

--- a/solution.py
+++ b/solution.py
@@ -211,7 +211,7 @@
                 piece = total[at : at + each].reshape(2, width, size)
                 for row in range(2):
                     out = outs[2 * j + row]
-                    out[t, :, :size] = piece[row].astype(out.dtype)
+                    out[t, :, col : col + size] = piece[row].astype(out.dtype)
 
     c_out = weights[0].shape[-1]
     for number, col in enumerate(range(0, c_out, TILE)):
@@ -277,9 +277,9 @@
             num_scalar_prefetch=1,
             grid=(pl.cdiv(c_out, TILE),),
             in_specs=[row_block(s) for _ in attended for s in slots] + [pl.BlockSpec(memory_space=pltpu.VMEM)] * 2,
-            out_specs=[pl.BlockSpec((2, width, TILE), lambda n, idx: (0, 0, n))] * (2 * count),
+            out_specs=[pl.BlockSpec(memory_space=pltpu.VMEM)] * (2 * count),
         ),
-        out_shape=[pltpu.HBM((2, width, c_out), dtype) for dtype in dtypes],
+        out_shape=[pltpu.VMEM((2, width, c_out), dtype) for dtype in dtypes],
         compiler_params=LIMIT,
         name="conv",
     )(index, *[a for a in attended for _ in slots], *weights)
@@ -397,23 +397,23 @@
     in_vmem = pl.BlockSpec(memory_space=pltpu.VMEM)
     joined_low, joined_high = pl.pallas_call(
         add_kernel,
-        in_specs=[whole(row), in_vmem, whole(row), in_vmem],
-        out_specs=[whole(row)] * 2,
-        out_shape=[pltpu.HBM(row, BF)] * 2,
+        in_specs=[in_vmem] * 4,
+        out_specs=[in_vmem] * 2,
+        out_shape=[pltpu.VMEM(row, BF)] * 2,
         compiler_params=LIMIT,
         name="join",
-    )(*off_chip(near[0]), up, *off_chip(near[3]), down)
+    )(near[0], up, near[3], down)
     low_0 = moved(joined_low, 1, 0)
     high_1 = moved(joined_high, 3, 0)
     own = conv_group(flags, (7,), attended, weights, (F32, F32))
     return pl.pallas_call(
         final_kernel,
-        in_specs=[whole(row), in_vmem, in_vmem] * 2 + [whole((1, c_out))],
+        in_specs=[in_vmem] * 6 + [whole((1, c_out))],
         out_specs=whole((2, *row)),
         out_shape=jax.ShapeDtypeStruct((2, *row), BF),
         compiler_params=LIMIT,
         name="silu",
-    )(*off_chip(own[0]), low_0, high_0, *off_chip(own[1]), low_1, high_1, conv_bias[None])
+    )(own[0], low_0, high_0, own[1], low_1, high_1, conv_bias[None])
 
 
 def solution(mesh):

time: 93.1 us -> 90 us (0.967)
  Pallas kernels: 25.9 us -> 19.9 us
  waiting for transfers between devices: 22.8 us -> 25.5 us
    pallas_call x2, Pallas kernels: 4.65 us -> 1.38 us  [the longest x1 1.27 us: block(): pl.pallas_call(final_kernel, in_specs=[in_vmem] * 6 + [whole((1, c_out))]...]
    pallas_call x3, Pallas kernels: 9.98 us -> 7.23 us  [conv_group(): pl.pallas_call(functools.partial(conv_kernel, count), grid_spec=pltpu.Pre...]
    ppermute x8, waiting for transfers between devices: 9.12 us -> 11.8 us  [moved(): lax.ppermute(value, 'head', [(y * 2 + c, (y + dy) % chips * 2 + (c + dc)...]
  transfers between devices with their start and end apart: 18 -> 18, of which waited for: 7 -> 8; matrix products, arithmetic and copies ran while one was open for 4% -> 4% of each run, Pallas kernels for 18% -> 14%
where the time goes in v5:
time: 90 us; the launch traced here: 89.7 us
  starting transfers between devices  39 us (43%)
  waiting for transfers between devices  25.5 us (28%)
  Pallas kernels  19.9 us (22%)
  other arithmetic  3.31 us (4%)
  local copies, waits for them, and re-layouts  1.72 us (2%)
    ppermute x4, starting transfers between devices, shifted(): lax.ppermute(value, 'frame', [(i, i + by) for i in range(length) if 0 <=...  19.4 us
    ppermute x6, waiting for transfers between devices, swapped(): lax.ppermute(value, 'frame', [(i, i ^ mask) for i in range(lax.axis_size(...  13.6 us
    ppermute x8, waiting for transfers between devices, moved(): lax.ppermute(value, 'head', [(y * 2 + c, (y + dy) % chips * 2 + (c + dc)...  11.8 us
    ppermute x6, starting transfers between devices, swapped(): lax.ppermute(value, 'frame', [(i, i ^ mask) for i in range(lax.axis_size(...  10.8 us
    ppermute x8, starting transfers between devices, moved(): lax.ppermute(value, 'head', [(y * 2 + c, (y + dy) % chips * 2 + (c + dc)...  8.89 us
    pallas_call x3, Pallas kernels, conv_group(): pl.pallas_call(functools.partial(conv_kernel, count), grid_spec=pltpu.Pre...  7.23 us
    pallas_call x1, Pallas kernels, attend(): pl.pallas_call(attend_kernel, grid_spec=pltpu.PrefetchScalarGridSpec(num_...  3.97 us
    pallas_call x1, Pallas kernels, block(): state_call(*off_chip(frame_block, frame_index, height_index, width_index,...  3.9 us
  transfers between devices with their start and end apart: 18, of which 8 were waited for; matrix products, arithmetic and copies ran while one was open for 4% of the time, Pallas kernels for 14%

profile of v5, /device:TPU:34, one launch (start us, length us, event | category | flops | bytes accessed | tf_op | source)
XLA Modules:
  0.0 89.7 jit_solution(8877979364606302416)
XLA Ops:
  0.0 0.0 collective-permute-start.2
  0.0 3.9 %frame_state.1 = (f32[120,224]{1,0:T(8,128)}, f32[120,224]{1,0:T(8,128)}, f32[120,224]{1,0:T(8,128)S(1)}, f32[120,224]{1,0:T(8,128)S(1)}, f32[48,224]{1,0:T(8,128)}, /*index=5*/f32[48,224]{1,0:T(8,128)}) custom-call(s32[2]{0:T(128)} %blocks.1, s32[2]{0:T(128)} %frames.1, s32[16]{0:T(128)} %heights.1, s32[32]{0:T(128)} %widths.1, ...), custom_call_target="tpu_custom_call" | custom-call | tf_op jit(solution)/shard_map/frame_state/pallas_call | solution.py:329
  3.9 0.1 collective-permute-start.3
  4.0 5.6 %collective-permute-start = (bf16[2,16,32,224]{3,2,1,0:T(8,128)(2,1)}, bf16[2,16,32,224]{3,2,1,0:T(8,128)(2,1)}, u32[]{:S(2)}, u32[]{:S(2)}) collective-permute-start(bf16[2,16,32,224]{3,2,1,0:T(8,128)(2,1)} %q_ref.1), channel_id=1, source_target_pairs={{0,8},{8,16},{16,24},{24,32},{32,40},{40,48},{48,56},{56,64},{64,7... | collective-permute-start | bytes 1376264 | tf_op jit(solution)/shard_map/ppermute | solution.py:290
  9.6 2.0 %collective-permute-start.1 = (f32[120,224]{1,0:T(8,128)}, f32[120,224]{1,0:T(8,128)}, u32[]{:S(2)}, u32[]{:S(2)}) collective-permute-start(f32[120,224]{1,0:T(8,128)} %get-tuple-element.33.own_ref.second_ref), channel_id=1, source_target_pairs={{0,8},{8,16},{16,24},{24,32},{32,40},{40,48},{48,56},{56,64},{64,7... | collective-permute-start | bytes 322568 | tf_op jit(solution)/shard_map/ppermute | solution.py:290
  11.7 3.8 %collective-permute-start.9 = (f32[120,224]{1,0:T(8,128)S(1)}, f32[120,224]{1,0:T(8,128)S(1)}, u32[]{:S(2)}, u32[]{:S(2)}) collective-permute-start(f32[120,224]{1,0:T(8,128)S(1)} %get-tuple-element.44), channel_id=1, source_target_pairs={{8,0},{16,8},{24,16},{32,24},{40,32},{48,40},{56,48},{64,56},{72,6... | collective-permute-start | bytes 322568 | tf_op jit(solution)/shard_map/ppermute | solution.py:290
  15.5 0.0 collective-permute-done.3
  15.5 0.9 %add.52 = f32[120,224]{1,0:T(8,128)S(1)} add(f32[120,224]{1,0:T(8,128)S(1)} %get-tuple-element.39, f32[120,224]{1,0:T(8,128)} %collective-permute-done.3) | non-fusion elementwise | flops 26880 | bytes 322560 | tf_op jit(solution)/shard_map/add | solution.py:339
  16.5 3.7 %collective-permute-start.4 = (f32[120,224]{1,0:T(8,128)S(1)}, f32[120,224]{1,0:T(8,128)S(1)}, u32[]{:S(2)}, u32[]{:S(2)}) collective-permute-start(f32[120,224]{1,0:T(8,128)S(1)} %add.52), channel_id=1, source_target_pairs={{0,16},{8,24},{16,0},{24,8},{32,48},{40,56},{48,32},{56,40},{64,80... | collective-permute-start | bytes 322568 | tf_op jit(solution)/shard_map/ppermute | solution.py:294
  20.1 9.2 %collective-permute-done.4 = f32[120,224]{1,0:T(8,128)S(1)} collective-permute-done((f32[120,224]{1,0:T(8,128)S(1)}, f32[120,224]{1,0:T(8,128)S(1)}, u32[]{:S(2)}, u32[]{:S(2)}) %collective-permute-start.4) | collective-permute-done | bytes 107552 | tf_op jit(solution)/shard_map/ppermute | solution.py:294
  29.3 3.5 %collective-permute-start.5 = (f32[120,224]{1,0:T(8,128)S(1)}, f32[120,224]{1,0:T(8,128)S(1)}, u32[]{:S(2)}, u32[]{:S(2)}) collective-permute-start(f32[120,224]{1,0:T(8,128)S(1)} %add.53), channel_id=1, source_target_pairs={{0,56},{8,48},{16,40},{24,32},{32,24},{40,16},{48,8},{56,0},{64,12... | collective-permute-start | bytes 322568 | tf_op jit(solution)/shard_map/ppermute | solution.py:294
  32.8 0.0 collective-permute-done.9.next_ref
  32.9 4.4 %collective-permute-done.5 = f32[120,224]{1,0:T(8,128)S(1)} collective-permute-done((f32[120,224]{1,0:T(8,128)S(1)}, f32[120,224]{1,0:T(8,128)S(1)}, u32[]{:S(2)}, u32[]{:S(2)}) %collective-permute-start.5) | collective-permute-done | bytes 107552 | tf_op jit(solution)/shard_map/ppermute | solution.py:294
  37.3 1.6 %select_add_fusion = (f32[120,224]{1,0:T(8,128)S(1)}, f32[120,224]{1,0:T(8,128)}) fusion(f32[120,224]{1,0:T(8,128)S(1)} %collective-permute-done.5, f32[120,224]{1,0:T(8,128)S(1)} %collective-permute-done.4, f32[120,224]{1,0:T(8,128)} %collective-permute-done.3, pred[]{:T(512)S(6)} %ne.45, pred[]{:T(512)S(6)} %ne.44, pred[]{:T(512)S(6)} %ne.43, ...), kind=kLoop, calls=%fused_computation | loop fusion | flops 161280 | bytes 645123 | tf_op jit(solution)/shard_map/add | solution.py:338
  38.9 0.5 collective-permute-start.6
  39.4 2.4 %collective-permute-start.7 = (f32[120,224]{1,0:T(8,128)}, f32[120,224]{1,0:T(8,128)}, u32[]{:S(2)}, u32[]{:S(2)}) collective-permute-start(f32[120,224]{1,0:T(8,128)} %get-tuple-element.62), channel_id=1, source_target_pairs={{0,128},{8,136},{16,144},{24,152},{32,160},{40,168},{48,176},{56,1... | collective-permute-start | bytes 322568 | tf_op jit(solution)/shard_map/ppermute | solution.py:294
  41.9 0.0 collective-permute-done.1.prev_ref
  41.9 0.5 collective-permute-start.8
  42.4 0.7 select_add_fusion.1
  43.1 0.0 collective-permute-done.halo_ref
  43.2 7.9 %collective-permute-start.10 = (f32[120,224]{1,0:T(8,128)}, f32[120,224]{1,0:T(8,128)S(1)}, u32[]{:S(2)}, u32[]{:S(2)}) collective-permute-start(f32[120,224]{1,0:T(8,128)} %select_add_fusion.1), channel_id=1, source_target_pairs={{16,0},{24,8},{32,16},{40,24},{48,32},{56,40},{64,48},{72,56},{80,... | collective-permute-start | bytes 322568 | tf_op jit(solution)/shard_map/ppermute | solution.py:290
  51.1 0.1 stack.47.flags.idx
  51.2 0.0 collective-permute-done.2._
  51.2 0.0 copy-start
  51.2 1.6 %copy-done = bf16[3,224,2240]{2,1,0:T(8,128)(2,1)} copy-done((bf16[3,224,2240]{2,1,0:T(8,128)(2,1)}, bf16[3,224,2240]{2,1,0:T(8,128)(2,1)S(1)}, u32[]{:S(2)}) %copy-start) | copy-done | bytes 3010584
  52.8 0.0 copy-start.2
  52.8 3.4 %queries.1 = (bf16[16,4,32,224]{3,2,1,0:T(8,128)(2,1)S(1)}, bf16[16,4,32,224]{3,2,1,0:T(8,128)(2,1)S(1)}, bf16[16,4,32,224]{3,2,1,0:T(8,128)(2,1)S(1)}, bf16[3,224,2240]{2,1,0:T(8,128)(2,1)}) custom-call(bf16[2,16,32,224]{3,2,1,0:T(8,128)(2,1)} %q_ref.1, bf16[2,16,32,224]{3,2,1,0:T(8,128)(2,1)} %collective-permute-done.halo_ref, ...), custom_call_target="tpu_custom_call", output_to_operand_aliasing={{3}: (8, {})} | custom-call | tf_op jit(solution)/shard_map/queries/pallas_call | solution.py:373
  56.3 0.0 copy-start.1
  56.3 0.0 collective-permute-done.6.a_ref
  56.3 0.0 collective-permute-done.7.b_ref
  56.3 0.0 collective-permute-done.8.c_ref
  56.3 0.0 collective-permute-done.10.far_ref
  56.3 4.0 %attend.1 = (bf16[8,4,32,224]{3,2,1,0:T(8,128)(2,1)S(1)}, bf16[8,4,32,224]{3,2,1,0:T(8,128)(2,1)S(1)}) custom-call(s32[8]{0:T(128)S(1)} %stack.47.flags.idx, bf16[16,4,32,224]{3,2,1,0:T(8,128)(2,1)S(1)} %get-tuple-element.40.qp_ref, bf16[16,4,32,224]{3,2,1,0:T(8,128)(2,1)S(1)} %get-tuple-element.41.hi_ref, ...), custom_call_target="tpu_custom_call" | custom-call | tf_op jit(solution)/shard_map/attend/pallas_call | solution.py:238
  60.3 0.1 collective-permute-start.11
  60.4 1.9 %collective-permute-done.11.refs_1_.refs_2_.refs_3_ = bf16[8,4,32,224]{3,2,1,0:T(8,128)(2,1)S(1)} collective-permute-done((bf16[8,4,32,224]{3,2,1,0:T(8,128)(2,1)S(1)}, bf16[8,4,32,224]{3,2,1,0:T(8,128)(2,1)S(1)}, u32[]{:S(2)}, u32[]{:S(2)}) %collective-permute-start.11) | collective-permute-done | bytes 458784 | tf_op jit(solution)/shard_map/ppermute | solution.py:299
  62.3 0.0 copy-done.2
  62.3 0.0 copy-done.1
  62.3 2.1 %conv.5 = (bf16[2,32,2240]{2,1,0:T(8,128)(2,1)S(1)}, bf16[2,32,2240]{2,1,0:T(8,128)(2,1)S(1)}) custom-call(s32[8]{0:T(128)S(1)} %stack.47.flags.idx, bf16[8,4,32,224]{3,2,1,0:T(8,128)(2,1)S(1)} %get-tuple-element.48.refs_0_.refs_1_, bf16[8,4,32,224]{3,2,1,0:T(8,128)(2,1)S(1)} %collective-permute-done.11.refs_1_.refs_2_.refs_3_, ...), custom_call_target="tpu_custom_call" | custom-call | tf_op jit(solution)/shard_map/conv/pallas_call | solution.py:274
  64.4 1.7 %collective-permute-start.12 = (bf16[2,32,2240]{2,1,0:T(8,128)(2,1)S(1)}, bf16[2,32,2240]{2,1,0:T(8,128)(2,1)S(1)}, u32[]{:S(2)}, u32[]{:S(2)}) collective-permute-start(bf16[2,32,2240]{2,1,0:T(8,128)(2,1)S(1)} %get-tuple-element.53), channel_id=1, source_target_pairs={{0,2},{1,3},{2,4},{3,5},{4,6},{5,7},{6,0},{7,1},{8,10},{9,11},{10,... | collective-permute-start | bytes 860168 | tf_op jit(solution)/shard_map/ppermute | solution.py:299
  66.1 0.0 copy-start.3
  66.1 1.7 %collective-permute-start.13 = (bf16[2,32,2240]{2,1,0:T(8,128)(2,1)S(1)}, bf16[2,32,2240]{2,1,0:T(8,128)(2,1)S(1)}, u32[]{:S(2)}, u32[]{:S(2)}) collective-permute-start(bf16[2,32,2240]{2,1,0:T(8,128)(2,1)S(1)} %get-tuple-element.55), channel_id=1, source_target_pairs={{0,6},{1,7},{2,0},{3,1},{4,2},{5,3},{6,4},{7,5},{8,14},{9,15},{10,... | collective-permute-start | bytes 860168 | tf_op jit(solution)/shard_map/ppermute | solution.py:299
  67.8 3.0 %conv.4 = (f32[2,32,2240]{2,1,0:T(8,128)S(1)}, bf16[2,32,2240]{2,1,0:T(8,128)(2,1)S(1)}, bf16[2,32,2240]{2,1,0:T(8,128)(2,1)S(1)}, f32[2,32,2240]{2,1,0:T(8,128)S(1)}) custom-call(s32[8]{0:T(128)S(1)} %stack.47.flags.idx, bf16[8,4,32,224]{3,2,1,0:T(8,128)(2,1)S(1)} %get-tuple-element.48.refs_0_.refs_1_, ...), custom_call_target="tpu_custom_call" | custom-call | tf_op jit(solution)/shard_map/conv/pallas_call | solution.py:274
  70.9 1.8 %collective-permute-start.15 = (bf16[2,32,2240]{2,1,0:T(8,128)(2,1)S(1)}, bf16[2,32,2240]{2,1,0:T(8,128)(2,1)S(1)}, u32[]{:S(2)}, u32[]{:S(2)}) collective-permute-start(bf16[2,32,2240]{2,1,0:T(8,128)(2,1)S(1)} %get-tuple-element.57), channel_id=1, source_target_pairs={{0,6},{1,7},{2,0},{3,1},{4,2},{5,3},{6,4},{7,5},{8,14},{9,15},{10,... | collective-permute-start | bytes 860168 | tf_op jit(solution)/shard_map/ppermute | solution.py:299
  72.7 0.3 collective-permute-start.16
  73.0 1.9 %collective-permute-done.12.b_ref = bf16[2,32,2240]{2,1,0:T(8,128)(2,1)S(1)} collective-permute-done((bf16[2,32,2240]{2,1,0:T(8,128)(2,1)S(1)}, bf16[2,32,2240]{2,1,0:T(8,128)(2,1)S(1)}, u32[]{:S(2)}, u32[]{:S(2)}) %collective-permute-start.12) | collective-permute-done | bytes 286752 | tf_op jit(solution)/shard_map/ppermute | solution.py:299
  74.8 1.1 %collective-permute-done.13.d_ref = bf16[2,32,2240]{2,1,0:T(8,128)(2,1)S(1)} collective-permute-done((bf16[2,32,2240]{2,1,0:T(8,128)(2,1)S(1)}, bf16[2,32,2240]{2,1,0:T(8,128)(2,1)S(1)}, u32[]{:S(2)}, u32[]{:S(2)}) %collective-permute-start.13) | collective-permute-done | bytes 286752 | tf_op jit(solution)/shard_map/ppermute | solution.py:299
  76.0 0.1 join.1
  76.1 1.6 %collective-permute-start.14 = (bf16[2,32,2240]{2,1,0:T(8,128)(2,1)S(1)}, bf16[2,32,2240]{2,1,0:T(8,128)(2,1)S(1)}, u32[]{:S(2)}, u32[]{:S(2)}) collective-permute-start(bf16[2,32,2240]{2,1,0:T(8,128)(2,1)S(1)} %get-tuple-element.56), channel_id=1, source_target_pairs={{0,2},{1,3},{2,4},{3,5},{4,6},{5,7},{6,0},{7,1},{8,10},{9,11},{10,... | collective-permute-start | bytes 860168 | tf_op jit(solution)/shard_map/ppermute | solution.py:299
  77.7 1.7 %collective-permute-start.17 = (bf16[2,32,2240]{2,1,0:T(8,128)(2,1)S(1)}, bf16[2,32,2240]{2,1,0:T(8,128)(2,1)S(1)}, u32[]{:S(2)}, u32[]{:S(2)}) collective-permute-start(bf16[2,32,2240]{2,1,0:T(8,128)(2,1)S(1)} %get-tuple-element.60), channel_id=1, source_target_pairs={{0,6},{1,7},{2,0},{3,1},{4,2},{5,3},{6,4},{7,5},{8,14},{9,15},{10,... | collective-permute-start | bytes 860168 | tf_op jit(solution)/shard_map/ppermute | solution.py:299
  79.4 0.0 copy-done.3
  79.4 2.1 %conv.3 = (f32[2,32,2240]{2,1,0:T(8,128)S(1)}, f32[2,32,2240]{2,1,0:T(8,128)S(1)}) custom-call(s32[8]{0:T(128)S(1)} %stack.47.flags.idx, bf16[8,4,32,224]{3,2,1,0:T(8,128)(2,1)S(1)} %get-tuple-element.48.refs_0_.refs_1_, bf16[8,4,32,224]{3,2,1,0:T(8,128)(2,1)S(1)} %collective-permute-done.11.refs_1_.refs_2_.refs_3_, bf16[3,224,2240]{2,1,0:T(8,128)(2,1)S(1)} %copy-done.2, ...), custom_call_target="tpu_custom_call" | custom-call | tf_op jit(solution)/shard_map/conv/pallas_call | solution.py:274
  81.5 0.8 collective-permute-done.15.refs_2_
  82.3 1.5 %collective-permute-done.16.refs_4_ = bf16[2,32,2240]{2,1,0:T(8,128)(2,1)S(1)} collective-permute-done((bf16[2,32,2240]{2,1,0:T(8,128)(2,1)S(1)}, bf16[2,32,2240]{2,1,0:T(8,128)(2,1)S(1)}, u32[]{:S(2)}, u32[]{:S(2)}) %collective-permute-start.16) | collective-permute-done | bytes 286752 | tf_op jit(solution)/shard_map/ppermute | solution.py:299
  83.8 4.7 %collective-permute-done.14.refs_1_ = bf16[2,32,2240]{2,1,0:T(8,128)(2,1)S(1)} collective-permute-done((bf16[2,32,2240]{2,1,0:T(8,128)(2,1)S(1)}, bf16[2,32,2240]{2,1,0:T(8,128)(2,1)S(1)}, u32[]{:S(2)}, u32[]{:S(2)}) %collective-permute-start.14) | collective-permute-done | bytes 286752 | tf_op jit(solution)/shard_map/ppermute | solution.py:299
  88.4 0.0 collective-permute-done.17.refs_5_
  88.4 1.3 %silu.1 = bf16[2,2,32,2240]{3,2,1,0:T(8,128)(2,1)} custom-call(f32[2,32,2240]{2,1,0:T(8,128)S(1)} %get-tuple-element.51.refs_0_, bf16[2,32,2240]{2,1,0:T(8,128)(2,1)S(1)} %collective-permute-done.14.refs_1_, bf16[2,32,2240]{2,1,0:T(8,128)(2,1)S(1)} %collective-permute-done.15.refs_2_, f32[2,32,2240]{2,1,0:T(8,128)S(1)} %get-tuple-element.58.refs_3_, ...), custom_call_target="tpu_custom_call" | custom-call | tf_op jit(solution)/shard_map/silu/pallas_call | solution.py:409
  (4 shorter events, 0.1 us)
Async XLA Ops:
  0.0 51.2 %collective-permute-start.2 = (bf16[3,224,2240]{2,1,0:T(8,128)(2,1)}, bf16[3,224,2240]{2,1,0:T(8,128)(2,1)S(1)}, u32[]{:S(2)}, u32[]{:S(2)}) collective-permute-start(bf16[3,224,2240]{2,1,0:T(8,128)(2,1)} %refs_2_.3), channel_id=1, source_target_pairs={{0,1},{1,0},{2,3},{3,2},{4,5},{5,4},{6,7},{7,6},{8,9},{9,8},{10,11... | collective-permute-start | bytes 9031688 | tf_op jit(solution)/shard_map/ppermute | solution.py:299
  3.9 11.6 %collective-permute-start.3 = (f32[120,224]{1,0:T(8,128)S(1)}, f32[120,224]{1,0:T(8,128)}, u32[]{:S(2)}, u32[]{:S(2)}) collective-permute-start(f32[120,224]{1,0:T(8,128)S(1)} %get-tuple-element.39), channel_id=1, source_target_pairs={{0,8},{8,0},{16,24},{24,16},{32,40},{40,32},{48,56},{56,48},{64,72... | collective-permute-start | bytes 322568 | tf_op jit(solution)/shard_map/ppermute | solution.py:294
  4.0 39.1 %collective-permute-start = (bf16[2,16,32,224]{3,2,1,0:T(8,128)(2,1)}, bf16[2,16,32,224]{3,2,1,0:T(8,128)(2,1)}, u32[]{:S(2)}, u32[]{:S(2)}) collective-permute-start(bf16[2,16,32,224]{3,2,1,0:T(8,128)(2,1)} %q_ref.1), channel_id=1, source_target_pairs={{0,8},{8,16},{16,24},{24,32},{32,40},{40,48},{48,56},{56,64},{64,7... | collective-permute-start | bytes 1376264 | tf_op jit(solution)/shard_map/ppermute | solution.py:290
  9.6 32.2 %collective-permute-start.1 = (f32[120,224]{1,0:T(8,128)}, f32[120,224]{1,0:T(8,128)}, u32[]{:S(2)}, u32[]{:S(2)}) collective-permute-start(f32[120,224]{1,0:T(8,128)} %get-tuple-element.33.own_ref.second_ref), channel_id=1, source_target_pairs={{0,8},{8,16},{16,24},{24,32},{32,40},{40,48},{48,56},{56,64},{64,7... | collective-permute-start | bytes 322568 | tf_op jit(solution)/shard_map/ppermute | solution.py:290
  11.7 21.2 %collective-permute-start.9 = (f32[120,224]{1,0:T(8,128)S(1)}, f32[120,224]{1,0:T(8,128)S(1)}, u32[]{:S(2)}, u32[]{:S(2)}) collective-permute-start(f32[120,224]{1,0:T(8,128)S(1)} %get-tuple-element.44), channel_id=1, source_target_pairs={{8,0},{16,8},{24,16},{32,24},{40,32},{48,40},{56,48},{64,56},{72,6... | collective-permute-start | bytes 322568 | tf_op jit(solution)/shard_map/ppermute | solution.py:290
  16.5 12.9 %collective-permute-start.4 = (f32[120,224]{1,0:T(8,128)S(1)}, f32[120,224]{1,0:T(8,128)S(1)}, u32[]{:S(2)}, u32[]{:S(2)}) collective-permute-start(f32[120,224]{1,0:T(8,128)S(1)} %add.52), channel_id=1, source_target_pairs={{0,16},{8,24},{16,0},{24,8},{32,48},{40,56},{48,32},{56,40},{64,80... | collective-permute-start | bytes 322568 | tf_op jit(solution)/shard_map/ppermute | solution.py:294
  29.3 8.0 %collective-permute-start.5 = (f32[120,224]{1,0:T(8,128)S(1)}, f32[120,224]{1,0:T(8,128)S(1)}, u32[]{:S(2)}, u32[]{:S(2)}) collective-permute-start(f32[120,224]{1,0:T(8,128)S(1)} %add.53), channel_id=1, source_target_pairs={{0,56},{8,48},{16,40},{24,32},{32,24},{40,16},{48,8},{56,0},{64,12... | collective-permute-start | bytes 322568 | tf_op jit(solution)/shard_map/ppermute | solution.py:294
  38.9 17.4 %collective-permute-start.6 = (f32[120,224]{1,0:T(8,128)}, f32[120,224]{1,0:T(8,128)}, u32[]{:S(2)}, u32[]{:S(2)}) collective-permute-start(f32[120,224]{1,0:T(8,128)} %get-tuple-element.62), channel_id=1, source_target_pairs={{0,64},{8,72},{16,80},{24,88},{32,96},{40,104},{48,112},{56,120},{... | collective-permute-start | bytes 322568 | tf_op jit(solution)/shard_map/ppermute | solution.py:294
  39.4 16.9 %collective-permute-start.7 = (f32[120,224]{1,0:T(8,128)}, f32[120,224]{1,0:T(8,128)}, u32[]{:S(2)}, u32[]{:S(2)}) collective-permute-start(f32[120,224]{1,0:T(8,128)} %get-tuple-element.62), channel_id=1, source_target_pairs={{0,128},{8,136},{16,144},{24,152},{32,160},{40,168},{48,176},{56,1... | collective-permute-start | bytes 322568 | tf_op jit(solution)/shard_map/ppermute | solution.py:294
  41.9 14.5 %collective-permute-start.8 = (f32[120,224]{1,0:T(8,128)}, f32[120,224]{1,0:T(8,128)}, u32[]{:S(2)}, u32[]{:S(2)}) collective-permute-start(f32[120,224]{1,0:T(8,128)} %get-tuple-element.62), channel_id=1, source_target_pairs={{0,192},{8,200},{16,208},{24,216},{32,224},{40,232},{48,240},{56,2... | collective-permute-start | bytes 322568 | tf_op jit(solution)/shard_map/ppermute | solution.py:294
  43.2 13.2 %collective-permute-start.10 = (f32[120,224]{1,0:T(8,128)}, f32[120,224]{1,0:T(8,128)S(1)}, u32[]{:S(2)}, u32[]{:S(2)}) collective-permute-start(f32[120,224]{1,0:T(8,128)} %select_add_fusion.1), channel_id=1, source_target_pairs={{16,0},{24,8},{32,16},{40,24},{48,32},{56,40},{64,48},{72,56},{80,... | collective-permute-start | bytes 322568 | tf_op jit(solution)/shard_map/ppermute | solution.py:290
  51.2 1.6 %copy-start = (bf16[3,224,2240]{2,1,0:T(8,128)(2,1)}, bf16[3,224,2240]{2,1,0:T(8,128)(2,1)S(1)}, u32[]{:S(2)}) copy-start(bf16[3,224,2240]{2,1,0:T(8,128)(2,1)S(1)} %collective-permute-done.2._) | copy-start | bytes 9031684
  52.8 9.5 %copy-start.2 = (bf16[3,224,2240]{2,1,0:T(8,128)(2,1)S(1)}, bf16[3,224,2240]{2,1,0:T(8,128)(2,1)}, u32[]{:S(2)}) copy-start(bf16[3,224,2240]{2,1,0:T(8,128)(2,1)} %refs_2_.3) | copy-start | bytes 9031684
  56.3 6.0 %copy-start.1 = (bf16[3,224,2240]{2,1,0:T(8,128)(2,1)S(1)}, bf16[3,224,2240]{2,1,0:T(8,128)(2,1)}, u32[]{:S(2)}) copy-start(bf16[3,224,2240]{2,1,0:T(8,128)(2,1)} %get-tuple-element.50.refs_3_.refs_5_) | copy-start | bytes 9031684
  60.3 2.0 %collective-permute-start.11 = (bf16[8,4,32,224]{3,2,1,0:T(8,128)(2,1)S(1)}, bf16[8,4,32,224]{3,2,1,0:T(8,128)(2,1)S(1)}, u32[]{:S(2)}, u32[]{:S(2)}) collective-permute-start(bf16[8,4,32,224]{3,2,1,0:T(8,128)(2,1)S(1)} %get-tuple-element.49), channel_id=1, source_target_pairs={{0,1},{1,0},{2,3},{3,2},{4,5},{5,4},{6,7},{7,6},{8,9},{9,8},{10,11... | collective-permute-start | bytes 1376264 | tf_op jit(solution)/shard_map/ppermute | solution.py:299
  64.4 10.4 %collective-permute-start.12 = (bf16[2,32,2240]{2,1,0:T(8,128)(2,1)S(1)}, bf16[2,32,2240]{2,1,0:T(8,128)(2,1)S(1)}, u32[]{:S(2)}, u32[]{:S(2)}) collective-permute-start(bf16[2,32,2240]{2,1,0:T(8,128)(2,1)S(1)} %get-tuple-element.53), channel_id=1, source_target_pairs={{0,2},{1,3},{2,4},{3,5},{4,6},{5,7},{6,0},{7,1},{8,10},{9,11},{10,... | collective-permute-start | bytes 860168 | tf_op jit(solution)/shard_map/ppermute | solution.py:299
  66.1 13.3 %copy-start.3 = (f32[2240]{0:T(1024)S(1)}, f32[2240]{0:T(1024)}, u32[]{:S(2)}) copy-start(f32[2240]{0:T(1024)} %param.20) | copy-start | bytes 26884
  66.1 9.9 %collective-permute-start.13 = (bf16[2,32,2240]{2,1,0:T(8,128)(2,1)S(1)}, bf16[2,32,2240]{2,1,0:T(8,128)(2,1)S(1)}, u32[]{:S(2)}, u32[]{:S(2)}) collective-permute-start(bf16[2,32,2240]{2,1,0:T(8,128)(2,1)S(1)} %get-tuple-element.55), channel_id=1, source_target_pairs={{0,6},{1,7},{2,0},{3,1},{4,2},{5,3},{6,4},{7,5},{8,14},{9,15},{10,... | collective-permute-start | bytes 860168 | tf_op jit(solution)/shard_map/ppermute | solution.py:299
  70.9 11.4 %collective-permute-start.15 = (bf16[2,32,2240]{2,1,0:T(8,128)(2,1)S(1)}, bf16[2,32,2240]{2,1,0:T(8,128)(2,1)S(1)}, u32[]{:S(2)}, u32[]{:S(2)}) collective-permute-start(bf16[2,32,2240]{2,1,0:T(8,128)(2,1)S(1)} %get-tuple-element.57), channel_id=1, source_target_pairs={{0,6},{1,7},{2,0},{3,1},{4,2},{5,3},{6,4},{7,5},{8,14},{9,15},{10,... | collective-permute-start | bytes 860168 | tf_op jit(solution)/shard_map/ppermute | solution.py:299
  72.7 11.1 %collective-permute-start.16 = (bf16[2,32,2240]{2,1,0:T(8,128)(2,1)S(1)}, bf16[2,32,2240]{2,1,0:T(8,128)(2,1)S(1)}, u32[]{:S(2)}, u32[]{:S(2)}) collective-permute-start(bf16[2,32,2240]{2,1,0:T(8,128)(2,1)S(1)} %get-tuple-element.59), channel_id=1, source_target_pairs={{0,2},{1,3},{2,4},{3,5},{4,6},{5,7},{6,0},{7,1},{8,10},{9,11},{10,... | collective-permute-start | bytes 860168 | tf_op jit(solution)/shard_map/ppermute | solution.py:299
  76.1 12.3 %collective-permute-start.14 = (bf16[2,32,2240]{2,1,0:T(8,128)(2,1)S(1)}, bf16[2,32,2240]{2,1,0:T(8,128)(2,1)S(1)}, u32[]{:S(2)}, u32[]{:S(2)}) collective-permute-start(bf16[2,32,2240]{2,1,0:T(8,128)(2,1)S(1)} %get-tuple-element.56), channel_id=1, source_target_pairs={{0,2},{1,3},{2,4},{3,5},{4,6},{5,7},{6,0},{7,1},{8,10},{9,11},{10,... | collective-permute-start | bytes 860168 | tf_op jit(solution)/shard_map/ppermute | solution.py:299
  77.7 10.7 %collective-permute-start.17 = (bf16[2,32,2240]{2,1,0:T(8,128)(2,1)S(1)}, bf16[2,32,2240]{2,1,0:T(8,128)(2,1)S(1)}, u32[]{:S(2)}, u32[]{:S(2)}) collective-permute-start(bf16[2,32,2240]{2,1,0:T(8,128)(2,1)S(1)} %get-tuple-element.60), channel_id=1, source_target_pairs={{0,6},{1,7},{2,0},{3,1},{4,2},{5,3},{6,4},{7,5},{8,14},{9,15},{10,... | collective-permute-start | bytes 860168 | tf_op jit(solution)/shard_map/ppermute | solution.py:299
